TPU v7x, 32 devices: a whole 2x2x4 slice. The times are simulated.
32 devices in a mesh: sec: 2 (over core), tile: 16 (over z, y, x).
Axes of the slice: x: 2, y: 2, z: 4, core: 2. Of those that a mesh axis runs over, the one named last changes fastest.
Arguments:
- atm_state: bfloat16 [32768, 1024], P(('sec', 'tile')), may hold values from -6 to 6
- gain_atm: float32 [1024], replicated, may hold values from 0.25 to 1.75
- w_up_atm: bfloat16 [1024, 2048], replicated, may hold values from -0.1875 to 0.1875
- w_down_atm: bfloat16 [2048, 1024], replicated, may hold values from -0.125 to 0.125
- w_flux: bfloat16 [1024, 128], replicated, may hold values from -0.1875 to 0.1875
- ent_source: int32 [4096], P(('sec', 'tile')), may hold values from 0 to 7
- ent_target: int32 [4096, 1], P(('sec', 'tile')), may hold values from 0 to 31; in each aligned block of 128 rows (0 to 127, 128 to 255, ...) at most 8 rows name the same one
- ent_block: int32 [4096], P(('sec', 'tile')), may hold values from 0 to 44
- remap_weights: bfloat16 [4096, 128, 128], P(('sec', 'tile')), may hold values from -0.5 to 0.5
- ocean_state: bfloat16 [200, 184320], P(None, ('sec', 'tile')), may hold values from -6 to 6
- land_sea: int32 [184320], P(('sec', 'tile')), may hold values 0 or 1
- conv_kernel: float32 [200, 9], replicated, may hold values from -2.5 to 2.5
- w_force: bfloat16 [128, 200], replicated, may hold values from -0.5 to 0.5
- gain_ocn: float32 [200], replicated, may hold values from 0.25 to 1.75
- w_up_ocn: bfloat16 [200, 800], replicated, may hold values from -0.4375 to 0.4375
- w_down_ocn: bfloat16 [800, 200], replicated, may hold values from -0.21875 to 0.21875
Outputs:
- atm_next: bfloat16 [32768, 1024], P(('sec', 'tile'))
- ocean_next: bfloat16 [200, 184320], P(None, ('sec', 'tile'))
Inputs may be any that keep to these rules, and one draw needn't show every extreme that they name: `ent_target`: among the 128 entries of one device no ocean tile is named more than 8 times, a bound that some block reaches; every tile is named by some entry.
All inputs are finite; a program needn't handle non-finite values. No bound on the sum of `land_sea` on one device may be relied on, other than what follows from the above.
Results may differ from a plain program's by a relative error of at most 0.009.
Values may be sent and summed in bfloat16 or wider, within the bound.
No kernel may reach another device: no remote copies, remote signals or barrier semaphores. Data moves between devices by JAX's collectives and lax.ppermute only.
A program may use at most 192 MiB of HBM per device.

v0:
```python
import jax
import jax.numpy as jnp
from jax import lax
from jax.sharding import PartitionSpec as P

OX = 1440


def extended_2(block, sides, width):
    for axis, dim in sides:
        count = lax.axis_size(axis)
        forward = [(i, i + 1) for i in range(count - 1)]
        backward = [(target, source) for source, target in forward]
        low = lax.ppermute(
            lax.slice_in_dim(block, block.shape[dim] - width, None, axis=dim), axis, forward
        )
        high = lax.ppermute(lax.slice_in_dim(block, 0, width, axis=dim), axis, backward)
        block = jnp.concatenate([low, block, high], axis=dim)
    return block


def atmosphere_layer(columns, gain_atm, w_up_atm, w_down_atm, w_flux):
    values = columns.astype(jnp.float32)
    centred = values - jnp.mean(values, axis=-1, keepdims=True)
    spread_sq = jnp.mean(centred * centred, axis=-1, keepdims=True)
    normed = (centred * lax.rsqrt(spread_sq + 1e-05) * gain_atm).astype(jnp.bfloat16)
    hidden = jax.nn.gelu(jnp.dot(normed, w_up_atm, preferred_element_type=jnp.float32)).astype(
        jnp.bfloat16
    )
    updated = (values + jnp.dot(hidden, w_down_atm, preferred_element_type=jnp.float32)).astype(
        jnp.bfloat16
    )
    surface = jnp.dot(updated, w_flux, preferred_element_type=jnp.float32).astype(jnp.bfloat16)
    return (updated, surface)


def flat_mixing(padded_flat, kernel, row_len, cell_count):
    extended = jnp.pad(padded_flat.astype(jnp.float32), ((0, 0), (row_len, row_len)))
    column_at = (jnp.arange(cell_count, dtype=jnp.int32) % row_len)[None, :]
    first_col = column_at == 0
    last_col = column_at == row_len - 1

    def window(offset):
        return lax.slice_in_dim(extended, row_len + offset, row_len + offset + cell_count, axis=1)

    summed = jnp.zeros((padded_flat.shape[0], cell_count), jnp.float32)
    for row_step in range(3):
        base = row_step * row_len
        for col_step in range(3):
            if col_step == 0:
                shifted = jnp.where(first_col, window(base + row_len - 1), window(base - 1))
            elif col_step == 2:
                shifted = jnp.where(last_col, window(base - row_len + 1), window(base + 1))
            else:
                shifted = window(base)
            summed = summed + kernel[:, 3 * row_step + col_step][:, None] * shifted
    return summed


def ocean_update(mixing, forcing, ocean_now, sea_mask, w_force, gain_ocn, w_up_ocn, w_down_ocn):
    contract = (((0,), (1,)), ((), ()))
    driven = mixing + lax.dot_general(
        w_force, forcing, contract, preferred_element_type=jnp.float32
    )
    centred = driven - jnp.mean(driven, axis=0, keepdims=True)
    spread_sq = jnp.mean(centred * centred, axis=0, keepdims=True)
    normed = (centred * lax.rsqrt(spread_sq + 1e-05) * gain_ocn[:, None]).astype(jnp.bfloat16)
    leading = (((0,), (0,)), ((), ()))
    hidden = jax.nn.gelu(
        lax.dot_general(w_up_ocn, normed, leading, preferred_element_type=jnp.float32)
    ).astype(jnp.bfloat16)
    change = lax.dot_general(w_down_ocn, hidden, leading, preferred_element_type=jnp.float32)
    return (ocean_now.astype(jnp.float32) + sea_mask.astype(jnp.float32)[None, :] * change).astype(
        jnp.bfloat16
    )


def local(
    atm_state,
    gain_atm,
    w_up_atm,
    w_down_atm,
    w_flux,
    ent_source,
    ent_target,
    ent_block,
    remap_weights,
    ocean_state,
    land_sea,
    conv_kernel,
    w_force,
    gain_ocn,
    w_up_ocn,
    w_down_ocn,
):
    cell_count = ocean_state.shape[1]
    padded = extended_2(ocean_state, ((("sec", "tile"), 1),), OX)
    mixing = flat_mixing(padded, conv_kernel, OX, cell_count)
    atm_next, surface = atmosphere_layer(atm_state, gain_atm, w_up_atm, w_down_atm, w_flux)
    block_rows = remap_weights.shape[1]
    features = surface.shape[1]
    atm_blocks = surface.shape[0] // block_rows
    surface_flat = surface.reshape(atm_blocks, block_rows * features)
    sections = lax.axis_size("sec")
    devices = sections * lax.axis_size("tile")
    entries = ent_source.shape[0]
    capacity = max(2, 2 * entries // devices)
    targets = ent_target[:, 0]
    matches = (targets[:, None] == jnp.arange(devices, dtype=jnp.int32)[None, :]).astype(jnp.int32)
    earlier = jnp.cumsum(matches, axis=0) - matches
    position = jnp.sum(earlier * matches, axis=1)
    slot_index = targets * capacity + position
    source_pick = (ent_source[:, None] == jnp.arange(atm_blocks, dtype=jnp.int32)[None, :]).astype(
        jnp.bfloat16
    )
    picked = (
        jnp.dot(source_pick, surface_flat, preferred_element_type=jnp.float32)
        .astype(jnp.bfloat16)
        .reshape(entries, block_rows, features)
    )
    payload = jnp.einsum(
        "eij,ejf->eif", remap_weights, picked, preferred_element_type=jnp.float32
    ).astype(jnp.bfloat16)
    item_shape = payload.shape[1:]
    slot_count = devices * capacity
    slot_table_int = (
        jnp.arange(slot_count, dtype=jnp.int32)[:, None] == slot_index[None, :]
    ).astype(jnp.int32)
    slot_table = slot_table_int.astype(jnp.bfloat16)
    outgoing = (
        jnp.dot(slot_table, payload.reshape(entries, -1), preferred_element_type=jnp.float32)
        .astype(jnp.bfloat16)
        .reshape((slot_count,) + item_shape)
    )
    labels = jnp.sum(slot_table_int * (ent_block[None, :] + 1), axis=1) - 1
    arrived, arrived_labels = (
        lax.all_to_all(
            outgoing.reshape((devices, capacity) + item_shape),
            ("sec", "tile"),
            split_axis=0,
            concat_axis=0,
            tiled=True,
        ),
        lax.all_to_all(
            labels.reshape(devices, capacity),
            ("sec", "tile"),
            split_axis=0,
            concat_axis=0,
            tiled=True,
        ),
    )
    arrived = arrived.reshape((slot_count,) + item_shape)
    arrived_labels = arrived_labels.reshape(slot_count)
    ocean_blocks = cell_count // block_rows
    select = (jnp.arange(ocean_blocks, dtype=jnp.int32)[:, None] == arrived_labels[None, :]).astype(
        jnp.bfloat16
    )
    forcing = (
        jnp.einsum("ks,sif->kif", select, arrived, preferred_element_type=jnp.float32)
        .astype(jnp.bfloat16)
        .reshape(cell_count, features)
    )
    ocean_next = ocean_update(
        mixing, forcing, ocean_state, land_sea, w_force, gain_ocn, w_up_ocn, w_down_ocn
    )
    return (atm_next, ocean_next)


def solution(mesh):
    placed = (
        P(("sec", "tile"), None),
        P(),
        P(),
        P(),
        P(),
        P(("sec", "tile")),
        P(("sec", "tile"), None),
        P(("sec", "tile")),
        P(("sec", "tile"), None, None),
        P(None, ("sec", "tile")),
        P(("sec", "tile")),
        P(),
        P(),
        P(),
        P(),
        P(),
    )
    return jax.shard_map(
        local,
        mesh=mesh,
        in_specs=placed,
        out_specs=(P(("sec", "tile"), None), P(None, ("sec", "tile"))),
        check_vma=False,
    )
```

profile of v0, /device:TPU:14, one launch (start us, length us, event | category | flops | bytes accessed | tf_op | source)
XLA Modules:
  0.0 319.0 jit_solution(13339609071989077875)
XLA Ops:
  0.6 0.8 fusion.70
  1.4 0.2 reduce_window_sum.11
  1.6 0.8 select_reduce_fusion.1
  2.4 0.7 multiply_add_fusion
  3.2 0.7 sub.29
  3.9 6.0 %all-to-all-start = ((s32[32,1,8]{2,1,0:T(1,128)}), s32[32,1,8]{2,1,0:T(1,128)S(1)}, u32[]{:S(2)}, u32[]{:S(2)}) async-start(s32[32,1,8]{2,1,0:T(1,128)} %bitcast.10), calls=%async_computation | async-start | bytes 32768 | tf_op jit(solution)/shard_map/all_to_all | solution.py:144
  9.9 1.9 convert_reduce_fusion
  11.9 2.3 fusion.42
  14.2 13.8 %fusion.45 = bf16[1024,1024]{1,0:T(8,128)(2,1)S(1)} fusion(bf16[1024,1024]{1,0:T(8,128)(2,1)} %param.16, bf16[2048,1024]{1,0:T(8,128)(2,1)} %param.19, bf16[1024,2048]{1,0:T(8,128)(2,1)} %param.18, f32[1024]{0:T(1024)} %param.17, f32[1024]{0:T(1024)S(1)} %add_rsqrt_fusion.1, f32[1024]{0:T(1024)S(1)} %broadcast_multiply_fusion.1), kind=kOutput, calls=%fused_computation.63 | convolution fusion | flops 8617197568 | bytes 12595200 | tf_op jit(solution)/shard_map/dot_general | solution.py:30
  28.0 0.7 convolution_convert_fusion.2
  28.7 0.1 reshape.90
  28.8 1.3 fusion.54
  30.1 1.2 copy.35
  31.4 0.9 copy-done.2
  32.3 5.2 %convert_bitcast_fusion = bf16[128,128,128]{1,2,0:T(8,128)(2,1)} fusion(bf16[128,128,128]{2,1,0:T(8,128)(2,1)S(1)} %bitcast.56, bf16[128,128,128]{2,1,0:T(8,128)(2,1)S(1)} %copy-done.2), kind=kOutput, calls=%fused_computation.64 | convolution fusion | flops 538968064 | bytes 12582912 | tf_op jit(solution)/shard_map/eij,ejf->eif/dot_general | solution.py:121
  37.5 7.3 %copy.31 = bf16[128,128,128]{0,2,1:T(8,128)(2,1)} copy(bf16[128,128,128]{1,2,0:T(8,128)(2,1)} %convert_bitcast_fusion) | data formatting | bytes 8388608 | tf_op jit(solution)/shard_map/convert_element_type | solution.py:123
  44.8 7.8 %fusion.23 = bf16[32,8,128,128]{3,1,2,0:T(8,128)(2,1)} fusion(bf16[128,16384]{0,1:T(8,128)(2,1)} %bitcast.55, s32[128]{0:T(128)S(1)} %get-tuple-element.15), kind=kOutput, calls=%fused_computation.36 | convolution fusion | flops 1078034432 | bytes 12583424 | tf_op jit(solution)/shard_map/dot_general | solution.py:131
  52.5 5.9 %all-to-all-start.1 = ((bf16[32,8,128,128]{3,1,2,0:T(8,128)(2,1)}), bf16[32,8,128,128]{3,1,2,0:T(8,128)(2,1)}, u32[]{:S(2)}, u32[]{:S(2)}) async-start(bf16[32,8,128,128]{3,1,2,0:T(8,128)(2,1)} %fusion.23), calls=%async_computation.1 | async-start | bytes 16777216 | tf_op jit(solution)/shard_map/all_to_all | solution.py:137
  58.5 1.2 fusion.88
  59.7 3.4 %collective-permute-start = (bf16[200,1440]{1,0:T(8,128)(2,1)}, bf16[200,1440]{1,0:T(8,128)(2,1)S(1)}, u32[]{:S(2)}, u32[]{:S(2)}) collective-permute-start(bf16[200,1440]{1,0:T(8,128)(2,1)} %get-tuple-element.3), channel_id=1, source_target_pairs={{0,1},{1,2},{2,3},{3,4},{4,5},{5,6},{6,7},{7,8},{8,9},{9,10},{10,1... | collective-permute-start | bytes 1728008 | tf_op jit(solution)/shard_map/ppermute | solution.py:14
  63.0 2.5 collective-permute-start.1
  65.6 0.6 broadcast.127
  66.2 0.7 reduce.3
  67.0 191.2 %collective-permute-done = bf16[200,1440]{1,0:T(8,128)(2,1)S(1)} collective-permute-done((bf16[200,1440]{1,0:T(8,128)(2,1)}, bf16[200,1440]{1,0:T(8,128)(2,1)S(1)}, u32[]{:S(2)}, u32[]{:S(2)}) %collective-permute-start) | collective-permute-done | bytes 576032 | tf_op jit(solution)/shard_map/ppermute | solution.py:14
  258.3 3.9 %collective-permute-done.1 = bf16[200,1440]{1,0:T(8,128)(2,1)} collective-permute-done((bf16[200,1440]{1,0:T(8,128)(2,1)}, bf16[200,1440]{1,0:T(8,128)(2,1)}, u32[]{:S(2)}, u32[]{:S(2)}) %collective-permute-start.1) | collective-permute-done | bytes 576032 | tf_op jit(solution)/shard_map/ppermute | solution.py:17
  262.2 7.1 %concatenate.3 = bf16[200,8640]{1,0:T(8,128)(2,1)} concatenate(bf16[200,1440]{1,0:T(8,128)(2,1)S(1)} %collective-permute-done, bf16[200,5760]{1,0:T(8,128)(2,1)S(1)} %copy-done.1, bf16[200,1440]{1,0:T(8,128)(2,1)} %collective-permute-done.1), dimensions={1} | concatenate | bytes 6912000 | tf_op jit(solution)/shard_map/concatenate | solution.py:18
  269.3 5.6 %convert_element_type.67 = f32[200,8640]{1,0:T(8,128)} convert(bf16[200,8640]{1,0:T(8,128)(2,1)} %concatenate.3) | non-fusion elementwise | flops 1728000 | bytes 10368000 | tf_op jit(solution)/shard_map/convert_element_type | solution.py:38
  275.0 4.9 %fusion.60 = bf16[45,128,128]{2,0,1:T(8,128)(2,1)S(1)} fusion(bf16[32,8,128,128]{3,1,2,0:T(8,128)(2,1)} %all-to-all-done.1, s32[256]{0:T(256)S(1)} %eq.94), kind=kOutput, calls=%fused_computation.74 | convolution fusion | flops 378236160 | bytes 9864192 | tf_op jit(solution)/shard_map/ks,sif->kif/dot_general | solution.py:159
  279.9 1.5 copy.33
  281.4 24.1 %fusion.90 = (f32[5760]{0:T(1024)S(1)}, f32[200,5760]{1,0:T(8,128)}) fusion(bf16[5760,128]{1,0:T(8,128)(2,1)} %bitcast.57, bf16[128,200]{0,1:T(8,128)(2,1)S(1)} %copy-done.9, f32[200]{0:T(256)S(1)} %bitcast.67, f32[200,8640]{1,0:T(8,128)} %convert_element_type.67, f32[200]{0:T(256)S(1)} %bitcast.68, f32[200]{0:T(256)S(1)} %bitcast.61, ...), kind=kOutput, calls=%fused_computation.112 | convolution fusion | flops 323706240 | bytes 45394720 | tf_op jit(solution)/shard_map/dot_general | solution.py:62
  305.5 2.8 multiply_reduce_fusion
  308.4 10.5 %fusion.22 = bf16[200,5760]{1,0:T(8,128)(2,1)} fusion(bf16[800,200]{0,1:T(8,128)(2,1)S(1)} %copy-done, bf16[200,5760]{1,0:T(8,128)(2,1)S(1)} %copy-done.1, bf16[200,800]{1,0:T(8,128)(2,1)S(1)} %copy-done.8, f32[200,5760]{1,0:T(8,128)} %get-tuple-element.14, f32[200]{0:T(256)S(1)} %copy-done.10, f32[5760]{0:T(1024)S(1)} %add_rsqrt_fusion, ...), kind=kOutput, calls=%fused_computation.32 | convolution fusion | flops 3737088000 | bytes 9925920 | tf_op jit(solution)/shard_map/dot_general | solution.py:72
  (33 shorter events, 0.3 us)
Async XLA Ops:
  0.6 307.8 %copy-start = (bf16[800,200]{0,1:T(8,128)(2,1)S(1)}, bf16[800,200]{0,1:T(8,128)(2,1)}, u32[]{:S(2)}) copy-start(bf16[800,200]{0,1:T(8,128)(2,1)} %param.31) | copy-start | bytes 960004
  3.9 48.6 %all-to-all-start = ((s32[32,1,8]{2,1,0:T(1,128)}), s32[32,1,8]{2,1,0:T(1,128)S(1)}, u32[]{:S(2)}, u32[]{:S(2)}) async-start(s32[32,1,8]{2,1,0:T(1,128)} %bitcast.10), calls=%async_computation | async-start | bytes 32768 | tf_op jit(solution)/shard_map/all_to_all | solution.py:144
  14.2 13.8 %copy-start.4 = (bf16[1024,128]{1,0:T(8,128)(2,1)S(1)}, bf16[1024,128]{1,0:T(8,128)(2,1)}, u32[]{:S(2)}) copy-start(bf16[1024,128]{1,0:T(8,128)(2,1)} %param.20) | copy-start | bytes 786436
  14.2 14.7 %copy-start.7 = (s32[128]{0:T(128)S(1)}, s32[128]{0:T(128)}, u32[]{:S(2)}) copy-start(s32[128]{0:T(128)} %param.21) | copy-start | bytes 1540
  28.0 3.4 %copy-start.3 = (bf16[1024,1024]{1,0:T(8,128)(2,1)}, bf16[1024,1024]{1,0:T(8,128)(2,1)S(1)}, u32[]{:S(2)}) copy-start(bf16[1024,1024]{1,0:T(8,128)(2,1)S(1)} %fusion.45) | copy-start | bytes 6291460
  30.1 2.2 copy-start.2
  52.5 5.9 %copy-start.1 = (bf16[200,5760]{1,0:T(8,128)(2,1)S(1)}, bf16[200,5760]{1,0:T(8,128)(2,1)}, u32[]{:S(2)}) copy-start(bf16[200,5760]{1,0:T(8,128)(2,1)} %param.25) | copy-start | bytes 6912004
  52.5 13.0 %copy-start.5 = (s32[5760]{0:T(1024)S(1)}, s32[5760]{0:T(1024)}, u32[]{:S(2)}) copy-start(s32[5760]{0:T(1024)} %param.26) | copy-start | bytes 69124
  52.5 13.1 %copy-start.6 = (f32[200,9]{0,1:T(8,128)S(1)}, f32[200,9]{0,1:T(8,128)}, u32[]{:S(2)}) copy-start(f32[200,9]{0,1:T(8,128)} %param.27) | copy-start | bytes 21604
  52.5 222.4 %all-to-all-start.1 = ((bf16[32,8,128,128]{3,1,2,0:T(8,128)(2,1)}), bf16[32,8,128,128]{3,1,2,0:T(8,128)(2,1)}, u32[]{:S(2)}, u32[]{:S(2)}) async-start(bf16[32,8,128,128]{3,1,2,0:T(8,128)(2,1)} %fusion.23), calls=%async_computation.1 | async-start | bytes 16777216 | tf_op jit(solution)/shard_map/all_to_all | solution.py:137
  59.7 198.6 %collective-permute-start = (bf16[200,1440]{1,0:T(8,128)(2,1)}, bf16[200,1440]{1,0:T(8,128)(2,1)S(1)}, u32[]{:S(2)}, u32[]{:S(2)}) collective-permute-start(bf16[200,1440]{1,0:T(8,128)(2,1)} %get-tuple-element.3), channel_id=1, source_target_pairs={{0,1},{1,2},{2,3},{3,4},{4,5},{5,6},{6,7},{7,8},{8,9},{9,10},{10,1... | collective-permute-start | bytes 1728008 | tf_op jit(solution)/shard_map/ppermute | solution.py:14
  63.0 199.2 %collective-permute-start.1 = (bf16[200,1440]{1,0:T(8,128)(2,1)}, bf16[200,1440]{1,0:T(8,128)(2,1)}, u32[]{:S(2)}, u32[]{:S(2)}) collective-permute-start(bf16[200,1440]{1,0:T(8,128)(2,1)} %get-tuple-element.2), channel_id=1, source_target_pairs={{1,0},{2,1},{3,2},{4,3},{5,4},{6,5},{7,6},{8,7},{9,8},{10,9},{11,1... | collective-permute-start | bytes 1728008 | tf_op jit(solution)/shard_map/ppermute | solution.py:17
  274.9 6.5 %copy-start.9 = (bf16[128,200]{0,1:T(8,128)(2,1)S(1)}, bf16[128,200]{0,1:T(8,128)(2,1)}, u32[]{:S(2)}) copy-start(bf16[128,200]{0,1:T(8,128)(2,1)} %param.28) | copy-start | bytes 153604
  305.5 2.9 copy-start.8
  305.5 2.9 copy-start.10
where the time goes:
time: 320 us; the launch traced here: 319 us
  waiting for transfers between devices  195 us (61%)
  matrix products  68.3 us (21%)
  local copies, waits for them, and re-layouts  20.8 us (6%)
  starting transfers between devices  17.7 us (6%)
  other arithmetic  16 us (5%)
    ppermute x1, waiting for transfers between devices, extended_2(): lax.ppermute(lax.slice_in_dim(block, block.shape[dim] - width, None, axis...  191 us
    dot_general x1, matrix products, ocean_update(): lax.dot_general(w_force, forcing, contract, preferred_element_type=jnp.fl...  24.1 us
    dot_general x1, matrix products, atmosphere_layer(): jnp.dot(hidden, w_down_atm, preferred_element_type=jnp.float32)  13.8 us
    dot_general x1, matrix products, ocean_update(): lax.dot_general(w_down_ocn, hidden, leading, preferred_element_type=jnp.f...  10.5 us
    dot_general x1, matrix products, local(): jnp.dot(slot_table, payload.reshape(entries, -1), preferred_element_type=...  7.76 us
    convert_element_type x1, local copies, waits for them, and re-layouts, local(): payload = jnp.einsum('eij,ejf->eif', remap_weights, picked, preferred_ele...  7.28 us
    concatenate x1, local copies, waits for them, and re-layouts, extended_2(): block = jnp.concatenate([low, block, high], axis=dim)  7.12 us
  transfers between devices with their start and end apart: 4, of which 2 were waited for; matrix products, arithmetic and copies ran while one was open for 18% of the time, Pallas kernels for 0%

commit v1 on v0

--- a/solution.py
+++ b/solution.py
@@ -107,7 +107,12 @@
     capacity = max(2, 2 * entries // devices)
     targets = ent_target[:, 0]
     matches = (targets[:, None] == jnp.arange(devices, dtype=jnp.int32)[None, :]).astype(jnp.int32)
-    earlier = jnp.cumsum(matches, axis=0) - matches
+    before = (
+        jnp.arange(entries, dtype=jnp.int32)[:, None] > jnp.arange(entries, dtype=jnp.int32)[None, :]
+    ).astype(jnp.bfloat16)
+    earlier = jnp.dot(
+        before, matches.astype(jnp.bfloat16), preferred_element_type=jnp.float32
+    ).astype(jnp.int32)
     position = jnp.sum(earlier * matches, axis=1)
     slot_index = targets * capacity + position
     source_pick = (ent_source[:, None] == jnp.arange(atm_blocks, dtype=jnp.int32)[None, :]).astype(

time: 320 us -> 319 us (level)
  no operation moved by 1% of the time
where the time goes in v1:
time: 319 us; the launch traced here: 318 us
  waiting for transfers between devices  195 us (61%)
  matrix products  69.1 us (22%)
  local copies, waits for them, and re-layouts  20.9 us (7%)
  starting transfers between devices  17.7 us (6%)
  other arithmetic  14.3 us (4%)
    ppermute x1, waiting for transfers between devices, extended_2(): lax.ppermute(lax.slice_in_dim(block, block.shape[dim] - width, None, axis...  191 us
    dot_general x1, matrix products, ocean_update(): lax.dot_general(w_force, forcing, contract, preferred_element_type=jnp.fl...  24 us
    dot_general x1, matrix products, atmosphere_layer(): jnp.dot(hidden, w_down_atm, preferred_element_type=jnp.float32)  13.8 us
    dot_general x1, matrix products, ocean_update(): lax.dot_general(w_down_ocn, hidden, leading, preferred_element_type=jnp.f...  10.5 us
    dot_general x1, matrix products, local(): jnp.dot(slot_table, payload.reshape(entries, -1), preferred_element_type=...  7.75 us
    convert_element_type x1, local copies, waits for them, and re-layouts, local(): payload = jnp.einsum('eij,ejf->eif', remap_weights, picked, preferred_ele...  7.28 us
    concatenate x1, local copies, waits for them, and re-layouts, extended_2(): block = jnp.concatenate([low, block, high], axis=dim)  7.15 us
  transfers between devices with their start and end apart: 4, of which 2 were waited for; matrix products, arithmetic and copies ran while one was open for 18% of the time, Pallas kernels for 0%

profile of v1, /device:TPU:14, one launch (start us, length us, event | category | flops | bytes accessed | tf_op | source)
XLA Modules:
  0.0 318.0 jit_solution(5658865547311719514)
XLA Ops:
  0.6 0.9 fusion.70
  1.5 0.7 multiply_add_fusion
  2.2 0.1 select_reduce_fusion
  2.4 0.7 sub.25
  3.0 6.0 %all-to-all-start = ((s32[32,1,8]{2,1,0:T(1,128)}), s32[32,1,8]{2,1,0:T(1,128)S(1)}, u32[]{:S(2)}, u32[]{:S(2)}) async-start(s32[32,1,8]{2,1,0:T(1,128)} %bitcast.10), calls=%async_computation | async-start | bytes 32768 | tf_op jit(solution)/shard_map/all_to_all | solution.py:149
  9.0 1.9 convert_reduce_fusion
  11.0 2.3 fusion.42
  13.3 13.8 %fusion.45 = bf16[1024,1024]{1,0:T(8,128)(2,1)S(1)} fusion(bf16[1024,1024]{1,0:T(8,128)(2,1)} %param.16, bf16[2048,1024]{1,0:T(8,128)(2,1)} %param.19, bf16[1024,2048]{1,0:T(8,128)(2,1)} %param.18, f32[1024]{0:T(1024)} %param.17, f32[1024]{0:T(1024)S(1)} %add_rsqrt_fusion.1, f32[1024]{0:T(1024)S(1)} %broadcast_multiply_fusion.1), kind=kOutput, calls=%fused_computation.63 | convolution fusion | flops 8617197568 | bytes 12595200 | tf_op jit(solution)/shard_map/dot_general | solution.py:30
  27.1 0.7 convolution_convert_fusion.2
  27.8 0.1 reshape.90
  27.9 1.3 fusion.54
  29.2 1.2 copy.35
  30.5 0.9 copy-done.2
  31.4 5.2 %convert_bitcast_fusion = bf16[128,128,128]{1,2,0:T(8,128)(2,1)} fusion(bf16[128,128,128]{2,1,0:T(8,128)(2,1)S(1)} %bitcast.56, bf16[128,128,128]{2,1,0:T(8,128)(2,1)S(1)} %copy-done.2), kind=kOutput, calls=%fused_computation.64 | convolution fusion | flops 538968064 | bytes 12582912 | tf_op jit(solution)/shard_map/eij,ejf->eif/dot_general | solution.py:126
  36.6 7.3 %copy.31 = bf16[128,128,128]{0,2,1:T(8,128)(2,1)} copy(bf16[128,128,128]{1,2,0:T(8,128)(2,1)} %convert_bitcast_fusion) | data formatting | bytes 8388608 | tf_op jit(solution)/shard_map/convert_element_type | solution.py:128
  43.9 7.7 %fusion.23 = bf16[32,8,128,128]{3,1,2,0:T(8,128)(2,1)} fusion(bf16[128,16384]{0,1:T(8,128)(2,1)} %bitcast.55, s32[128]{0:T(128)S(1)} %get-tuple-element.15), kind=kOutput, calls=%fused_computation.36 | convolution fusion | flops 1078034432 | bytes 12583424 | tf_op jit(solution)/shard_map/dot_general | solution.py:136
  51.6 5.9 %all-to-all-start.1 = ((bf16[32,8,128,128]{3,1,2,0:T(8,128)(2,1)}), bf16[32,8,128,128]{3,1,2,0:T(8,128)(2,1)}, u32[]{:S(2)}, u32[]{:S(2)}) async-start(bf16[32,8,128,128]{3,1,2,0:T(8,128)(2,1)} %fusion.23), calls=%async_computation.1 | async-start | bytes 16777216 | tf_op jit(solution)/shard_map/all_to_all | solution.py:142
  57.6 1.2 fusion.90
  58.8 3.4 %collective-permute-start = (bf16[200,1440]{1,0:T(8,128)(2,1)}, bf16[200,1440]{1,0:T(8,128)(2,1)S(1)}, u32[]{:S(2)}, u32[]{:S(2)}) collective-permute-start(bf16[200,1440]{1,0:T(8,128)(2,1)} %get-tuple-element.3), channel_id=1, source_target_pairs={{0,1},{1,2},{2,3},{3,4},{4,5},{5,6},{6,7},{7,8},{8,9},{9,10},{10,1... | collective-permute-start | bytes 1728008 | tf_op jit(solution)/shard_map/ppermute | solution.py:14
  62.2 2.5 collective-permute-start.1
  64.7 0.6 broadcast.127
  65.3 0.7 reduce.3
  66.1 0.1 eq.94
  66.2 191.2 %collective-permute-done = bf16[200,1440]{1,0:T(8,128)(2,1)S(1)} collective-permute-done((bf16[200,1440]{1,0:T(8,128)(2,1)}, bf16[200,1440]{1,0:T(8,128)(2,1)S(1)}, u32[]{:S(2)}, u32[]{:S(2)}) %collective-permute-start) | collective-permute-done | bytes 576032 | tf_op jit(solution)/shard_map/ppermute | solution.py:14
  257.4 3.9 %collective-permute-done.1 = bf16[200,1440]{1,0:T(8,128)(2,1)} collective-permute-done((bf16[200,1440]{1,0:T(8,128)(2,1)}, bf16[200,1440]{1,0:T(8,128)(2,1)}, u32[]{:S(2)}, u32[]{:S(2)}) %collective-permute-start.1) | collective-permute-done | bytes 576032 | tf_op jit(solution)/shard_map/ppermute | solution.py:17
  261.3 7.2 %concatenate.3 = bf16[200,8640]{1,0:T(8,128)(2,1)} concatenate(bf16[200,1440]{1,0:T(8,128)(2,1)S(1)} %collective-permute-done, bf16[200,5760]{1,0:T(8,128)(2,1)S(1)} %copy-done.1, bf16[200,1440]{1,0:T(8,128)(2,1)} %collective-permute-done.1), dimensions={1} | concatenate | bytes 6912000 | tf_op jit(solution)/shard_map/concatenate | solution.py:18
  268.5 5.6 %convert_element_type.74 = f32[200,8640]{1,0:T(8,128)} convert(bf16[200,8640]{1,0:T(8,128)(2,1)} %concatenate.3) | non-fusion elementwise | flops 1728000 | bytes 10368000 | tf_op jit(solution)/shard_map/convert_element_type | solution.py:38
  274.1 4.9 %fusion.60 = bf16[45,128,128]{2,0,1:T(8,128)(2,1)S(1)} fusion(bf16[32,8,128,128]{3,1,2,0:T(8,128)(2,1)} %all-to-all-done.1, s32[256]{0:T(256)S(1)} %eq.94), kind=kOutput, calls=%fused_computation.74 | convolution fusion | flops 378236160 | bytes 9864192 | tf_op jit(solution)/shard_map/ks,sif->kif/dot_general | solution.py:164
  279.0 1.5 copy.33
  280.5 24.0 %fusion.92 = (f32[5760]{0:T(1024)S(1)}, f32[200,5760]{1,0:T(8,128)}) fusion(bf16[5760,128]{1,0:T(8,128)(2,1)} %bitcast.57, bf16[128,200]{0,1:T(8,128)(2,1)S(1)} %copy-done.9, f32[200]{0:T(256)S(1)} %bitcast.65, f32[200,8640]{1,0:T(8,128)} %convert_element_type.74, f32[200]{0:T(256)S(1)} %bitcast.66, f32[200]{0:T(256)S(1)} %bitcast.59, ...), kind=kOutput, calls=%fused_computation.116 | convolution fusion | flops 323706240 | bytes 45394720 | tf_op jit(solution)/shard_map/dot_general | solution.py:62
  304.6 2.8 multiply_reduce_fusion
  307.5 10.5 %fusion.22 = bf16[200,5760]{1,0:T(8,128)(2,1)} fusion(bf16[800,200]{0,1:T(8,128)(2,1)S(1)} %copy-done, bf16[200,5760]{1,0:T(8,128)(2,1)S(1)} %copy-done.1, bf16[200,800]{1,0:T(8,128)(2,1)S(1)} %copy-done.8, f32[200,5760]{1,0:T(8,128)} %get-tuple-element.14, f32[200]{0:T(256)S(1)} %copy-done.10, f32[5760]{0:T(1024)S(1)} %add_rsqrt_fusion, ...), kind=kOutput, calls=%fused_computation.32 | convolution fusion | flops 3737088000 | bytes 9925920 | tf_op jit(solution)/shard_map/dot_general | solution.py:72
  (31 shorter events, 0.1 us)
Async XLA Ops:
  0.6 306.8 %copy-start = (bf16[800,200]{0,1:T(8,128)(2,1)S(1)}, bf16[800,200]{0,1:T(8,128)(2,1)}, u32[]{:S(2)}) copy-start(bf16[800,200]{0,1:T(8,128)(2,1)} %param.31) | copy-start | bytes 960004
  3.0 48.6 %all-to-all-start = ((s32[32,1,8]{2,1,0:T(1,128)}), s32[32,1,8]{2,1,0:T(1,128)S(1)}, u32[]{:S(2)}, u32[]{:S(2)}) async-start(s32[32,1,8]{2,1,0:T(1,128)} %bitcast.10), calls=%async_computation | async-start | bytes 32768 | tf_op jit(solution)/shard_map/all_to_all | solution.py:149
  13.3 13.8 %copy-start.4 = (bf16[1024,128]{1,0:T(8,128)(2,1)S(1)}, bf16[1024,128]{1,0:T(8,128)(2,1)}, u32[]{:S(2)}) copy-start(bf16[1024,128]{1,0:T(8,128)(2,1)} %param.20) | copy-start | bytes 786436
  13.3 14.7 %copy-start.7 = (s32[128]{0:T(128)S(1)}, s32[128]{0:T(128)}, u32[]{:S(2)}) copy-start(s32[128]{0:T(128)} %param.21) | copy-start | bytes 1540
  27.1 3.4 %copy-start.3 = (bf16[1024,1024]{1,0:T(8,128)(2,1)}, bf16[1024,1024]{1,0:T(8,128)(2,1)S(1)}, u32[]{:S(2)}) copy-start(bf16[1024,1024]{1,0:T(8,128)(2,1)S(1)} %fusion.45) | copy-start | bytes 6291460
  29.2 2.2 copy-start.2
  51.6 5.9 %copy-start.1 = (bf16[200,5760]{1,0:T(8,128)(2,1)S(1)}, bf16[200,5760]{1,0:T(8,128)(2,1)}, u32[]{:S(2)}) copy-start(bf16[200,5760]{1,0:T(8,128)(2,1)} %param.25) | copy-start | bytes 6912004
  51.6 13.0 %copy-start.5 = (s32[5760]{0:T(1024)S(1)}, s32[5760]{0:T(1024)}, u32[]{:S(2)}) copy-start(s32[5760]{0:T(1024)} %param.26) | copy-start | bytes 69124
  51.6 13.1 %copy-start.6 = (f32[200,9]{0,1:T(8,128)S(1)}, f32[200,9]{0,1:T(8,128)}, u32[]{:S(2)}) copy-start(f32[200,9]{0,1:T(8,128)} %param.27) | copy-start | bytes 21604
  51.6 222.4 %all-to-all-start.1 = ((bf16[32,8,128,128]{3,1,2,0:T(8,128)(2,1)}), bf16[32,8,128,128]{3,1,2,0:T(8,128)(2,1)}, u32[]{:S(2)}, u32[]{:S(2)}) async-start(bf16[32,8,128,128]{3,1,2,0:T(8,128)(2,1)} %fusion.23), calls=%async_computation.1 | async-start | bytes 16777216 | tf_op jit(solution)/shard_map/all_to_all | solution.py:142
  58.8 198.6 %collective-permute-start = (bf16[200,1440]{1,0:T(8,128)(2,1)}, bf16[200,1440]{1,0:T(8,128)(2,1)S(1)}, u32[]{:S(2)}, u32[]{:S(2)}) collective-permute-start(bf16[200,1440]{1,0:T(8,128)(2,1)} %get-tuple-element.3), channel_id=1, source_target_pairs={{0,1},{1,2},{2,3},{3,4},{4,5},{5,6},{6,7},{7,8},{8,9},{9,10},{10,1... | collective-permute-start | bytes 1728008 | tf_op jit(solution)/shard_map/ppermute | solution.py:14
  62.2 199.1 %collective-permute-start.1 = (bf16[200,1440]{1,0:T(8,128)(2,1)}, bf16[200,1440]{1,0:T(8,128)(2,1)}, u32[]{:S(2)}, u32[]{:S(2)}) collective-permute-start(bf16[200,1440]{1,0:T(8,128)(2,1)} %get-tuple-element.2), channel_id=1, source_target_pairs={{1,0},{2,1},{3,2},{4,3},{5,4},{6,5},{7,6},{8,7},{9,8},{10,9},{11,1... | collective-permute-start | bytes 1728008 | tf_op jit(solution)/shard_map/ppermute | solution.py:17
  274.1 6.5 %copy-start.9 = (bf16[128,200]{0,1:T(8,128)(2,1)S(1)}, bf16[128,200]{0,1:T(8,128)(2,1)}, u32[]{:S(2)}) copy-start(bf16[128,200]{0,1:T(8,128)(2,1)} %param.28) | copy-start | bytes 153604
  304.5 2.9 copy-start.8
  304.5 2.9 copy-start.10

commit v2 on v0

v2 whole, which is shorter than its diff:
```python
import functools
import math

import jax
import jax.numpy as jnp
from jax import lax
from jax.experimental import pallas as pl
from jax.experimental.pallas import tpu as pltpu
from jax.sharding import Mesh, PartitionSpec as P

OX = 1440
ALL = ("sec", "half", "near")
PEERS = ("sec", "near")
F32 = jnp.float32
BF16 = jnp.bfloat16


def gelu(x):
    half = 0.5 * x
    return half + half * jnp.tanh(x * (0.7978845608028654 + 0.035677408136300125 * (x * x)))


def normalised(values, axis):
    centred = values - jnp.mean(values, axis=axis, keepdims=True)
    spread_sq = jnp.mean(centred * centred, axis=axis, keepdims=True)
    return centred * lax.rsqrt(spread_sq + 1e-05)


def whole(shape):
    return pl.BlockSpec(shape, lambda *_: (0,) * len(shape))


def atm_kernel(x_ref, gain_ref, up_ref, down_ref, flux_ref, next_ref, surface_ref, normed, total):
    step = pl.program_id(0)

    @pl.when(step == 0)
    def _():
        values = x_ref[...].astype(F32)
        normed[...] = (normalised(values, -1) * gain_ref[...]).astype(BF16)
        total[...] = values

    hidden = gelu(jnp.dot(normed[...], up_ref[...], preferred_element_type=F32)).astype(BF16)
    total[...] += jnp.dot(hidden, down_ref[...], preferred_element_type=F32)

    @pl.when(step == pl.num_programs(0) - 1)
    def _():
        updated = total[...].astype(BF16)
        next_ref[...] = updated
        surface_ref[...] = jnp.dot(updated, flux_ref[...], preferred_element_type=F32).astype(BF16)


def atmosphere(columns, gain, w_up, w_down, w_flux):
    rows, width = columns.shape
    hidden = w_up.shape[1]
    part = hidden // 4
    return pl.pallas_call(
        atm_kernel,
        name="atmosphere",
        grid=(hidden // part,),
        in_specs=[
            whole((rows, width)),
            whole((1, width)),
            pl.BlockSpec((width, part), lambda i: (0, i)),
            pl.BlockSpec((part, width), lambda i: (i, 0)),
            whole(w_flux.shape),
        ],
        out_specs=[whole((rows, width)), whole((rows, w_flux.shape[1]))],
        out_shape=[
            jax.ShapeDtypeStruct((rows, width), BF16),
            jax.ShapeDtypeStruct((rows, w_flux.shape[1]), BF16),
        ],
        scratch_shapes=[pltpu.VMEM((rows, width), BF16), pltpu.VMEM((rows, width), F32)],
        compiler_params=pltpu.CompilerParams(vmem_limit_bytes=48 << 20),
    )(columns, gain[None, :], w_up, w_down, w_flux)


def remap_kernel(first, group, slot_ref, source_ref, surface_ref, weight_ref, out_ref, made, sems):
    step = pl.program_id(0)
    slots = out_ref.shape[0]
    entries = made.shape[0]

    def copy(entry):
        slot = slot_ref[entry] - first
        return pltpu.make_async_copy(made.at[entry], out_ref.at[slot], sems.at[entry])

    def mine(entry):
        slot = slot_ref[entry] - first
        return (slot >= 0) & (slot < slots)

    for i in range(group):
        entry = step * group + i

        @pl.when(mine(entry))
        def _():
            made[entry] = jnp.dot(
                weight_ref[i], surface_ref[source_ref[entry]], preferred_element_type=F32
            ).astype(BF16)
            copy(entry).start()

    @pl.when(step == pl.num_programs(0) - 1)
    def _():
        def drain(entry, carry):
            @pl.when(mine(entry))
            def _():
                copy(entry).wait()

            return carry

        lax.fori_loop(0, entries, drain, 0)


def remapped(first, slots, slot_of, source, surface, weights):
    entries, block, _ = weights.shape
    group = 16 if entries % 16 == 0 else 1
    return pl.pallas_call(
        functools.partial(remap_kernel, first, group),
        name="remap",
        grid_spec=pltpu.PrefetchScalarGridSpec(
            num_scalar_prefetch=2,
            grid=(entries // group,),
            in_specs=[
                whole(surface.shape),
                pl.BlockSpec((group, block, block), lambda i, *_: (i, 0, 0)),
            ],
            out_specs=pl.BlockSpec(memory_space=pltpu.HBM),
            scratch_shapes=[
                pltpu.VMEM((entries, block, surface.shape[2]), BF16),
                pltpu.SemaphoreType.DMA((entries,)),
            ],
        ),
        out_shape=pltpu.HBM((slots, block, surface.shape[2]), BF16),
        compiler_params=pltpu.CompilerParams(vmem_limit_bytes=32 << 20),
    )(slot_of, source, surface, weights)


def merge_kernel(group, label_ref, arrived_ref, out_ref, total):
    step = pl.program_id(0)

    @pl.when(step == 0)
    def _():
        total[...] = jnp.zeros_like(total)

    for i in range(group):
        label = label_ref[step * group + i]

        @pl.when(label >= 0)
        def _():
            total[label] += arrived_ref[i].astype(F32)

    @pl.when(step == pl.num_programs(0) - 1)
    def _():
        out_ref[...] = total[...].astype(BF16)


def merged(labels, arrived, blocks):
    slots, block, features = arrived.shape
    group = 16 if slots % 16 == 0 else 1
    return pl.pallas_call(
        functools.partial(merge_kernel, group),
        name="merge",
        grid_spec=pltpu.PrefetchScalarGridSpec(
            num_scalar_prefetch=1,
            grid=(slots // group,),
            in_specs=[pl.BlockSpec((group, block, features), lambda i, *_: (i, 0, 0))],
            out_specs=whole((blocks, block, features)),
            scratch_shapes=[pltpu.VMEM((blocks, block, features), F32)],
        ),
        out_shape=jax.ShapeDtypeStruct((blocks, block, features), BF16),
        compiler_params=pltpu.CompilerParams(vmem_limit_bytes=32 << 20),
    )(labels, arrived)


def ocean_kernel(mix_ref, near_ref, far_ref, now_ref, sea_ref, force_ref, gain_ref, up_ref, down_ref, out_ref):
    forcing = (near_ref[...].astype(F32) + far_ref[...].astype(F32)).astype(BF16)
    driven = mix_ref[...] + lax.dot_general(
        force_ref[...], forcing, (((1,), (1,)), ((), ())), preferred_element_type=F32
    )
    normed = (normalised(driven, 0) * gain_ref[...]).astype(BF16)
    hidden = gelu(jnp.dot(up_ref[...], normed, preferred_element_type=F32)).astype(BF16)
    change = jnp.dot(down_ref[...], hidden, preferred_element_type=F32)
    out_ref[...] = (
        now_ref[...].astype(F32) + sea_ref[...].astype(F32) * change
    ).astype(BF16)


def ocean(mixing, near, far, now, sea, w_force, gain, w_up, w_down):
    channels, cells = now.shape
    features = near.shape[1]
    part = cells // 5
    if part % 128:
        part = cells
    tall = pl.BlockSpec((channels, part), lambda i: (0, i))
    flat = pl.BlockSpec((part, features), lambda i: (i, 0))
    return pl.pallas_call(
        ocean_kernel,
        name="ocean",
        grid=(cells // part,),
        in_specs=[
            tall,
            flat,
            flat,
            tall,
            pl.BlockSpec((1, part), lambda i: (0, i)),
            whole(w_force.shape),
            whole((channels, 1)),
            whole(w_up.shape),
            whole(w_down.shape),
        ],
        out_specs=tall,
        out_shape=jax.ShapeDtypeStruct((channels, cells), BF16),
        compiler_params=pltpu.CompilerParams(vmem_limit_bytes=48 << 20),
    )(mixing, near, far, now, sea[None, :], w_force, gain[:, None], w_up, w_down)


def edge_rows(block):
    count = math.prod(lax.axis_size(axis) for axis in ALL)
    forward = [(i, i + 1) for i in range(count - 1)]
    backward = [(target, source) for source, target in forward]
    low = lax.ppermute(block[:, -OX:], ALL, forward)
    high = lax.ppermute(block[:, :OX], ALL, backward)
    return low, high


def flat_mixing(padded_flat, kernel, row_len, cell_count):
    extended = jnp.pad(padded_flat.astype(F32), ((0, 0), (row_len, row_len)))
    column_at = (jnp.arange(cell_count, dtype=jnp.int32) % row_len)[None, :]
    first_col = column_at == 0
    last_col = column_at == row_len - 1

    def window(offset):
        return lax.slice_in_dim(extended, row_len + offset, row_len + offset + cell_count, axis=1)

    summed = jnp.zeros((padded_flat.shape[0], cell_count), F32)
    for row_step in range(3):
        base = row_step * row_len
        for col_step in range(3):
            if col_step == 0:
                shifted = jnp.where(first_col, window(base + row_len - 1), window(base - 1))
            elif col_step == 2:
                shifted = jnp.where(last_col, window(base - row_len + 1), window(base + 1))
            else:
                shifted = window(base)
            summed = summed + kernel[:, 3 * row_step + col_step][:, None] * shifted
    return summed


def local(
    atm_state,
    gain_atm,
    w_up_atm,
    w_down_atm,
    w_flux,
    ent_source,
    ent_target,
    ent_block,
    remap_weights,
    ocean_state,
    land_sea,
    conv_kernel,
    w_force,
    gain_ocn,
    w_up_ocn,
    w_down_ocn,
):
    sections, halves, nears = (lax.axis_size(axis) for axis in ALL)
    sec, half, near = (lax.axis_index(axis) for axis in ALL)
    peers = sections * nears
    entries, block_rows, _ = remap_weights.shape
    capacity = max(2, 2 * entries // (peers * halves))
    slots = peers * capacity
    cell_count = ocean_state.shape[1]
    ocean_blocks = cell_count // block_rows
    low, high = edge_rows(ocean_state)

    targets = ent_target[:, 0]
    at = jnp.arange(entries, dtype=jnp.int32)
    rank = jnp.sum(
        ((targets[:, None] == targets[None, :]) & (at[:, None] > at[None, :])).astype(jnp.int32),
        axis=1,
    )
    peer = targets // (halves * nears) * nears + targets % nears
    far = targets // nears % halves != half
    slot_of = peer * capacity + rank + jnp.where(far, 0, slots)

    place = jnp.arange(2 * slots, dtype=jnp.int32)
    sent_labels = (
        jnp.sum(jnp.where(place[:, None] == slot_of[None, :], ent_block[None, :] + 1, 0), axis=1)
        - 1
    )
    sent_labels = sent_labels.reshape(2, peers, capacity).transpose(1, 0, 2)
    got_labels = lax.all_to_all(
        sent_labels.reshape(peers, 2 * capacity), PEERS, split_axis=0, concat_axis=0, tiled=True
    ).reshape(peers, 2, capacity)
    far_labels = got_labels[:, 0].reshape(slots)
    near_labels = got_labels[:, 1].reshape(slots)

    atm_next, surface = atmosphere(atm_state, gain_atm, w_up_atm, w_down_atm, w_flux)
    surface = surface.reshape(-1, block_rows, surface.shape[1])
    surface, low, high, far_labels, near_labels = lax.optimization_barrier(
        (surface, low, high, far_labels, near_labels)
    )

    def exchange(values):
        return lax.all_to_all(values, PEERS, split_axis=0, concat_axis=0, tiled=True)

    far_arrived = exchange(remapped(0, slots, slot_of, ent_source, surface, remap_weights))
    near_made = remapped(slots, slots, slot_of, ent_source, surface, remap_weights)
    padded = jnp.concatenate([low, ocean_state, high], axis=1)
    mixing = flat_mixing(padded, conv_kernel, OX, cell_count)
    far_arrived, near_made, mixing = lax.optimization_barrier((far_arrived, near_made, mixing))
    near_arrived = exchange(near_made)
    far_sum = merged(far_labels, far_arrived, ocean_blocks)
    far_sum = lax.ppermute(far_sum, "half", [(0, 1), (1, 0)])
    near_sum = merged(near_labels, near_arrived, ocean_blocks)
    features = far_sum.shape[2]
    ocean_next = ocean(
        mixing,
        near_sum.reshape(cell_count, features),
        far_sum.reshape(cell_count, features),
        ocean_state,
        land_sea,
        w_force.T,
        gain_ocn,
        w_up_ocn.T,
        w_down_ocn.T,
    )
    return (atm_next, ocean_next)


def solution(mesh):
    sections, tiles = mesh.shape["sec"], mesh.shape["tile"]
    fine = Mesh(mesh.devices.reshape(sections, 2, tiles // 2), ALL)
    placed = (
        P(ALL, None),
        P(),
        P(),
        P(),
        P(),
        P(ALL),
        P(ALL, None),
        P(ALL),
        P(ALL, None, None),
        P(None, ALL),
        P(ALL),
        P(),
        P(),
        P(),
        P(),
        P(),
    )
    return jax.shard_map(
        local,
        mesh=fine,
        in_specs=placed,
        out_specs=(P(ALL, None), P(None, ALL)),
        check_vma=False,
    )
```

time: 320 us -> 218 us (0.68)
  waiting for transfers between devices: 195 us -> 89.5 us
  matrix products: 68.3 us -> 0 us
  Pallas kernels: 0 us -> 65.1 us
  starting transfers between devices: 17.7 us -> 24.5 us
    ppermute x2 -> x3, waiting for transfers between devices: 195 us -> 3.22 us  [the longest x1 3.21 us: local(): far_sum = lax.ppermute(far_sum, 'half', [(0, 1), (1, 0)])]
    all_to_all x2 -> x3, waiting for transfers between devices: 0.01 us -> 86.3 us  [the longest x2 86.2 us: exchange(): lax.all_to_all(values, PEERS, split_axis=0, concat_axis=0, tiled=True)]
    dot_general x8 -> x0, matrix products: 68.3 us -> none  [the longest x1 24.1 us: ocean_update(): lax.dot_general(w_force, forcing, contract, preferred_element_type=jnp.fl...]
    pallas_call x0 -> x6, Pallas kernels: none -> 65.1 us  [the longest x2 23.9 us: remapped(): pl.pallas_call(functools.partial(remap_kernel, first, group), name='remap...]
    add x1 -> x2, other arithmetic: 0.68 us -> 14.1 us  [the longest x1 13.4 us: flat_mixing(): summed = summed + kernel[:, 3 * row_step + col_step][:, None] * shifted]
    convert_element_type x2 -> x0, local copies, waits for them, and re-layouts: 8.77 us -> none  [the longest x1 7.28 us: local(): payload = jnp.einsum('eij,ejf->eif', remap_weights, picked, preferred_ele...]
    reduce_sum x5 -> x2, other arithmetic: 7.99 us -> 1.01 us  [the longest x1 0.9 us: local(): jnp.sum(((targets[:, None] == targets[None, :]) & (at[:, None] > at[None,...]
    unnamed x23 -> x29, local copies, waits for them, and re-layouts: 2.22 us -> 8.64 us
  transfers between devices with their start and end apart: 4 -> 6, of which waited for: 2 -> 3; matrix products, arithmetic and copies ran while one was open for 18% -> 12% of each run, Pallas kernels for 0% -> 18%
where the time goes in v2:
time: 218 us; the launch traced here: 217 us
  waiting for transfers between devices  89.5 us (41%)
  Pallas kernels  65.1 us (30%)
  starting transfers between devices  24.5 us (11%)
  local copies, waits for them, and re-layouts  18.6 us (9%)
  other arithmetic  17.9 us (8%)
    all_to_all x2, waiting for transfers between devices, exchange(): lax.all_to_all(values, PEERS, split_axis=0, concat_axis=0, tiled=True)  86.2 us
    pallas_call x2, Pallas kernels, remapped(): pl.pallas_call(functools.partial(remap_kernel, first, group), name='remap...  23.9 us
    pallas_call x1, Pallas kernels, atmosphere(): pl.pallas_call(atm_kernel, name='atmosphere', grid=(hidden // part,), in_...  15.2 us
    add x1, other arithmetic, flat_mixing(): summed = summed + kernel[:, 3 * row_step + col_step][:, None] * shifted  13.4 us
    pallas_call x2, Pallas kernels, merged(): pl.pallas_call(functools.partial(merge_kernel, group), name='merge', grid...  13.3 us
    pallas_call x1, Pallas kernels, ocean(): pl.pallas_call(ocean_kernel, name='ocean', grid=(cells // part,), in_spec...  12.6 us
    all_to_all x2, starting transfers between devices, exchange(): lax.all_to_all(values, PEERS, split_axis=0, concat_axis=0, tiled=True)  12.1 us
    unnamed x29, local copies, waits for them, and re-layouts  8.64 us
  transfers between devices with their start and end apart: 6, of which 3 were waited for; matrix products, arithmetic and copies ran while one was open for 12% of the time, Pallas kernels for 18%

profile of v2, /device:TPU:14, one launch (start us, length us, event | category | flops | bytes accessed | tf_op | source)
XLA Modules:
  0.0 216.5 jit_solution(6103852887020761517)
XLA Ops:
  0.6 1.5 fusion.25
  2.1 3.4 %collective-permute-start = (bf16[200,1440]{1,0:T(8,128)(2,1)S(1)}, bf16[200,1440]{1,0:T(8,128)(2,1)S(1)}, u32[]{:S(2)}, u32[]{:S(2)}) collective-permute-start(bf16[200,1440]{1,0:T(8,128)(2,1)S(1)} %get-tuple-element.23), channel_id=1, source_target_pairs={{0,1},{1,2},{2,3},{3,4},{4,5},{5,6},{6,7},{7,8},{8,9},{9,10},{10,1... | collective-permute-start | bytes 1728008 | tf_op jit(solution)/shard_map/ppermute | solution.py:219
  5.5 2.4 %collective-permute-start.1 = (bf16[200,1440]{1,0:T(8,128)(2,1)S(1)}, bf16[200,1440]{1,0:T(8,128)(2,1)S(1)}, u32[]{:S(2)}, u32[]{:S(2)}) collective-permute-start(bf16[200,1440]{1,0:T(8,128)(2,1)S(1)} %get-tuple-element.22), channel_id=1, source_target_pairs={{1,0},{2,1},{3,2},{4,3},{5,4},{6,5},{7,6},{8,7},{9,8},{10,9},{11,1... | collective-permute-start | bytes 1728008 | tf_op jit(solution)/shard_map/ppermute | solution.py:220
  8.0 0.9 convert_reduce_fusion
  8.9 0.7 fusion.23
  9.6 0.1 select_reduce_fusion
  9.9 0.7 copy.32
  10.6 5.2 %all-to-all-start = ((s32[16,1,16]{2,1,0:T(1,128)}), s32[16,1,16]{2,1,0:T(1,128)S(1)}, u32[]{:S(2)}, u32[]{:S(2)}) async-start(s32[16,1,16]{2,1,0:T(1,128)} %copy.32), calls=%async_computation | async-start | bytes 16384 | tf_op jit(solution)/shard_map/all_to_all | solution.py:291
  15.8 1.6 copy-done.3
  17.4 0.9 copy-done.5
  18.4 0.7 copy-done.7
  19.0 15.2 %atmosphere.1 = (bf16[1024,1024]{1,0:T(8,128)(2,1)}, bf16[1024,128]{1,0:T(8,128)(2,1)S(1)}) custom-call(bf16[1024,1024]{1,0:T(8,128)(2,1)S(1)} %copy-done.3, f32[1,1024]{1,0:T(1,128)S(1)} %bitcast.32, bf16[1024,2048]{1,0:T(8,128)(2,1)} %up_ref.1, bf16[2048,1024]{1,0:T(8,128)(2,1)} %down_ref.1, bf16[1024,128]{1,0:T(8,128)(2,1)S(1)} %copy-done.5), custom_call_target="tpu_custom_call" | custom-call | tf_op jit(solution)/shard_map/atmosphere/pallas_call | solution.py:56
  34.6 0.1 reshape_squeeze.7.label_ref
  34.7 0.8 copy-done.9
  35.5 2.2 %copy-done = bf16[128,128,128]{2,1,0:T(8,128)(2,1)S(1)} copy-done((bf16[128,128,128]{2,1,0:T(8,128)(2,1)S(1)}, bf16[128,128,128]{2,1,0:T(8,128)(2,1)}, u32[]{:S(2)}) %copy-start) | copy-done | bytes 4194328
  37.7 12.5 %remap.2 = bf16[128,128,128]{2,1,0:T(8,128)(2,1)} custom-call(s32[128]{0:T(128)S(1)} %get-tuple-element.35.slot_ref, s32[128]{0:T(128)S(1)} %copy-done.8, bf16[8,128,128]{2,1,0:T(8,128)(2,1)S(1)} %bitcast.28, bf16[128,128,128]{2,1,0:T(8,128)(2,1)S(1)} %copy-done), custom_call_target="tpu_custom_call" | custom-call | tf_op jit(solution)/shard_map/remap/pallas_call | solution.py:115
  50.2 5.3 %all-to-all-start.1 = ((bf16[128,128,128]{2,1,0:T(8,128)(2,1)}), bf16[128,128,128]{2,1,0:T(8,128)(2,1)}, u32[]{:S(2)}, u32[]{:S(2)}) async-start(bf16[128,128,128]{2,1,0:T(8,128)(2,1)} %remap.2), calls=%async_computation.1 | async-start | bytes 8388608 | tf_op jit(solution)/shard_map/all_to_all | solution.py:304
  55.5 2.2 %copy-done.1 = bf16[128,128,128]{2,1,0:T(8,128)(2,1)S(1)} copy-done((bf16[128,128,128]{2,1,0:T(8,128)(2,1)S(1)}, bf16[128,128,128]{2,1,0:T(8,128)(2,1)}, u32[]{:S(2)}) %copy-start.1) | copy-done | bytes 4194328
  57.7 11.5 %remap.3 = bf16[128,128,128]{2,1,0:T(8,128)(2,1)} custom-call(s32[128]{0:T(128)S(1)} %get-tuple-element.35.slot_ref, s32[128]{0:T(128)S(1)} %copy-done.8, bf16[8,128,128]{2,1,0:T(8,128)(2,1)S(1)} %bitcast.29, bf16[128,128,128]{2,1,0:T(8,128)(2,1)S(1)} %copy-done.1), custom_call_target="tpu_custom_call" | custom-call | tf_op jit(solution)/shard_map/remap/pallas_call | solution.py:115
  69.2 7.1 %concatenate.3 = bf16[200,8640]{1,0:T(8,128)(2,1)} concatenate(bf16[200,1440]{1,0:T(8,128)(2,1)S(1)} %collective-permute-done, bf16[200,5760]{1,0:T(8,128)(2,1)S(1)} %copy-done.2, bf16[200,1440]{1,0:T(8,128)(2,1)} %copy-done.9), dimensions={1} | concatenate | bytes 6912000 | tf_op jit(solution)/shard_map/concatenate | solution.py:308
  76.3 2.8 %convert_element_type.9 = f32[200,8640]{1,0:T(8,128)S(1)} convert(bf16[200,8640]{1,0:T(8,128)(2,1)} %concatenate.3) | non-fusion elementwise | flops 1728000 | bytes 10368000 | tf_op jit(solution)/shard_map/convert_element_type | solution.py:225
  79.1 13.4 %fusion.9.mix_ref = f32[200,5760]{1,0:T(8,128)} fusion(f32[200,8640]{1,0:T(8,128)S(1)} %convert_element_type.9, f32[200]{0:T(256)S(1)} %bitcast.43, f32[200]{0:T(256)S(1)} %bitcast.44, f32[200]{0:T(256)S(1)} %bitcast.37, f32[200]{0:T(256)S(1)} %bitcast.38, f32[200]{0:T(256)S(1)} %bitcast.39, f32[200]{0:T(256)S(1)} %bitcast.40, f32[200]{0:T(256)S(1)} %bitcast.41, ...), kind=kLoop, calls=%fused_computation.13 | loop fusion | flops 26496000 | bytes 43848704 | tf_op jit(solution)/shard_map/add | solution.py:243
  92.5 17.0 %all-to-all-done.1.arrived_ref = bf16[128,128,128]{2,1,0:T(8,128)(2,1)} async-done(((bf16[128,128,128]{2,1,0:T(8,128)(2,1)}), bf16[128,128,128]{2,1,0:T(8,128)(2,1)}, u32[]{:S(2)}, u32[]{:S(2)}) %all-to-all-start.1) | async-done | bytes 4194336 | tf_op jit(solution)/shard_map/all_to_all | solution.py:304
  109.5 6.9 %all-to-all-start.2 = ((bf16[128,128,128]{2,1,0:T(8,128)(2,1)}), bf16[128,128,128]{2,1,0:T(8,128)(2,1)}, u32[]{:S(2)}, u32[]{:S(2)}) async-start(bf16[128,128,128]{2,1,0:T(8,128)(2,1)} %remap.3), calls=%async_computation.2 | async-start | bytes 8388608 | tf_op jit(solution)/shard_map/all_to_all | solution.py:304
  116.4 7.3 %merge.3 = bf16[45,128,128]{2,1,0:T(8,128)(2,1)} custom-call(s32[128]{0:T(128)S(1)} %reshape_squeeze.6.label_ref, bf16[128,128,128]{2,1,0:T(8,128)(2,1)} %all-to-all-done.1.arrived_ref), custom_call_target="tpu_custom_call" | custom-call | tf_op jit(solution)/shard_map/merge/pallas_call | solution.py:158
  123.7 1.3 collective-permute-start.2
  125.0 0.2 copy.36
  125.2 0.1 copy.37.gain_ref
  125.3 69.3 %all-to-all-done.2.arrived_ref = bf16[128,128,128]{2,1,0:T(8,128)(2,1)} async-done(((bf16[128,128,128]{2,1,0:T(8,128)(2,1)}), bf16[128,128,128]{2,1,0:T(8,128)(2,1)}, u32[]{:S(2)}, u32[]{:S(2)}) %all-to-all-start.2) | async-done | bytes 4194336 | tf_op jit(solution)/shard_map/all_to_all | solution.py:304
  194.6 6.0 %merge.2 = bf16[45,128,128]{2,1,0:T(8,128)(2,1)S(1)} custom-call(s32[128]{0:T(128)S(1)} %reshape_squeeze.7.label_ref, bf16[128,128,128]{2,1,0:T(8,128)(2,1)} %all-to-all-done.2.arrived_ref), custom_call_target="tpu_custom_call" | custom-call | tf_op jit(solution)/shard_map/merge/pallas_call | solution.py:158
  200.6 3.2 %collective-permute-done.2 = bf16[45,128,128]{2,1,0:T(8,128)(2,1)} collective-permute-done((bf16[45,128,128]{2,1,0:T(8,128)(2,1)}, bf16[45,128,128]{2,1,0:T(8,128)(2,1)}, u32[]{:S(2)}, u32[]{:S(2)}) %collective-permute-start.2) | collective-permute-done | bytes 1474592 | tf_op jit(solution)/shard_map/ppermute | solution.py:313
  203.9 12.6 %ocean.1 = bf16[200,5760]{1,0:T(8,128)(2,1)} custom-call(f32[200,5760]{1,0:T(8,128)} %fusion.9.mix_ref, bf16[5760,128]{1,0:T(8,128)(2,1)S(1)} %bitcast.26, bf16[5760,128]{1,0:T(8,128)(2,1)} %bitcast.16.far_ref, bf16[200,5760]{1,0:T(8,128)(2,1)S(1)} %copy-done.2, s32[1,5760]{1,0:T(1,128)S(1)} %broadcast_in_dim.72.sea_ref, bf16[200,128]{1,0:T(8,128)(2,1)S(1)} %bitcast.31, ...), custom_call_target="tpu_custom_call" | custom-call | tf_op jit(solution)/shard_map/ocean/pallas_call | solution.py:194
  (36 shorter events, 0.6 us)
Async XLA Ops:
  2.1 32.5 %collective-permute-start = (bf16[200,1440]{1,0:T(8,128)(2,1)S(1)}, bf16[200,1440]{1,0:T(8,128)(2,1)S(1)}, u32[]{:S(2)}, u32[]{:S(2)}) collective-permute-start(bf16[200,1440]{1,0:T(8,128)(2,1)S(1)} %get-tuple-element.23), channel_id=1, source_target_pairs={{0,1},{1,2},{2,3},{3,4},{4,5},{5,6},{6,7},{7,8},{8,9},{9,10},{10,1... | collective-permute-start | bytes 1728008 | tf_op jit(solution)/shard_map/ppermute | solution.py:219
  5.5 29.1 %collective-permute-start.1 = (bf16[200,1440]{1,0:T(8,128)(2,1)S(1)}, bf16[200,1440]{1,0:T(8,128)(2,1)S(1)}, u32[]{:S(2)}, u32[]{:S(2)}) collective-permute-start(bf16[200,1440]{1,0:T(8,128)(2,1)S(1)} %get-tuple-element.22), channel_id=1, source_target_pairs={{1,0},{2,1},{3,2},{4,3},{5,4},{6,5},{7,6},{8,7},{9,8},{10,9},{11,1... | collective-permute-start | bytes 1728008 | tf_op jit(solution)/shard_map/ppermute | solution.py:220
  10.6 23.7 %all-to-all-start = ((s32[16,1,16]{2,1,0:T(1,128)}), s32[16,1,16]{2,1,0:T(1,128)S(1)}, u32[]{:S(2)}, u32[]{:S(2)}) async-start(s32[16,1,16]{2,1,0:T(1,128)} %copy.32), calls=%async_computation | async-start | bytes 16384 | tf_op jit(solution)/shard_map/all_to_all | solution.py:291
  15.8 1.6 copy-start.3
  17.4 0.9 copy-start.5
  18.4 0.7 copy-start.7
  19.0 16.5 %copy-start.8 = (s32[128]{0:T(128)S(1)}, s32[128]{0:T(128)}, u32[]{:S(2)}) copy-start(s32[128]{0:T(128)} %source_ref.3) | copy-start | bytes 1540
  34.7 0.8 copy-start.9
  35.5 2.2 %copy-start = (bf16[128,128,128]{2,1,0:T(8,128)(2,1)S(1)}, bf16[128,128,128]{2,1,0:T(8,128)(2,1)}, u32[]{:S(2)}) copy-start(bf16[128,128,128]{2,1,0:T(8,128)(2,1)} %weight_ref.3) | copy-start | bytes 12582916
  50.2 5.3 %copy-start.12 = (f32[200,9]{0,1:T(8,128)S(1)}, f32[200,9]{0,1:T(8,128)}, u32[]{:S(2)}) copy-start(f32[200,9]{0,1:T(8,128)} %param.27) | copy-start | bytes 21604
  50.2 19.0 %copy-start.2 = (bf16[200,5760]{1,0:T(8,128)(2,1)S(1)}, bf16[200,5760]{1,0:T(8,128)(2,1)}, u32[]{:S(2)}) copy-start(bf16[200,5760]{1,0:T(8,128)(2,1)} %now_ref.1) | copy-start | bytes 6912004
  50.2 59.3 %all-to-all-start.1 = ((bf16[128,128,128]{2,1,0:T(8,128)(2,1)}), bf16[128,128,128]{2,1,0:T(8,128)(2,1)}, u32[]{:S(2)}, u32[]{:S(2)}) async-start(bf16[128,128,128]{2,1,0:T(8,128)(2,1)} %remap.2), calls=%async_computation.1 | async-start | bytes 8388608 | tf_op jit(solution)/shard_map/all_to_all | solution.py:304
  55.5 2.2 %copy-start.1 = (bf16[128,128,128]{2,1,0:T(8,128)(2,1)S(1)}, bf16[128,128,128]{2,1,0:T(8,128)(2,1)}, u32[]{:S(2)}) copy-start(bf16[128,128,128]{2,1,0:T(8,128)(2,1)} %weight_ref.3) | copy-start | bytes 12582916
  109.5 85.1 %all-to-all-start.2 = ((bf16[128,128,128]{2,1,0:T(8,128)(2,1)}), bf16[128,128,128]{2,1,0:T(8,128)(2,1)}, u32[]{:S(2)}, u32[]{:S(2)}) async-start(bf16[128,128,128]{2,1,0:T(8,128)(2,1)} %remap.3), calls=%async_computation.2 | async-start | bytes 8388608 | tf_op jit(solution)/shard_map/all_to_all | solution.py:304
  116.3 8.6 %copy-start.10 = (bf16[200,800]{1,0:T(8,128)(2,1)S(1)}, bf16[200,800]{1,0:T(8,128)(2,1)}, u32[]{:S(2)}) copy-start(bf16[200,800]{1,0:T(8,128)(2,1)} %param.30) | copy-start | bytes 960004
  116.4 8.8 %copy-start.13 = (f32[200]{0:T(256)S(1)}, f32[200]{0:T(256)}, u32[]{:S(2)}) copy-start(f32[200]{0:T(256)} %param.29) | copy-start | bytes 2404
  116.4 8.9 %copy-start.11 = (s32[5760]{0:T(1024)S(1)}, s32[5760]{0:T(1024)}, u32[]{:S(2)}) copy-start(s32[5760]{0:T(1024)} %param.26) | copy-start | bytes 69124
  123.7 80.2 %copy-start.4 = (bf16[800,200]{0,1:T(8,128)(2,1)S(1)}, bf16[800,200]{0,1:T(8,128)(2,1)}, u32[]{:S(2)}) copy-start(bf16[800,200]{0,1:T(8,128)(2,1)} %param.31) | copy-start | bytes 960004
  123.7 80.2 %copy-start.6 = (bf16[128,200]{0,1:T(8,128)(2,1)S(1)}, bf16[128,200]{0,1:T(8,128)(2,1)}, u32[]{:S(2)}) copy-start(bf16[128,200]{0,1:T(8,128)(2,1)} %param.28) | copy-start | bytes 153604
  123.7 80.2 %collective-permute-start.2 = (bf16[45,128,128]{2,1,0:T(8,128)(2,1)}, bf16[45,128,128]{2,1,0:T(8,128)(2,1)}, u32[]{:S(2)}, u32[]{:S(2)}) collective-permute-start(bf16[45,128,128]{2,1,0:T(8,128)(2,1)} %merge.3), channel_id=1, source_target_pairs={{0,8},{8,0},{1,9},{9,1},{2,10},{10,2},{3,11},{11,3},{4,12},{12,4},... | collective-permute-start | bytes 4423688 | tf_op jit(solution)/shard_map/ppermute | solution.py:313

commit v3 on v2

v3 whole, which is shorter than its diff:
```python
import functools
import math

import jax
import jax.numpy as jnp
from jax import lax
from jax.experimental import pallas as pl
from jax.experimental.pallas import tpu as pltpu
from jax.sharding import Mesh, PartitionSpec as P

OX = 1440
ALL = ("sec", "half", "near")
PEERS = ("sec", "near")
F32 = jnp.float32
BF16 = jnp.bfloat16


def gelu(x):
    half = 0.5 * x
    return half + half * jnp.tanh(x * (0.7978845608028654 + 0.035677408136300125 * (x * x)))


def normalised(values, axis):
    centred = values - jnp.mean(values, axis=axis, keepdims=True)
    spread_sq = jnp.mean(centred * centred, axis=axis, keepdims=True)
    return centred * lax.rsqrt(spread_sq + 1e-05)


def in_hbm(value):
    return pltpu.with_memory_space_constraint(value, pltpu.HBM)


def whole(shape):
    return pl.BlockSpec(shape, lambda *_: (0,) * len(shape))


def split(index, size):
    if size & (size - 1) == 0:
        return index >> (size.bit_length() - 1), index & (size - 1)
    return lax.div(index, size), lax.rem(index, size)


def pick(plan, want_far, half_ref, target_ref, listed, slots, counts):
    _, halves, nears, capacity = plan

    def none(tile, carry):
        counts[tile] = 0
        return carry

    def step(entry, count):
        target = target_ref[entry]
        rank = counts[target]
        counts[target] = rank + 1
        upper, near = split(target, nears)
        sec, half = split(upper, halves)
        listed[count] = entry
        slots[count] = (sec * nears + near) * capacity + rank
        far = (half != half_ref[0]).astype(jnp.int32)
        return count + (far if want_far else 1 - far)

    lax.fori_loop(0, counts.shape[0], none, 0)
    return lax.fori_loop(0, target_ref.shape[0], step, jnp.int32(0), unroll=4)


def multiply(plan, count, source_ref, block_ref, surface_ref, weights, listed, slots, made, labels, tile, out_ref, sems, tile_sem):
    capacity = plan[3]
    block = weights.shape[1]
    labels[...] = jnp.full_like(labels, -1)
    lane = lax.broadcasted_iota(jnp.int32, (1, labels.shape[1]), 1)

    def copy(at):
        peer, rank = split(slots[at], capacity)
        rows = pl.ds(pl.multiple_of(rank * block, block), block)
        return pltpu.make_async_copy(made.at[at], out_ref.at[peer, rows], sems.at[at])

    def group(size, first):
        for i in range(size):
            entry = listed[first + i]
            rows = pl.ds(pl.multiple_of(source_ref[entry] * block, block), block)
            made[first + i] = jnp.dot(
                weights[entry], surface_ref[rows, :], preferred_element_type=F32
            ).astype(BF16)
            peer, rank = split(slots[first + i], capacity)
            row = labels[pl.ds(peer, 1), :]
            labels[pl.ds(peer, 1), :] = jnp.where(lane == rank, block_ref[entry], row)
        for i in range(size):
            copy(first + i).start()

    def eight(i, carry):
        group(8, i * 8)
        return carry

    def one(i, carry):
        group(1, i)
        return carry

    def drain(i, carry):
        copy(i).wait()
        return carry

    full = count >> 3
    lax.fori_loop(0, full, eight, 0)
    lax.fori_loop(full * 8, count, one, 0)
    tile[...] = jnp.broadcast_to(labels[...].astype(F32)[:, None, :], tile.shape).astype(BF16)
    told = pltpu.make_async_copy(
        tile, out_ref.at[:, pl.ds(capacity * block, tile.shape[1])], tile_sem
    )
    told.start()
    lax.fori_loop(0, count, drain, 0)
    told.wait()


def remap_scratch(plan, entries, block, features):
    sections, halves, nears, _ = plan
    peers = sections * nears
    return [
        pltpu.SMEM((entries + 1,), jnp.int32),
        pltpu.SMEM((entries + 1,), jnp.int32),
        pltpu.SMEM((sections * halves * nears,), jnp.int32),
        pltpu.VMEM((entries, block, block), BF16),
        pltpu.VMEM((entries, block, features), BF16),
        pltpu.VMEM((peers, 128), jnp.int32),
        pltpu.VMEM((peers, 16, features), BF16),
        pltpu.SemaphoreType.DMA((entries,)),
        pltpu.SemaphoreType.DMA,
        pltpu.SemaphoreType.DMA,
    ]


def atm_kernel(
    plan,
    half_ref,
    target_ref,
    source_ref,
    block_ref,
    x_ref,
    gain_ref,
    up_ref,
    down_ref,
    flux_ref,
    weight_ref,
    next_ref,
    surface_ref,
    far_ref,
    normed,
    total,
    listed,
    slots,
    counts,
    weights,
    made,
    labels,
    tile,
    sems,
    tile_sem,
    weight_sem,
):
    step = pl.program_id(0)
    last = step == pl.num_programs(0) - 1
    parts = [slice(at, at + x_ref.shape[0] // 2) for at in (0, x_ref.shape[0] // 2)]
    fetch = pltpu.make_async_copy(weight_ref, weights, weight_sem)

    @pl.when(step == 0)
    def _():
        for rows in parts:
            values = x_ref[rows, :].astype(F32)
            normed[rows, :] = (normalised(values, -1) * gain_ref[...]).astype(BF16)
            total[rows, :] = values

    @pl.when(step == 1)
    def _():
        fetch.start()

    for rows in parts:
        raised = jnp.dot(normed[rows, :], up_ref[...], preferred_element_type=F32)
        hidden = gelu(raised.astype(BF16))
        total[rows, :] += jnp.dot(hidden, down_ref[...], preferred_element_type=F32)

    @pl.when(last)
    def _():
        for rows in parts:
            updated = total[rows, :].astype(BF16)
            next_ref[rows, :] = updated
            surface_ref[rows, :] = jnp.dot(
                updated, flux_ref[...], preferred_element_type=F32
            ).astype(BF16)
        count = pick(plan, True, half_ref, target_ref, listed, slots, counts)
        fetch.wait()
        multiply(plan, count, source_ref, block_ref, surface_ref, weights, listed, slots, made, labels, tile, far_ref, sems, tile_sem)


def atmosphere(plan, half, target, source, target_block, columns, gain, w_up, w_down, w_flux, weights):
    rows, width = columns.shape
    features = w_flux.shape[1]
    inner = w_up.shape[1]
    entries, block, _ = weights.shape
    part = inner // 4
    peers = plan[0] * plan[2]
    return pl.pallas_call(
        functools.partial(atm_kernel, plan),
        name="atmosphere",
        grid_spec=pltpu.PrefetchScalarGridSpec(
            num_scalar_prefetch=4,
            grid=(inner // part,),
            in_specs=[
                whole((rows, width)),
                whole((1, width)),
                pl.BlockSpec((width, part), lambda i, *_: (0, i)),
                pl.BlockSpec((part, width), lambda i, *_: (i, 0)),
                whole(w_flux.shape),
                pl.BlockSpec(memory_space=pltpu.HBM),
            ],
            out_specs=[
                whole((rows, width)),
                whole((rows, features)),
                pl.BlockSpec(memory_space=pltpu.HBM),
            ],
            scratch_shapes=[
                pltpu.VMEM((rows, width), BF16),
                pltpu.VMEM((rows, width), F32),
                *remap_scratch(plan, entries, block, features),
            ],
        ),
        out_shape=[
            pltpu.HBM((rows, width), BF16),
            pltpu.HBM((rows, features), BF16),
            pltpu.HBM((peers, plan[3] * block + 16, features), BF16),
        ],
        compiler_params=pltpu.CompilerParams(vmem_limit_bytes=56 << 20),
    )(
        half,
        target,
        source,
        target_block,
        in_hbm(columns),
        in_hbm(gain[None, :]),
        in_hbm(w_up),
        in_hbm(w_down),
        in_hbm(w_flux),
        in_hbm(weights),
    )


def near_kernel(
    plan,
    half_ref,
    target_ref,
    source_ref,
    block_ref,
    surface_ref,
    weight_ref,
    near_ref,
    listed,
    slots,
    counts,
    weights,
    made,
    labels,
    tile,
    sems,
    tile_sem,
    weight_sem,
):
    fetch = pltpu.make_async_copy(weight_ref, weights, weight_sem)
    fetch.start()
    count = pick(plan, False, half_ref, target_ref, listed, slots, counts)
    fetch.wait()
    multiply(plan, count, source_ref, block_ref, surface_ref, weights, listed, slots, made, labels, tile, near_ref, sems, tile_sem)


def near_remap(plan, half, target, source, target_block, surface, weights):
    entries, block, _ = weights.shape
    features = surface.shape[1]
    peers = plan[0] * plan[2]
    return pl.pallas_call(
        functools.partial(near_kernel, plan),
        name="near_remap",
        grid_spec=pltpu.PrefetchScalarGridSpec(
            num_scalar_prefetch=4,
            grid=(1,),
            in_specs=[whole(surface.shape), pl.BlockSpec(memory_space=pltpu.HBM)],
            out_specs=pl.BlockSpec(memory_space=pltpu.HBM),
            scratch_shapes=remap_scratch(plan, entries, block, features),
        ),
        out_shape=pltpu.HBM((peers, plan[3] * block + 16, features), BF16),
        compiler_params=pltpu.CompilerParams(vmem_limit_bytes=48 << 20),
    )(half, target, source, target_block, in_hbm(surface), in_hbm(weights))


def merge_kernel(capacity, arrived_ref, out_ref, arrived, tile, listed, labels, total, sems, tile_sem):
    peers = arrived.shape[0]
    block = out_ref.shape[1]

    def fetch(peer):
        return pltpu.make_async_copy(
            arrived_ref.at[peer, pl.ds(0, capacity * block)], arrived.at[peer], sems.at[peer]
        )

    told = pltpu.make_async_copy(
        arrived_ref.at[:, pl.ds(capacity * block, tile.shape[1])], tile, tile_sem
    )
    told.start()
    for peer in range(peers):
        fetch(peer).start()
    total[...] = jnp.zeros_like(total)
    told.wait()
    listed[...] = jnp.max(tile[...].astype(F32), axis=1).astype(jnp.int32)
    read = pltpu.make_async_copy(listed, labels, tile_sem)
    read.start()
    read.wait()

    def add(peer, carry):
        fetch(peer).wait()
        for rank in range(capacity):
            label = labels[peer, rank]

            @pl.when(label >= 0)
            def _():
                total[label] += arrived[peer, rank * block : (rank + 1) * block].astype(F32)

        return carry

    lax.fori_loop(0, peers, add, 0)
    out_ref[...] = total[...].astype(BF16)


def merged(capacity, arrived, blocks, block):
    peers, _, features = arrived.shape
    return pl.pallas_call(
        functools.partial(merge_kernel, capacity),
        name="merge",
        grid=(1,),
        in_specs=[pl.BlockSpec(memory_space=pltpu.HBM)],
        out_specs=whole((blocks, block, features)),
        scratch_shapes=[
            pltpu.VMEM((peers, capacity * block, features), BF16),
            pltpu.VMEM((peers, 16, features), BF16),
            pltpu.VMEM((peers, features), jnp.int32),
            pltpu.SMEM((peers, features), jnp.int32),
            pltpu.VMEM((blocks, block, features), F32),
            pltpu.SemaphoreType.DMA((peers,)),
            pltpu.SemaphoreType.DMA,
        ],
        out_shape=pltpu.HBM((blocks, block, features), BF16),
        compiler_params=pltpu.CompilerParams(vmem_limit_bytes=32 << 20),
    )(in_hbm(arrived))


def ocean_kernel(mix_ref, near_ref, far_ref, now_ref, sea_ref, force_ref, gain_ref, up_ref, down_ref, out_ref):
    forcing = (near_ref[...].astype(F32) + far_ref[...].astype(F32)).astype(BF16)
    driven = mix_ref[...] + lax.dot_general(
        force_ref[...], forcing, (((1,), (1,)), ((), ())), preferred_element_type=F32
    )
    normed = (normalised(driven, 0) * gain_ref[...]).astype(BF16)
    hidden = gelu(jnp.dot(up_ref[...], normed, preferred_element_type=F32)).astype(BF16)
    change = jnp.dot(down_ref[...], hidden, preferred_element_type=F32)
    out_ref[...] = (
        now_ref[...].astype(F32) + sea_ref[...].astype(F32) * change
    ).astype(BF16)


def ocean(mixing, near, far, now, sea, w_force, gain, w_up, w_down):
    channels, cells = now.shape
    features = near.shape[1]
    part = cells // 5
    if part % 128:
        part = cells
    tall = pl.BlockSpec((channels, part), lambda i: (0, i))
    flat = pl.BlockSpec((part, features), lambda i: (i, 0))
    return pl.pallas_call(
        ocean_kernel,
        name="ocean",
        grid=(cells // part,),
        in_specs=[
            tall,
            flat,
            flat,
            tall,
            pl.BlockSpec((1, part), lambda i: (0, i)),
            whole(w_force.shape),
            whole((channels, 1)),
            whole(w_up.shape),
            whole(w_down.shape),
        ],
        out_specs=tall,
        out_shape=jax.ShapeDtypeStruct((channels, cells), BF16),
        compiler_params=pltpu.CompilerParams(vmem_limit_bytes=48 << 20),
    )(
        in_hbm(mixing),
        in_hbm(near),
        far,
        in_hbm(now),
        sea[None, :],
        w_force,
        gain[:, None],
        w_up,
        w_down,
    )


def edge_rows(block):
    count = math.prod(lax.axis_size(axis) for axis in ALL)
    forward = [(i, i + 1) for i in range(count - 1)]
    backward = [(target, source) for source, target in forward]
    low = lax.ppermute(block[:, -OX:], ALL, forward)
    high = lax.ppermute(block[:, :OX], ALL, backward)
    return low, high


def flat_mixing(padded_flat, kernel, row_len, cell_count):
    extended = jnp.pad(padded_flat.astype(F32), ((0, 0), (row_len, row_len)))
    column_at = (jnp.arange(cell_count, dtype=jnp.int32) % row_len)[None, :]
    first_col = column_at == 0
    last_col = column_at == row_len - 1

    def window(offset):
        return lax.slice_in_dim(extended, row_len + offset, row_len + offset + cell_count, axis=1)

    summed = jnp.zeros((padded_flat.shape[0], cell_count), F32)
    for row_step in range(3):
        base = row_step * row_len
        for col_step in range(3):
            if col_step == 0:
                shifted = jnp.where(first_col, window(base + row_len - 1), window(base - 1))
            elif col_step == 2:
                shifted = jnp.where(last_col, window(base - row_len + 1), window(base + 1))
            else:
                shifted = window(base)
            summed = summed + kernel[:, 3 * row_step + col_step][:, None] * shifted
    return summed


def local(
    atm_state,
    gain_atm,
    w_up_atm,
    w_down_atm,
    w_flux,
    ent_source,
    ent_target,
    ent_block,
    remap_weights,
    ocean_state,
    land_sea,
    conv_kernel,
    w_force,
    gain_ocn,
    w_up_ocn,
    w_down_ocn,
):
    sections, halves, nears = (lax.axis_size(axis) for axis in ALL)
    half = lax.axis_index("half")
    peers = sections * nears
    entries, block_rows, _ = remap_weights.shape
    capacity = max(2, 2 * entries // (peers * halves))
    cell_count = ocean_state.shape[1]
    ocean_blocks = cell_count // block_rows

    def exchange(values):
        return lax.all_to_all(values, PEERS, split_axis=0, concat_axis=0, tiled=True)

    plan = (sections, halves, nears, capacity)
    entry = (half[None], ent_target[:, 0], ent_source, ent_block)
    atm_next, surface, far_made = atmosphere(
        plan, *entry, atm_state, gain_atm, w_up_atm, w_down_atm, w_flux, remap_weights
    )
    far_made, edge_source = lax.optimization_barrier((far_made, ocean_state))
    far_arrived = exchange(far_made)
    near_made = near_remap(plan, *entry, surface, remap_weights)
    low, high = edge_rows(edge_source)
    padded = jnp.concatenate([low, ocean_state, high], axis=1)
    mixing = flat_mixing(padded, conv_kernel, OX, cell_count)
    far_arrived, near_made, mixing = lax.optimization_barrier((far_arrived, near_made, mixing))
    near_arrived = exchange(near_made)
    far_sum = merged(capacity, far_arrived, ocean_blocks, block_rows)
    far_sum = lax.ppermute(far_sum, "half", [(0, 1), (1, 0)])
    near_sum = merged(capacity, near_arrived, ocean_blocks, block_rows)
    features = far_sum.shape[2]
    ocean_next = ocean(
        mixing,
        near_sum.reshape(cell_count, features),
        far_sum.reshape(cell_count, features),
        ocean_state,
        land_sea,
        w_force.T,
        gain_ocn,
        w_up_ocn.T,
        w_down_ocn.T,
    )
    return (atm_next, ocean_next)


def solution(mesh):
    sections, tiles = mesh.shape["sec"], mesh.shape["tile"]
    fine = Mesh(mesh.devices.reshape(sections, 2, tiles // 2), ALL)
    placed = (
        P(ALL, None),
        P(),
        P(),
        P(),
        P(),
        P(ALL),
        P(ALL, None),
        P(ALL),
        P(ALL, None, None),
        P(None, ALL),
        P(ALL),
        P(),
        P(),
        P(),
        P(),
        P(),
    )
    return jax.shard_map(
        local,
        mesh=fine,
        in_specs=placed,
        out_specs=(P(ALL, None), P(None, ALL)),
        check_vma=False,
    )
```

time: 218 us -> 238 us (1.092)
  waiting for transfers between devices: 89.5 us -> 133 us
  Pallas kernels: 65.1 us -> 53.2 us
  local copies, waits for them, and re-layouts: 18.6 us -> 6.83 us
  starting transfers between devices: 24.5 us -> 27.3 us
    ppermute x1, waiting for transfers between devices: 0.01 us -> 54.1 us  [edge_rows(): low = lax.ppermute(block[:, -OX:], ALL, forward)]
    all_to_all x2, waiting for transfers between devices: 86.2 us -> 69.5 us  [exchange(): lax.all_to_all(values, PEERS, split_axis=0, concat_axis=0, tiled=True)]
    pallas_call x5 -> x4, Pallas kernels: 52.5 us -> 40.5 us  [the longest x1 21.4 us: atmosphere(): pl.pallas_call(functools.partial(atm_kernel, plan), name='atmosphere', gr...]
    unnamed x29 -> x37, local copies, waits for them, and re-layouts: 8.64 us -> 0.28 us
    all_to_all x2, starting transfers between devices: 12.1 us -> 18.9 us  [exchange(): lax.all_to_all(values, PEERS, split_axis=0, concat_axis=0, tiled=True)]
    all_to_all x1 -> x0, starting transfers between devices: 5.24 us -> none  [local(): lax.all_to_all(sent_labels.reshape(peers, 2 * capacity), PEERS, split_axi...]
    ppermute x1, waiting for transfers between devices: 0.01 us -> 4.17 us  [edge_rows(): high = lax.ppermute(block[:, :OX], ALL, backward)]
  transfers between devices with their start and end apart: 6 -> 5, of which waited for: 3 -> 4; matrix products, arithmetic and copies ran while one was open for 12% -> 10% of each run, Pallas kernels for 18% -> 8%
where the time goes in v3:
time: 238 us
  waiting for transfers between devices  133 us (56%)
  Pallas kernels  53.2 us (22%)
  starting transfers between devices  27.3 us (11%)
  other arithmetic  16.2 us (7%)
  local copies, waits for them, and re-layouts  6.83 us (3%)
    all_to_all x2, waiting for transfers between devices, exchange(): lax.all_to_all(values, PEERS, split_axis=0, concat_axis=0, tiled=True)  69.5 us
    ppermute x1, waiting for transfers between devices, edge_rows(): low = lax.ppermute(block[:, -OX:], ALL, forward)  54.1 us
    pallas_call x1, Pallas kernels, atmosphere(): pl.pallas_call(functools.partial(atm_kernel, plan), name='atmosphere', gr...  21.4 us
    all_to_all x2, starting transfers between devices, exchange(): lax.all_to_all(values, PEERS, split_axis=0, concat_axis=0, tiled=True)  18.9 us
    add x1, other arithmetic, flat_mixing(): summed = summed + kernel[:, 3 * row_step + col_step][:, None] * shifted  13.4 us
    pallas_call x1, Pallas kernels, ocean(): pl.pallas_call(ocean_kernel, name='ocean', grid=(cells // part,), in_spec...  12.7 us
    pallas_call x2, Pallas kernels, merged(): pl.pallas_call(functools.partial(merge_kernel, capacity), name='merge', g...  11.4 us
    pallas_call x1, Pallas kernels, near_remap(): pl.pallas_call(functools.partial(near_kernel, plan), name='near_remap', g...  7.64 us
  transfers between devices with their start and end apart: 5, of which 4 were waited for; matrix products, arithmetic and copies ran while one was open for 10% of the time, Pallas kernels for 8%

profile of v3, /device:TPU:14, one launch (start us, length us, event | category | flops | bytes accessed | tf_op | source)
XLA Modules:
  0.0 237.5 jit_solution(15576661965004185005)
XLA Ops:
  0.6 21.4 %atmosphere.1 = (bf16[1024,1024]{1,0:T(8,128)(2,1)}, bf16[1024,128]{1,0:T(8,128)(2,1)}, bf16[16,1040,128]{2,1,0:T(8,128)(2,1)}) custom-call(s32[1]{0:T(128)} %bitcast.half_ref, s32[128]{0:T(128)} %bitcast.22, s32[128]{0:T(128)} %source_ref.3, s32[128]{0:T(128)} %block_ref.3, bf16[1024,1024]{1,0:T(8,128)(2,1)} %x_ref.1, f32[1,1024]{1,0:T(1,128)} %bitcast.34, ...), custom_call_target="tpu_custom_call" | custom-call | tf_op jit(solution)/shard_map/atmosphere/pallas_call | solution.py:199
  22.1 0.0 copy-start.5
  22.1 0.0 copy-start.2
  22.1 0.0 copy-start.3
  22.1 0.0 copy-start.4
  22.1 5.3 %all-to-all-start = ((bf16[16,1040,128]{2,1,0:T(8,128)(2,1)}), bf16[16,1040,128]{2,1,0:T(8,128)(2,1)}, u32[]{:S(2)}, u32[]{:S(2)}) async-start(bf16[16,1040,128]{2,1,0:T(8,128)(2,1)} %get-tuple-element.12), calls=%async_computation | async-start | bytes 8519680 | tf_op jit(solution)/shard_map/all_to_all | solution.py:460
  27.4 0.0 copy-done.5
  27.4 0.2 fusion.21
  27.6 0.0 copy-start.8
  27.6 2.9 %collective-permute-start = (bf16[200,1440]{1,0:T(8,128)(2,1)S(1)}, bf16[200,1440]{1,0:T(8,128)(2,1)S(1)}, u32[]{:S(2)}, u32[]{:S(2)}) collective-permute-start(bf16[200,1440]{1,0:T(8,128)(2,1)S(1)} %get-tuple-element.19), channel_id=1, source_target_pairs={{0,1},{1,2},{2,3},{3,4},{4,5},{5,6},{6,7},{7,8},{8,9},{9,10},{10,1... | collective-permute-start | bytes 1728008 | tf_op jit(solution)/shard_map/ppermute | solution.py:405
  30.6 2.9 %collective-permute-start.1 = (bf16[200,1440]{1,0:T(8,128)(2,1)S(1)}, bf16[200,1440]{1,0:T(8,128)(2,1)S(1)}, u32[]{:S(2)}, u32[]{:S(2)}) collective-permute-start(bf16[200,1440]{1,0:T(8,128)(2,1)S(1)} %get-tuple-element.18), channel_id=1, source_target_pairs={{1,0},{2,1},{3,2},{4,3},{5,4},{6,5},{7,6},{8,7},{9,8},{10,9},{11,1... | collective-permute-start | bytes 1728008 | tf_op jit(solution)/shard_map/ppermute | solution.py:406
  33.5 7.6 %near_remap.1 = bf16[16,1040,128]{2,1,0:T(8,128)(2,1)} custom-call(s32[1]{0:T(128)} %bitcast.half_ref, s32[128]{0:T(128)S(1)} %bitcast.23, s32[128]{0:T(128)S(1)} %copy-done.3, s32[128]{0:T(128)S(1)} %copy-done.4, bf16[1024,128]{1,0:T(8,128)(2,1)} %get-tuple-element.13.surface_ref, bf16[128,128,128]{2,1,0:T(8,128)(2,1)} %weight_ref.3), custom_call_target="tpu_custom_call" | custom-call | tf_op jit(solution)/shard_map/near_remap/pallas_call | solution.py:275
  41.2 0.6 fusion.22
  41.8 54.1 %collective-permute-done = bf16[200,1440]{1,0:T(8,128)(2,1)S(1)} collective-permute-done((bf16[200,1440]{1,0:T(8,128)(2,1)S(1)}, bf16[200,1440]{1,0:T(8,128)(2,1)S(1)}, u32[]{:S(2)}, u32[]{:S(2)}) %collective-permute-start) | collective-permute-done | bytes 576032 | tf_op jit(solution)/shard_map/ppermute | solution.py:405
  96.0 4.2 %collective-permute-done.1 = bf16[200,1440]{1,0:T(8,128)(2,1)S(1)} collective-permute-done((bf16[200,1440]{1,0:T(8,128)(2,1)S(1)}, bf16[200,1440]{1,0:T(8,128)(2,1)S(1)}, u32[]{:S(2)}, u32[]{:S(2)}) %collective-permute-start.1) | collective-permute-done | bytes 576032 | tf_op jit(solution)/shard_map/ppermute | solution.py:406
  100.1 5.5 %concatenate.3 = bf16[200,8640]{1,0:T(8,128)(2,1)} concatenate(bf16[200,1440]{1,0:T(8,128)(2,1)S(1)} %collective-permute-done, bf16[200,5760]{1,0:T(8,128)(2,1)S(1)} %copy-done.5, bf16[200,1440]{1,0:T(8,128)(2,1)S(1)} %collective-permute-done.1), dimensions={1} | concatenate | bytes 6912000 | tf_op jit(solution)/shard_map/concatenate | solution.py:471
  105.7 2.8 %convert_element_type.5 = f32[200,8640]{1,0:T(8,128)S(1)} convert(bf16[200,8640]{1,0:T(8,128)(2,1)} %concatenate.3) | non-fusion elementwise | flops 1728000 | bytes 10368000 | tf_op jit(solution)/shard_map/convert_element_type | solution.py:411
  108.6 13.4 %fusion.9.mix_ref = f32[200,5760]{1,0:T(8,128)} fusion(f32[200,8640]{1,0:T(8,128)S(1)} %convert_element_type.5, f32[200]{0:T(256)S(1)} %bitcast.32, f32[200]{0:T(256)S(1)} %bitcast.33, f32[200]{0:T(256)S(1)} %bitcast.26, f32[200]{0:T(256)S(1)} %bitcast.27, f32[200]{0:T(256)S(1)} %bitcast.28, f32[200]{0:T(256)S(1)} %bitcast.29, f32[200]{0:T(256)S(1)} %bitcast.30, ...), kind=kLoop, calls=%fused_computation.13 | loop fusion | flops 26496000 | bytes 43848704 | tf_op jit(solution)/shard_map/add | solution.py:429
  122.0 0.0 all-to-all-done.arrived_ref
  122.0 13.6 %all-to-all-start.1 = ((bf16[16,1040,128]{2,1,0:T(8,128)(2,1)}), bf16[16,1040,128]{2,1,0:T(8,128)(2,1)}, u32[]{:S(2)}, u32[]{:S(2)}) async-start(bf16[16,1040,128]{2,1,0:T(8,128)(2,1)} %near_remap.1), calls=%async_computation.1 | async-start | bytes 8519680 | tf_op jit(solution)/shard_map/all_to_all | solution.py:460
  135.7 0.0 copy-start.17
  135.7 0.0 copy-start.7
  135.7 5.7 %merge.3 = bf16[45,128,128]{2,1,0:T(8,128)(2,1)} custom-call(bf16[16,1040,128]{2,1,0:T(8,128)(2,1)} %all-to-all-done.arrived_ref), custom_call_target="tpu_custom_call" | custom-call | tf_op jit(solution)/shard_map/merge/pallas_call | solution.py:329
  141.4 0.0 copy-start
  141.4 0.0 copy-start.1
  141.4 2.5 %collective-permute-start.2 = (bf16[45,128,128]{2,1,0:T(8,128)(2,1)}, bf16[45,128,128]{2,1,0:T(8,128)(2,1)S(1)}, u32[]{:S(2)}, u32[]{:S(2)}) collective-permute-start(bf16[45,128,128]{2,1,0:T(8,128)(2,1)} %merge.3), channel_id=1, source_target_pairs={{0,8},{8,0},{1,9},{9,1},{2,10},{10,2},{3,11},{11,3},{4,12},{12,4},... | collective-permute-start | bytes 4423688 | tf_op jit(solution)/shard_map/ppermute | solution.py:476
  143.9 0.2 copy.19
  144.1 0.1 copy.20.gain_ref
  144.3 69.5 %all-to-all-done.1.arrived_ref = bf16[16,1040,128]{2,1,0:T(8,128)(2,1)} async-done(((bf16[16,1040,128]{2,1,0:T(8,128)(2,1)}), bf16[16,1040,128]{2,1,0:T(8,128)(2,1)}, u32[]{:S(2)}, u32[]{:S(2)}) %all-to-all-start.1) | async-done | bytes 4259872 | tf_op jit(solution)/shard_map/all_to_all | solution.py:460
  213.8 5.8 %merge.2 = bf16[45,128,128]{2,1,0:T(8,128)(2,1)} custom-call(bf16[16,1040,128]{2,1,0:T(8,128)(2,1)} %all-to-all-done.1.arrived_ref), custom_call_target="tpu_custom_call" | custom-call | tf_op jit(solution)/shard_map/merge/pallas_call | solution.py:329
  219.6 5.3 %collective-permute-done.2 = bf16[45,128,128]{2,1,0:T(8,128)(2,1)S(1)} collective-permute-done((bf16[45,128,128]{2,1,0:T(8,128)(2,1)}, bf16[45,128,128]{2,1,0:T(8,128)(2,1)S(1)}, u32[]{:S(2)}, u32[]{:S(2)}) %collective-permute-start.2) | collective-permute-done | bytes 1474592 | tf_op jit(solution)/shard_map/ppermute | solution.py:476
  224.8 12.7 %ocean.1 = bf16[200,5760]{1,0:T(8,128)(2,1)} custom-call(f32[200,5760]{1,0:T(8,128)} %fusion.9.mix_ref, bf16[5760,128]{1,0:T(8,128)(2,1)} %bitcast.24, bf16[5760,128]{1,0:T(8,128)(2,1)S(1)} %bitcast.19, bf16[200,5760]{1,0:T(8,128)(2,1)} %now_ref.1, s32[1,5760]{1,0:T(1,128)S(1)} %broadcast_in_dim.50.sea_ref, bf16[200,128]{1,0:T(8,128)(2,1)S(1)} %bitcast.21, ...), custom_call_target="tpu_custom_call" | custom-call | tf_op jit(solution)/shard_map/ocean/pallas_call | solution.py:370
  (28 shorter events, 0.1 us)
Async XLA Ops:
  22.1 5.3 %copy-start.5 = (bf16[200,5760]{1,0:T(8,128)(2,1)S(1)}, bf16[200,5760]{1,0:T(8,128)(2,1)}, u32[]{:S(2)}) copy-start(bf16[200,5760]{1,0:T(8,128)(2,1)} %now_ref.1) | copy-start | bytes 6912004
  22.1 11.4 %copy-start.2 = (s32[128,1]{0,1:T(1,128)S(1)}, s32[128,1]{0,1:T(1,128)}, u32[]{:S(2)}) copy-start(s32[128,1]{0,1:T(1,128)} %param.22) | copy-start | bytes 1540
  22.1 11.4 %copy-start.3 = (s32[128]{0:T(128)S(1)}, s32[128]{0:T(128)}, u32[]{:S(2)}) copy-start(s32[128]{0:T(128)} %source_ref.3) | copy-start | bytes 1540
  22.1 11.4 %copy-start.4 = (s32[128]{0:T(128)S(1)}, s32[128]{0:T(128)}, u32[]{:S(2)}) copy-start(s32[128]{0:T(128)} %block_ref.3) | copy-start | bytes 1540
  22.1 99.9 %all-to-all-start = ((bf16[16,1040,128]{2,1,0:T(8,128)(2,1)}), bf16[16,1040,128]{2,1,0:T(8,128)(2,1)}, u32[]{:S(2)}, u32[]{:S(2)}) async-start(bf16[16,1040,128]{2,1,0:T(8,128)(2,1)} %get-tuple-element.12), calls=%async_computation | async-start | bytes 8519680 | tf_op jit(solution)/shard_map/all_to_all | solution.py:460
  27.6 13.6 %copy-start.8 = (f32[200,9]{0,1:T(8,128)S(1)}, f32[200,9]{0,1:T(8,128)}, u32[]{:S(2)}) copy-start(f32[200,9]{0,1:T(8,128)} %param.27) | copy-start | bytes 21604
  27.6 68.3 %collective-permute-start = (bf16[200,1440]{1,0:T(8,128)(2,1)S(1)}, bf16[200,1440]{1,0:T(8,128)(2,1)S(1)}, u32[]{:S(2)}, u32[]{:S(2)}) collective-permute-start(bf16[200,1440]{1,0:T(8,128)(2,1)S(1)} %get-tuple-element.19), channel_id=1, source_target_pairs={{0,1},{1,2},{2,3},{3,4},{4,5},{5,6},{6,7},{7,8},{8,9},{9,10},{10,1... | collective-permute-start | bytes 1728008 | tf_op jit(solution)/shard_map/ppermute | solution.py:405
  30.6 69.6 %collective-permute-start.1 = (bf16[200,1440]{1,0:T(8,128)(2,1)S(1)}, bf16[200,1440]{1,0:T(8,128)(2,1)S(1)}, u32[]{:S(2)}, u32[]{:S(2)}) collective-permute-start(bf16[200,1440]{1,0:T(8,128)(2,1)S(1)} %get-tuple-element.18), channel_id=1, source_target_pairs={{1,0},{2,1},{3,2},{4,3},{5,4},{6,5},{7,6},{8,7},{9,8},{10,9},{11,1... | collective-permute-start | bytes 1728008 | tf_op jit(solution)/shard_map/ppermute | solution.py:406
  105.7 2.8 %copy-start.9 = (f32[200,1]{0,1:T(1,128)S(1)}, f32[200,1]{0,1:T(1,128)}, u32[]{:S(2)}) copy-start(f32[200,1]{0,1:T(1,128)} %get-tuple-element.21) | copy-start | bytes 2404
  105.7 2.8 %copy-start.10 = (f32[200,1]{0,1:T(1,128)S(1)}, f32[200,1]{0,1:T(1,128)}, u32[]{:S(2)}) copy-start(f32[200,1]{0,1:T(1,128)} %get-tuple-element.22) | copy-start | bytes 2404
  105.7 2.9 %copy-start.11 = (f32[200,1]{0,1:T(1,128)S(1)}, f32[200,1]{0,1:T(1,128)}, u32[]{:S(2)}) copy-start(f32[200,1]{0,1:T(1,128)} %get-tuple-element.23) | copy-start | bytes 2404
  105.7 2.9 %copy-start.12 = (f32[200,1]{0,1:T(1,128)S(1)}, f32[200,1]{0,1:T(1,128)}, u32[]{:S(2)}) copy-start(f32[200,1]{0,1:T(1,128)} %get-tuple-element.24) | copy-start | bytes 2404
  105.7 2.9 %copy-start.13 = (f32[200,1]{0,1:T(1,128)S(1)}, f32[200,1]{0,1:T(1,128)}, u32[]{:S(2)}) copy-start(f32[200,1]{0,1:T(1,128)} %get-tuple-element.25) | copy-start | bytes 2404
  105.7 2.9 %copy-start.14 = (f32[200,1]{0,1:T(1,128)S(1)}, f32[200,1]{0,1:T(1,128)}, u32[]{:S(2)}) copy-start(f32[200,1]{0,1:T(1,128)} %get-tuple-element.26) | copy-start | bytes 2404
  105.7 2.9 %copy-start.15 = (f32[200,1]{0,1:T(1,128)S(1)}, f32[200,1]{0,1:T(1,128)}, u32[]{:S(2)}) copy-start(f32[200,1]{0,1:T(1,128)} %get-tuple-element.27) | copy-start | bytes 2404
  105.7 2.9 %copy-start.16 = (f32[200,1]{0,1:T(1,128)S(1)}, f32[200,1]{0,1:T(1,128)}, u32[]{:S(2)}) copy-start(f32[200,1]{0,1:T(1,128)} %get-tuple-element.28) | copy-start | bytes 2404
  122.0 91.8 %all-to-all-start.1 = ((bf16[16,1040,128]{2,1,0:T(8,128)(2,1)}), bf16[16,1040,128]{2,1,0:T(8,128)(2,1)}, u32[]{:S(2)}, u32[]{:S(2)}) async-start(bf16[16,1040,128]{2,1,0:T(8,128)(2,1)} %near_remap.1), calls=%async_computation.1 | async-start | bytes 8519680 | tf_op jit(solution)/shard_map/all_to_all | solution.py:460
  135.7 8.2 %copy-start.6 = (bf16[200,800]{1,0:T(8,128)(2,1)S(1)}, bf16[200,800]{1,0:T(8,128)(2,1)}, u32[]{:S(2)}) copy-start(bf16[200,800]{1,0:T(8,128)(2,1)} %param.30) | copy-start | bytes 960004
  135.7 8.4 %copy-start.17 = (f32[200]{0:T(256)S(1)}, f32[200]{0:T(256)}, u32[]{:S(2)}) copy-start(f32[200]{0:T(256)} %param.29) | copy-start | bytes 2404
  135.7 8.6 %copy-start.7 = (s32[5760]{0:T(1024)S(1)}, s32[5760]{0:T(1024)}, u32[]{:S(2)}) copy-start(s32[5760]{0:T(1024)} %param.26) | copy-start | bytes 69124
  141.4 83.5 %copy-start = (bf16[800,200]{0,1:T(8,128)(2,1)S(1)}, bf16[800,200]{0,1:T(8,128)(2,1)}, u32[]{:S(2)}) copy-start(bf16[800,200]{0,1:T(8,128)(2,1)} %param.31) | copy-start | bytes 960004
  141.4 83.4 %copy-start.1 = (bf16[128,200]{0,1:T(8,128)(2,1)S(1)}, bf16[128,200]{0,1:T(8,128)(2,1)}, u32[]{:S(2)}) copy-start(bf16[128,200]{0,1:T(8,128)(2,1)} %param.28) | copy-start | bytes 153604
  141.4 83.4 %collective-permute-start.2 = (bf16[45,128,128]{2,1,0:T(8,128)(2,1)}, bf16[45,128,128]{2,1,0:T(8,128)(2,1)S(1)}, u32[]{:S(2)}, u32[]{:S(2)}) collective-permute-start(bf16[45,128,128]{2,1,0:T(8,128)(2,1)} %merge.3), channel_id=1, source_target_pairs={{0,8},{8,0},{1,9},{9,1},{2,10},{10,2},{3,11},{11,3},{4,12},{12,4},... | collective-permute-start | bytes 4423688 | tf_op jit(solution)/shard_map/ppermute | solution.py:476

commit v4 on v3

--- a/solution.py
+++ b/solution.py
@@ -352,7 +352,7 @@
         force_ref[...], forcing, (((1,), (1,)), ((), ())), preferred_element_type=F32
     )
     normed = (normalised(driven, 0) * gain_ref[...]).astype(BF16)
-    hidden = gelu(jnp.dot(up_ref[...], normed, preferred_element_type=F32)).astype(BF16)
+    hidden = gelu(jnp.dot(up_ref[...], normed, preferred_element_type=F32).astype(BF16))
     change = jnp.dot(down_ref[...], hidden, preferred_element_type=F32)
     out_ref[...] = (
         now_ref[...].astype(F32) + sea_ref[...].astype(F32) * change
@@ -464,10 +464,10 @@
     atm_next, surface, far_made = atmosphere(
         plan, *entry, atm_state, gain_atm, w_up_atm, w_down_atm, w_flux, remap_weights
     )
-    far_made, edge_source = lax.optimization_barrier((far_made, ocean_state))
+    low, high = edge_rows(ocean_state)
+    far_made, low, high = lax.optimization_barrier((far_made, low, high))
     far_arrived = exchange(far_made)
     near_made = near_remap(plan, *entry, surface, remap_weights)
-    low, high = edge_rows(edge_source)
     padded = jnp.concatenate([low, ocean_state, high], axis=1)
     mixing = flat_mixing(padded, conv_kernel, OX, cell_count)
     far_arrived, near_made, mixing = lax.optimization_barrier((far_arrived, near_made, mixing))

time: 238 us -> 201 us (0.84)
  waiting for transfers between devices: 133 us -> 102 us
  starting transfers between devices: 27.3 us -> 22.1 us
    ppermute x1, waiting for transfers between devices: 54.1 us -> 0.01 us  [edge_rows(): low = lax.ppermute(block[:, -OX:], ALL, forward)]
    all_to_all x2, waiting for transfers between devices: 69.5 us -> 93.5 us  [exchange(): lax.all_to_all(values, PEERS, split_axis=0, concat_axis=0, tiled=True)]
    all_to_all x2, starting transfers between devices: 18.9 us -> 13.7 us  [exchange(): lax.all_to_all(values, PEERS, split_axis=0, concat_axis=0, tiled=True)]
  transfers between devices with their start and end apart: 5 -> 5, of which waited for: 4 -> 4; matrix products, arithmetic and copies ran while one was open for 10% -> 11% of each run, Pallas kernels for 8% -> 20%
where the time goes in v4:
time: 201 us
  waiting for transfers between devices  102 us (51%)
  Pallas kernels  51.5 us (26%)
  starting transfers between devices  22.1 us (11%)
  other arithmetic  16.2 us (8%)
  local copies, waits for them, and re-layouts  8.1 us (4%)
    all_to_all x2, waiting for transfers between devices, exchange(): lax.all_to_all(values, PEERS, split_axis=0, concat_axis=0, tiled=True)  93.5 us
    pallas_call x1, Pallas kernels, atmosphere(): pl.pallas_call(functools.partial(atm_kernel, plan), name='atmosphere', gr...  21 us
    all_to_all x2, starting transfers between devices, exchange(): lax.all_to_all(values, PEERS, split_axis=0, concat_axis=0, tiled=True)  13.7 us
    add x1, other arithmetic, flat_mixing(): summed = summed + kernel[:, 3 * row_step + col_step][:, None] * shifted  13.4 us
    pallas_call x2, Pallas kernels, merged(): pl.pallas_call(functools.partial(merge_kernel, capacity), name='merge', g...  11.4 us
    pallas_call x1, Pallas kernels, ocean(): pl.pallas_call(ocean_kernel, name='ocean', grid=(cells // part,), in_spec...  11 us
    pallas_call x1, Pallas kernels, near_remap(): pl.pallas_call(functools.partial(near_kernel, plan), name='near_remap', g...  8.16 us
    ppermute x1, waiting for transfers between devices, local(): far_sum = lax.ppermute(far_sum, 'half', [(0, 1), (1, 0)])  5.71 us
  transfers between devices with their start and end apart: 5, of which 4 were waited for; matrix products, arithmetic and copies ran while one was open for 11% of the time, Pallas kernels for 20%

profile of v4, /device:TPU:14, one launch (start us, length us, event | category | flops | bytes accessed | tf_op | source)
XLA Modules:
  0.0 200.7 jit_solution(2293946750595585665)
XLA Ops:
  0.6 1.5 fusion.21
  2.1 3.4 %collective-permute-start = (bf16[200,1440]{1,0:T(8,128)(2,1)S(1)}, bf16[200,1440]{1,0:T(8,128)(2,1)S(1)}, u32[]{:S(2)}, u32[]{:S(2)}) collective-permute-start(bf16[200,1440]{1,0:T(8,128)(2,1)S(1)} %get-tuple-element.21), channel_id=1, source_target_pairs={{0,1},{1,2},{2,3},{3,4},{4,5},{5,6},{6,7},{7,8},{8,9},{9,10},{10,1... | collective-permute-start | bytes 1728008 | tf_op jit(solution)/shard_map/ppermute | solution.py:405
  5.5 2.4 %collective-permute-start.1 = (bf16[200,1440]{1,0:T(8,128)(2,1)S(1)}, bf16[200,1440]{1,0:T(8,128)(2,1)S(1)}, u32[]{:S(2)}, u32[]{:S(2)}) collective-permute-start(bf16[200,1440]{1,0:T(8,128)(2,1)S(1)} %get-tuple-element.20), channel_id=1, source_target_pairs={{1,0},{2,1},{3,2},{4,3},{5,4},{6,5},{7,6},{8,7},{9,8},{10,9},{11,1... | collective-permute-start | bytes 1728008 | tf_op jit(solution)/shard_map/ppermute | solution.py:406
  8.0 21.0 %atmosphere.1 = (bf16[1024,1024]{1,0:T(8,128)(2,1)}, bf16[1024,128]{1,0:T(8,128)(2,1)}, bf16[16,1040,128]{2,1,0:T(8,128)(2,1)}) custom-call(s32[1]{0:T(128)} %bitcast.half_ref, s32[128]{0:T(128)} %bitcast.22, s32[128]{0:T(128)} %source_ref.3, s32[128]{0:T(128)} %block_ref.3, bf16[1024,1024]{1,0:T(8,128)(2,1)} %x_ref.1, f32[1,1024]{1,0:T(1,128)} %bitcast.34, ...), custom_call_target="tpu_custom_call" | custom-call | tf_op jit(solution)/shard_map/atmosphere/pallas_call | solution.py:199
  29.0 0.0 copy-start.2
  29.0 0.0 copy-start.3
  29.0 0.0 copy-start.4
  29.0 0.0 collective-permute-done
  29.0 2.7 %collective-permute-done.1 = bf16[200,1440]{1,0:T(8,128)(2,1)S(1)} collective-permute-done((bf16[200,1440]{1,0:T(8,128)(2,1)S(1)}, bf16[200,1440]{1,0:T(8,128)(2,1)S(1)}, u32[]{:S(2)}, u32[]{:S(2)}) %collective-permute-start.1) | collective-permute-done | bytes 576032 | tf_op jit(solution)/shard_map/ppermute | solution.py:406
  31.7 6.8 %all-to-all-start = ((bf16[16,1040,128]{2,1,0:T(8,128)(2,1)}), bf16[16,1040,128]{2,1,0:T(8,128)(2,1)}, u32[]{:S(2)}, u32[]{:S(2)}) async-start(bf16[16,1040,128]{2,1,0:T(8,128)(2,1)} %get-tuple-element.13), calls=%async_computation | async-start | bytes 8519680 | tf_op jit(solution)/shard_map/all_to_all | solution.py:460
  38.4 0.0 copy-start.5
  38.5 0.0 copy-done.2
  38.5 0.0 copy-done.3
  38.5 8.2 %near_remap.1 = bf16[16,1040,128]{2,1,0:T(8,128)(2,1)} custom-call(s32[1]{0:T(128)} %bitcast.half_ref, s32[128]{0:T(128)S(1)} %bitcast.23, s32[128]{0:T(128)S(1)} %copy-done.3, s32[128]{0:T(128)S(1)} %copy-done.4, bf16[1024,128]{1,0:T(8,128)(2,1)} %get-tuple-element.14.surface_ref, bf16[128,128,128]{2,1,0:T(8,128)(2,1)} %weight_ref.3), custom_call_target="tpu_custom_call" | custom-call | tf_op jit(solution)/shard_map/near_remap/pallas_call | solution.py:275
  46.7 0.6 fusion.22
  47.3 5.6 %concatenate.3 = bf16[200,8640]{1,0:T(8,128)(2,1)} concatenate(bf16[200,1440]{1,0:T(8,128)(2,1)S(1)} %collective-permute-done, bf16[200,5760]{1,0:T(8,128)(2,1)S(1)} %copy-done.5, bf16[200,1440]{1,0:T(8,128)(2,1)S(1)} %collective-permute-done.1), dimensions={1} | concatenate | bytes 6912000 | tf_op jit(solution)/shard_map/concatenate | solution.py:471
  52.9 2.8 %convert_element_type.5 = f32[200,8640]{1,0:T(8,128)S(1)} convert(bf16[200,8640]{1,0:T(8,128)(2,1)} %concatenate.3) | non-fusion elementwise | flops 1728000 | bytes 10368000 | tf_op jit(solution)/shard_map/convert_element_type | solution.py:411
  55.8 13.4 %fusion.9.mix_ref = f32[200,5760]{1,0:T(8,128)} fusion(f32[200,8640]{1,0:T(8,128)S(1)} %convert_element_type.5, f32[200]{0:T(256)S(1)} %bitcast.32, f32[200]{0:T(256)S(1)} %bitcast.33, f32[200]{0:T(256)S(1)} %bitcast.26, f32[200]{0:T(256)S(1)} %bitcast.27, f32[200]{0:T(256)S(1)} %bitcast.28, f32[200]{0:T(256)S(1)} %bitcast.29, f32[200]{0:T(256)S(1)} %bitcast.30, ...), kind=kLoop, calls=%fused_computation.13 | loop fusion | flops 26496000 | bytes 43848704 | tf_op jit(solution)/shard_map/add | solution.py:429
  69.2 24.1 %all-to-all-done.arrived_ref = bf16[16,1040,128]{2,1,0:T(8,128)(2,1)} async-done(((bf16[16,1040,128]{2,1,0:T(8,128)(2,1)}), bf16[16,1040,128]{2,1,0:T(8,128)(2,1)}, u32[]{:S(2)}, u32[]{:S(2)}) %all-to-all-start) | async-done | bytes 4259872 | tf_op jit(solution)/shard_map/all_to_all | solution.py:460
  93.3 6.9 %all-to-all-start.1 = ((bf16[16,1040,128]{2,1,0:T(8,128)(2,1)}), bf16[16,1040,128]{2,1,0:T(8,128)(2,1)}, u32[]{:S(2)}, u32[]{:S(2)}) async-start(bf16[16,1040,128]{2,1,0:T(8,128)(2,1)} %near_remap.1), calls=%async_computation.1 | async-start | bytes 8519680 | tf_op jit(solution)/shard_map/all_to_all | solution.py:460
  100.3 0.0 copy-start.17
  100.3 0.0 copy-start.7
  100.3 5.8 %merge.3 = bf16[45,128,128]{2,1,0:T(8,128)(2,1)} custom-call(bf16[16,1040,128]{2,1,0:T(8,128)(2,1)} %all-to-all-done.arrived_ref), custom_call_target="tpu_custom_call" | custom-call | tf_op jit(solution)/shard_map/merge/pallas_call | solution.py:329
  106.1 0.0 copy-start
  106.1 0.0 copy-start.1
  106.1 2.5 %collective-permute-start.2 = (bf16[45,128,128]{2,1,0:T(8,128)(2,1)}, bf16[45,128,128]{2,1,0:T(8,128)(2,1)S(1)}, u32[]{:S(2)}, u32[]{:S(2)}) collective-permute-start(bf16[45,128,128]{2,1,0:T(8,128)(2,1)} %merge.3), channel_id=1, source_target_pairs={{0,8},{8,0},{1,9},{9,1},{2,10},{10,2},{3,11},{11,3},{4,12},{12,4},... | collective-permute-start | bytes 4423688 | tf_op jit(solution)/shard_map/ppermute | solution.py:476
  108.7 0.2 copy.19
  108.9 0.1 copy.20.gain_ref
  109.0 69.4 %all-to-all-done.1.arrived_ref = bf16[16,1040,128]{2,1,0:T(8,128)(2,1)} async-done(((bf16[16,1040,128]{2,1,0:T(8,128)(2,1)}), bf16[16,1040,128]{2,1,0:T(8,128)(2,1)}, u32[]{:S(2)}, u32[]{:S(2)}) %all-to-all-start.1) | async-done | bytes 4259872 | tf_op jit(solution)/shard_map/all_to_all | solution.py:460
  178.4 5.6 %merge.2 = bf16[45,128,128]{2,1,0:T(8,128)(2,1)} custom-call(bf16[16,1040,128]{2,1,0:T(8,128)(2,1)} %all-to-all-done.1.arrived_ref), custom_call_target="tpu_custom_call" | custom-call | tf_op jit(solution)/shard_map/merge/pallas_call | solution.py:329
  184.0 5.7 %collective-permute-done.2 = bf16[45,128,128]{2,1,0:T(8,128)(2,1)S(1)} collective-permute-done((bf16[45,128,128]{2,1,0:T(8,128)(2,1)}, bf16[45,128,128]{2,1,0:T(8,128)(2,1)S(1)}, u32[]{:S(2)}, u32[]{:S(2)}) %collective-permute-start.2) | collective-permute-done | bytes 1474592 | tf_op jit(solution)/shard_map/ppermute | solution.py:476
  189.7 11.0 %ocean.1 = bf16[200,5760]{1,0:T(8,128)(2,1)} custom-call(f32[200,5760]{1,0:T(8,128)} %fusion.9.mix_ref, bf16[5760,128]{1,0:T(8,128)(2,1)} %bitcast.24, bf16[5760,128]{1,0:T(8,128)(2,1)S(1)} %bitcast.19, bf16[200,5760]{1,0:T(8,128)(2,1)} %now_ref.1, s32[1,5760]{1,0:T(1,128)S(1)} %broadcast_in_dim.50.sea_ref, bf16[200,128]{1,0:T(8,128)(2,1)S(1)} %bitcast.21, ...), custom_call_target="tpu_custom_call" | custom-call | tf_op jit(solution)/shard_map/ocean/pallas_call | solution.py:370
  (28 shorter events, 0.1 us)
Async XLA Ops:
  2.1 26.9 %collective-permute-start = (bf16[200,1440]{1,0:T(8,128)(2,1)S(1)}, bf16[200,1440]{1,0:T(8,128)(2,1)S(1)}, u32[]{:S(2)}, u32[]{:S(2)}) collective-permute-start(bf16[200,1440]{1,0:T(8,128)(2,1)S(1)} %get-tuple-element.21), channel_id=1, source_target_pairs={{0,1},{1,2},{2,3},{3,4},{4,5},{5,6},{6,7},{7,8},{8,9},{9,10},{10,1... | collective-permute-start | bytes 1728008 | tf_op jit(solution)/shard_map/ppermute | solution.py:405
  5.5 26.1 %collective-permute-start.1 = (bf16[200,1440]{1,0:T(8,128)(2,1)S(1)}, bf16[200,1440]{1,0:T(8,128)(2,1)S(1)}, u32[]{:S(2)}, u32[]{:S(2)}) collective-permute-start(bf16[200,1440]{1,0:T(8,128)(2,1)S(1)} %get-tuple-element.20), channel_id=1, source_target_pairs={{1,0},{2,1},{3,2},{4,3},{5,4},{6,5},{7,6},{8,7},{9,8},{10,9},{11,1... | collective-permute-start | bytes 1728008 | tf_op jit(solution)/shard_map/ppermute | solution.py:406
  29.0 9.5 %copy-start.2 = (s32[128,1]{0,1:T(1,128)S(1)}, s32[128,1]{0,1:T(1,128)}, u32[]{:S(2)}) copy-start(s32[128,1]{0,1:T(1,128)} %param.22) | copy-start | bytes 1540
  29.0 9.5 %copy-start.3 = (s32[128]{0:T(128)S(1)}, s32[128]{0:T(128)}, u32[]{:S(2)}) copy-start(s32[128]{0:T(128)} %source_ref.3) | copy-start | bytes 1540
  29.0 9.5 %copy-start.4 = (s32[128]{0:T(128)S(1)}, s32[128]{0:T(128)}, u32[]{:S(2)}) copy-start(s32[128]{0:T(128)} %block_ref.3) | copy-start | bytes 1540
  31.7 61.7 %all-to-all-start = ((bf16[16,1040,128]{2,1,0:T(8,128)(2,1)}), bf16[16,1040,128]{2,1,0:T(8,128)(2,1)}, u32[]{:S(2)}, u32[]{:S(2)}) async-start(bf16[16,1040,128]{2,1,0:T(8,128)(2,1)} %get-tuple-element.13), calls=%async_computation | async-start | bytes 8519680 | tf_op jit(solution)/shard_map/all_to_all | solution.py:460
  38.4 8.2 %copy-start.8 = (f32[200,9]{0,1:T(8,128)S(1)}, f32[200,9]{0,1:T(8,128)}, u32[]{:S(2)}) copy-start(f32[200,9]{0,1:T(8,128)} %param.27) | copy-start | bytes 21604
  38.4 8.9 %copy-start.5 = (bf16[200,5760]{1,0:T(8,128)(2,1)S(1)}, bf16[200,5760]{1,0:T(8,128)(2,1)}, u32[]{:S(2)}) copy-start(bf16[200,5760]{1,0:T(8,128)(2,1)} %now_ref.1) | copy-start | bytes 6912004
  52.9 2.8 %copy-start.9 = (f32[200,1]{0,1:T(1,128)S(1)}, f32[200,1]{0,1:T(1,128)}, u32[]{:S(2)}) copy-start(f32[200,1]{0,1:T(1,128)} %get-tuple-element.23) | copy-start | bytes 2404
  52.9 2.8 %copy-start.10 = (f32[200,1]{0,1:T(1,128)S(1)}, f32[200,1]{0,1:T(1,128)}, u32[]{:S(2)}) copy-start(f32[200,1]{0,1:T(1,128)} %get-tuple-element.24) | copy-start | bytes 2404
  52.9 2.9 %copy-start.11 = (f32[200,1]{0,1:T(1,128)S(1)}, f32[200,1]{0,1:T(1,128)}, u32[]{:S(2)}) copy-start(f32[200,1]{0,1:T(1,128)} %get-tuple-element.25) | copy-start | bytes 2404
  52.9 2.9 %copy-start.12 = (f32[200,1]{0,1:T(1,128)S(1)}, f32[200,1]{0,1:T(1,128)}, u32[]{:S(2)}) copy-start(f32[200,1]{0,1:T(1,128)} %get-tuple-element.26) | copy-start | bytes 2404
  52.9 2.9 %copy-start.13 = (f32[200,1]{0,1:T(1,128)S(1)}, f32[200,1]{0,1:T(1,128)}, u32[]{:S(2)}) copy-start(f32[200,1]{0,1:T(1,128)} %get-tuple-element.27) | copy-start | bytes 2404
  52.9 2.9 %copy-start.14 = (f32[200,1]{0,1:T(1,128)S(1)}, f32[200,1]{0,1:T(1,128)}, u32[]{:S(2)}) copy-start(f32[200,1]{0,1:T(1,128)} %get-tuple-element.28) | copy-start | bytes 2404
  52.9 2.9 %copy-start.15 = (f32[200,1]{0,1:T(1,128)S(1)}, f32[200,1]{0,1:T(1,128)}, u32[]{:S(2)}) copy-start(f32[200,1]{0,1:T(1,128)} %get-tuple-element.29) | copy-start | bytes 2404
  52.9 2.9 %copy-start.16 = (f32[200,1]{0,1:T(1,128)S(1)}, f32[200,1]{0,1:T(1,128)}, u32[]{:S(2)}) copy-start(f32[200,1]{0,1:T(1,128)} %get-tuple-element.30) | copy-start | bytes 2404
  93.3 85.0 %all-to-all-start.1 = ((bf16[16,1040,128]{2,1,0:T(8,128)(2,1)}), bf16[16,1040,128]{2,1,0:T(8,128)(2,1)}, u32[]{:S(2)}, u32[]{:S(2)}) async-start(bf16[16,1040,128]{2,1,0:T(8,128)(2,1)} %near_remap.1), calls=%async_computation.1 | async-start | bytes 8519680 | tf_op jit(solution)/shard_map/all_to_all | solution.py:460
  100.3 8.4 %copy-start.6 = (bf16[200,800]{1,0:T(8,128)(2,1)S(1)}, bf16[200,800]{1,0:T(8,128)(2,1)}, u32[]{:S(2)}) copy-start(bf16[200,800]{1,0:T(8,128)(2,1)} %param.30) | copy-start | bytes 960004
  100.3 8.6 %copy-start.17 = (f32[200]{0:T(256)S(1)}, f32[200]{0:T(256)}, u32[]{:S(2)}) copy-start(f32[200]{0:T(256)} %param.29) | copy-start | bytes 2404
  100.3 8.7 %copy-start.7 = (s32[5760]{0:T(1024)S(1)}, s32[5760]{0:T(1024)}, u32[]{:S(2)}) copy-start(s32[5760]{0:T(1024)} %param.26) | copy-start | bytes 69124
  106.1 83.6 %copy-start = (bf16[800,200]{0,1:T(8,128)(2,1)S(1)}, bf16[800,200]{0,1:T(8,128)(2,1)}, u32[]{:S(2)}) copy-start(bf16[800,200]{0,1:T(8,128)(2,1)} %param.31) | copy-start | bytes 960004
  106.1 83.6 %copy-start.1 = (bf16[128,200]{0,1:T(8,128)(2,1)S(1)}, bf16[128,200]{0,1:T(8,128)(2,1)}, u32[]{:S(2)}) copy-start(bf16[128,200]{0,1:T(8,128)(2,1)} %param.28) | copy-start | bytes 153604
  106.1 83.6 %collective-permute-start.2 = (bf16[45,128,128]{2,1,0:T(8,128)(2,1)}, bf16[45,128,128]{2,1,0:T(8,128)(2,1)S(1)}, u32[]{:S(2)}, u32[]{:S(2)}) collective-permute-start(bf16[45,128,128]{2,1,0:T(8,128)(2,1)} %merge.3), channel_id=1, source_target_pairs={{0,8},{8,0},{1,9},{9,1},{2,10},{10,2},{3,11},{11,3},{4,12},{12,4},... | collective-permute-start | bytes 4423688 | tf_op jit(solution)/shard_map/ppermute | solution.py:476

commit v5 on v4

--- a/solution.py
+++ b/solution.py
@@ -287,9 +287,9 @@
     )(half, target, source, target_block, in_hbm(surface), in_hbm(weights))
 
 
-def merge_kernel(capacity, arrived_ref, out_ref, arrived, tile, listed, labels, total, sems, tile_sem):
+def gather_slots(capacity, arrived_ref, arrived, tile, listed, labels, total, sems, tile_sem):
     peers = arrived.shape[0]
-    block = out_ref.shape[1]
+    block = total.shape[1]
 
     def fetch(peer):
         return pltpu.make_async_copy(
@@ -321,6 +321,22 @@
         return carry
 
     lax.fori_loop(0, peers, add, 0)
+
+
+def gather_scratch(peers, capacity, blocks, block, features):
+    return [
+        pltpu.VMEM((peers, capacity * block, features), BF16),
+        pltpu.VMEM((peers, 16, features), BF16),
+        pltpu.VMEM((peers, features), jnp.int32),
+        pltpu.SMEM((peers, features), jnp.int32),
+        pltpu.VMEM((blocks, block, features), F32),
+        pltpu.SemaphoreType.DMA((peers,)),
+        pltpu.SemaphoreType.DMA,
+    ]
+
+
+def merge_kernel(capacity, arrived_ref, out_ref, arrived, tile, listed, labels, total, sems, tile_sem):
+    gather_slots(capacity, arrived_ref, arrived, tile, listed, labels, total, sems, tile_sem)
     out_ref[...] = total[...].astype(BF16)
 
 
@@ -332,49 +348,65 @@
         grid=(1,),
         in_specs=[pl.BlockSpec(memory_space=pltpu.HBM)],
         out_specs=whole((blocks, block, features)),
-        scratch_shapes=[
-            pltpu.VMEM((peers, capacity * block, features), BF16),
-            pltpu.VMEM((peers, 16, features), BF16),
-            pltpu.VMEM((peers, features), jnp.int32),
-            pltpu.SMEM((peers, features), jnp.int32),
-            pltpu.VMEM((blocks, block, features), F32),
-            pltpu.SemaphoreType.DMA((peers,)),
-            pltpu.SemaphoreType.DMA,
-        ],
+        scratch_shapes=gather_scratch(peers, capacity, blocks, block, features),
         out_shape=pltpu.HBM((blocks, block, features), BF16),
         compiler_params=pltpu.CompilerParams(vmem_limit_bytes=32 << 20),
     )(in_hbm(arrived))
 
 
-def ocean_kernel(mix_ref, near_ref, far_ref, now_ref, sea_ref, force_ref, gain_ref, up_ref, down_ref, out_ref):
-    forcing = (near_ref[...].astype(F32) + far_ref[...].astype(F32)).astype(BF16)
-    driven = mix_ref[...] + lax.dot_general(
+def ocean_kernel(
+    capacity,
+    mix_ref,
+    near_ref,
+    far_ref,
+    now_ref,
+    sea_ref,
+    force_ref,
+    gain_ref,
+    up_ref,
+    down_ref,
+    out_ref,
+    arrived,
+    tile,
+    listed,
+    labels,
+    total,
+    sems,
+    tile_sem,
+):
+    step = pl.program_id(0)
+
+    @pl.when(step == 0)
+    def _():
+        gather_slots(capacity, near_ref, arrived, tile, listed, labels, total, sems, tile_sem)
+
+    blocks = far_ref.shape[0]
+    forcing = (total[pl.ds(step * blocks, blocks)] + far_ref[...].astype(F32)).astype(BF16)
+    forcing = forcing.reshape(blocks * forcing.shape[1], forcing.shape[2])
+    driven = mix_ref[...].astype(F32) + lax.dot_general(
         force_ref[...], forcing, (((1,), (1,)), ((), ())), preferred_element_type=F32
     )
     normed = (normalised(driven, 0) * gain_ref[...]).astype(BF16)
     hidden = gelu(jnp.dot(up_ref[...], normed, preferred_element_type=F32).astype(BF16))
     change = jnp.dot(down_ref[...], hidden, preferred_element_type=F32)
-    out_ref[...] = (
-        now_ref[...].astype(F32) + sea_ref[...].astype(F32) * change
-    ).astype(BF16)
-
-
-def ocean(mixing, near, far, now, sea, w_force, gain, w_up, w_down):
+    out_ref[...] = (now_ref[...].astype(F32) + sea_ref[...].astype(F32) * change).astype(BF16)
+
+
+def ocean(capacity, mixing, near, far, now, sea, w_force, gain, w_up, w_down):
     channels, cells = now.shape
-    features = near.shape[1]
-    part = cells // 5
-    if part % 128:
-        part = cells
+    blocks, block, features = far.shape
+    peers = near.shape[0]
+    steps = 5 if blocks % 5 == 0 else 1
+    part = cells // steps
     tall = pl.BlockSpec((channels, part), lambda i: (0, i))
-    flat = pl.BlockSpec((part, features), lambda i: (i, 0))
     return pl.pallas_call(
-        ocean_kernel,
+        functools.partial(ocean_kernel, capacity),
         name="ocean",
-        grid=(cells // part,),
+        grid=(steps,),
         in_specs=[
             tall,
-            flat,
-            flat,
+            pl.BlockSpec(memory_space=pltpu.HBM),
+            pl.BlockSpec((blocks // steps, block, features), lambda i: (i, 0, 0)),
             tall,
             pl.BlockSpec((1, part), lambda i: (0, i)),
             whole(w_force.shape),
@@ -384,6 +416,7 @@
         ],
         out_specs=tall,
         out_shape=jax.ShapeDtypeStruct((channels, cells), BF16),
+        scratch_shapes=gather_scratch(peers, capacity, blocks, block, features),
         compiler_params=pltpu.CompilerParams(vmem_limit_bytes=48 << 20),
     )(
         in_hbm(mixing),
@@ -469,17 +502,16 @@
     far_arrived = exchange(far_made)
     near_made = near_remap(plan, *entry, surface, remap_weights)
     padded = jnp.concatenate([low, ocean_state, high], axis=1)
-    mixing = flat_mixing(padded, conv_kernel, OX, cell_count)
+    mixing = flat_mixing(padded, conv_kernel, OX, cell_count).astype(BF16)
     far_arrived, near_made, mixing = lax.optimization_barrier((far_arrived, near_made, mixing))
     near_arrived = exchange(near_made)
     far_sum = merged(capacity, far_arrived, ocean_blocks, block_rows)
     far_sum = lax.ppermute(far_sum, "half", [(0, 1), (1, 0)])
-    near_sum = merged(capacity, near_arrived, ocean_blocks, block_rows)
-    features = far_sum.shape[2]
     ocean_next = ocean(
+        capacity,
         mixing,
-        near_sum.reshape(cell_count, features),
-        far_sum.reshape(cell_count, features),
+        near_arrived,
+        far_sum,
         ocean_state,
         land_sea,
         w_force.T,

time: 201 us -> 206 us (1.025)
  waiting for transfers between devices: 102 us -> 108 us
    ppermute x1, waiting for transfers between devices: 5.71 us -> 80.5 us  [local(): far_sum = lax.ppermute(far_sum, 'half', [(0, 1), (1, 0)])]
    all_to_all x2, waiting for transfers between devices: 93.5 us -> 24.4 us  [exchange(): lax.all_to_all(values, PEERS, split_axis=0, concat_axis=0, tiled=True)]
    add x1 -> x0, other arithmetic: 13.4 us -> none  [flat_mixing(): summed = summed + kernel[:, 3 * row_step + col_step][:, None] * shifted]
    convert_element_type x0 -> x1, other arithmetic: none -> 13.4 us  [local(): mixing = flat_mixing(padded, conv_kernel, OX, cell_count).astype(BF16)]
    pallas_call x2 -> x1, Pallas kernels: 11.4 us -> 5.58 us  [merged(): pl.pallas_call(functools.partial(merge_kernel, capacity), name='merge', g...]
    pallas_call x1, Pallas kernels: 11 us -> 15.5 us  [ocean(): pl.pallas_call(functools.partial(ocean_kernel, capacity), name='ocean', g...]
  transfers between devices with their start and end apart: 5 -> 5, of which waited for: 4 -> 3; matrix products, arithmetic and copies ran while one was open for 11% -> 11% of each run, Pallas kernels for 20% -> 17%
where the time goes in v5:
time: 206 us; the launch traced here: 205 us
  waiting for transfers between devices  108 us (52%)
  Pallas kernels  49.5 us (24%)
  starting transfers between devices  22.4 us (11%)
  other arithmetic  16.2 us (8%)
  local copies, waits for them, and re-layouts  8.13 us (4%)
    ppermute x1, waiting for transfers between devices, local(): far_sum = lax.ppermute(far_sum, 'half', [(0, 1), (1, 0)])  80.5 us
    all_to_all x2, waiting for transfers between devices, exchange(): lax.all_to_all(values, PEERS, split_axis=0, concat_axis=0, tiled=True)  24.4 us
    pallas_call x1, Pallas kernels, atmosphere(): pl.pallas_call(functools.partial(atm_kernel, plan), name='atmosphere', gr...  20.5 us
    pallas_call x1, Pallas kernels, ocean(): pl.pallas_call(functools.partial(ocean_kernel, capacity), name='ocean', g...  15.5 us
    all_to_all x2, starting transfers between devices, exchange(): lax.all_to_all(values, PEERS, split_axis=0, concat_axis=0, tiled=True)  13.7 us
    convert_element_type x1, other arithmetic, local(): mixing = flat_mixing(padded, conv_kernel, OX, cell_count).astype(BF16)  13.4 us
    pallas_call x1, Pallas kernels, near_remap(): pl.pallas_call(functools.partial(near_kernel, plan), name='near_remap', g...  7.91 us
    concatenate x1, local copies, waits for them, and re-layouts, local(): padded = jnp.concatenate([low, ocean_state, high], axis=1)  5.6 us
  transfers between devices with their start and end apart: 5, of which 3 were waited for; matrix products, arithmetic and copies ran while one was open for 11% of the time, Pallas kernels for 17%

profile of v5, /device:TPU:14, one launch (start us, length us, event | category | flops | bytes accessed | tf_op | source)
XLA Modules:
  0.0 205.3 jit_solution(8759583759801180339)
XLA Ops:
  0.6 1.5 fusion.22
  2.1 3.4 %collective-permute-start = (bf16[200,1440]{1,0:T(8,128)(2,1)S(1)}, bf16[200,1440]{1,0:T(8,128)(2,1)S(1)}, u32[]{:S(2)}, u32[]{:S(2)}) collective-permute-start(bf16[200,1440]{1,0:T(8,128)(2,1)S(1)} %get-tuple-element.21), channel_id=1, source_target_pairs={{0,1},{1,2},{2,3},{3,4},{4,5},{5,6},{6,7},{7,8},{8,9},{9,10},{10,1... | collective-permute-start | bytes 1728008 | tf_op jit(solution)/shard_map/ppermute | solution.py:438
  5.5 2.4 %collective-permute-start.1 = (bf16[200,1440]{1,0:T(8,128)(2,1)S(1)}, bf16[200,1440]{1,0:T(8,128)(2,1)S(1)}, u32[]{:S(2)}, u32[]{:S(2)}) collective-permute-start(bf16[200,1440]{1,0:T(8,128)(2,1)S(1)} %get-tuple-element.20), channel_id=1, source_target_pairs={{1,0},{2,1},{3,2},{4,3},{5,4},{6,5},{7,6},{8,7},{9,8},{10,9},{11,1... | collective-permute-start | bytes 1728008 | tf_op jit(solution)/shard_map/ppermute | solution.py:439
  8.0 20.5 %atmosphere.1 = (bf16[1024,1024]{1,0:T(8,128)(2,1)}, bf16[1024,128]{1,0:T(8,128)(2,1)}, bf16[16,1040,128]{2,1,0:T(8,128)(2,1)}) custom-call(s32[1]{0:T(128)} %bitcast.half_ref, s32[128]{0:T(128)} %bitcast.19, s32[128]{0:T(128)} %source_ref.3, s32[128]{0:T(128)} %block_ref.3, bf16[1024,1024]{1,0:T(8,128)(2,1)} %x_ref.1, f32[1,1024]{1,0:T(1,128)} %bitcast.21, ...), custom_call_target="tpu_custom_call" | custom-call | tf_op jit(solution)/shard_map/atmosphere/pallas_call | solution.py:199
  28.5 0.0 copy-start.2
  28.5 0.0 copy-start.3
  28.6 0.0 copy-start.4
  28.6 0.0 collective-permute-done
  28.6 3.1 %collective-permute-done.1 = bf16[200,1440]{1,0:T(8,128)(2,1)S(1)} collective-permute-done((bf16[200,1440]{1,0:T(8,128)(2,1)S(1)}, bf16[200,1440]{1,0:T(8,128)(2,1)S(1)}, u32[]{:S(2)}, u32[]{:S(2)}) %collective-permute-start.1) | collective-permute-done | bytes 576032 | tf_op jit(solution)/shard_map/ppermute | solution.py:439
  31.7 6.8 %all-to-all-start = ((bf16[16,1040,128]{2,1,0:T(8,128)(2,1)}), bf16[16,1040,128]{2,1,0:T(8,128)(2,1)}, u32[]{:S(2)}, u32[]{:S(2)}) async-start(bf16[16,1040,128]{2,1,0:T(8,128)(2,1)} %get-tuple-element.13), calls=%async_computation | async-start | bytes 8519680 | tf_op jit(solution)/shard_map/all_to_all | solution.py:493
  38.4 0.0 copy-start.5
  38.5 7.9 %near_remap.1 = bf16[16,1040,128]{2,1,0:T(8,128)(2,1)} custom-call(s32[1]{0:T(128)} %bitcast.half_ref, s32[128]{0:T(128)S(1)} %bitcast.20, s32[128]{0:T(128)S(1)} %copy-done.3, s32[128]{0:T(128)S(1)} %copy-done.4, bf16[1024,128]{1,0:T(8,128)(2,1)} %get-tuple-element.14.surface_ref, bf16[128,128,128]{2,1,0:T(8,128)(2,1)} %weight_ref.3), custom_call_target="tpu_custom_call" | custom-call | tf_op jit(solution)/shard_map/near_remap/pallas_call | solution.py:275
  46.4 0.6 fusion.23
  47.1 5.6 %concatenate.3 = bf16[200,8640]{1,0:T(8,128)(2,1)} concatenate(bf16[200,1440]{1,0:T(8,128)(2,1)S(1)} %collective-permute-done, bf16[200,5760]{1,0:T(8,128)(2,1)S(1)} %copy-done.5, bf16[200,1440]{1,0:T(8,128)(2,1)S(1)} %collective-permute-done.1), dimensions={1} | concatenate | bytes 6912000 | tf_op jit(solution)/shard_map/concatenate | solution.py:504
  52.7 0.0 copy-start.13
  52.7 0.0 copy-start.14
  52.7 0.0 copy-start.15
  52.7 2.8 %convert_element_type.8 = f32[200,8640]{1,0:T(8,128)S(1)} convert(bf16[200,8640]{1,0:T(8,128)(2,1)} %concatenate.3) | non-fusion elementwise | flops 1728000 | bytes 10368000 | tf_op jit(solution)/shard_map/convert_element_type | solution.py:444
  55.6 13.4 %fusion.16.mix_ref = bf16[200,5760]{1,0:T(8,128)(2,1)} fusion(f32[200,8640]{1,0:T(8,128)S(1)} %convert_element_type.8, f32[200]{0:T(256)S(1)} %bitcast.29, f32[200]{0:T(256)S(1)} %bitcast.30, f32[200]{0:T(256)S(1)} %bitcast.23, f32[200]{0:T(256)S(1)} %bitcast.24, f32[200]{0:T(256)S(1)} %bitcast.25, f32[200]{0:T(256)S(1)} %bitcast.26, f32[200]{0:T(256)S(1)} %bitcast.27, ...), kind=kLoop, calls=%fused_computation.23 | loop fusion | flops 27648000 | bytes 41544704 | tf_op jit(solution)/shard_map/convert_element_type | solution.py:505
  69.0 24.4 %all-to-all-done.arrived_ref = bf16[16,1040,128]{2,1,0:T(8,128)(2,1)} async-done(((bf16[16,1040,128]{2,1,0:T(8,128)(2,1)}), bf16[16,1040,128]{2,1,0:T(8,128)(2,1)}, u32[]{:S(2)}, u32[]{:S(2)}) %all-to-all-start) | async-done | bytes 4259872 | tf_op jit(solution)/shard_map/all_to_all | solution.py:493
  93.3 6.9 %all-to-all-start.1 = ((bf16[16,1040,128]{2,1,0:T(8,128)(2,1)}), bf16[16,1040,128]{2,1,0:T(8,128)(2,1)}, u32[]{:S(2)}, u32[]{:S(2)}) async-start(bf16[16,1040,128]{2,1,0:T(8,128)(2,1)} %near_remap.1), calls=%async_computation.1 | async-start | bytes 8519680 | tf_op jit(solution)/shard_map/all_to_all | solution.py:493
  100.3 0.0 copy-start.17
  100.3 0.0 copy-start.7
  100.3 0.0 copy-start
  100.3 0.0 copy-start.1
  100.3 5.6 %merge.1 = bf16[45,128,128]{2,1,0:T(8,128)(2,1)} custom-call(bf16[16,1040,128]{2,1,0:T(8,128)(2,1)} %all-to-all-done.arrived_ref), custom_call_target="tpu_custom_call" | custom-call | tf_op jit(solution)/shard_map/merge/pallas_call | solution.py:345
  105.9 2.9 %collective-permute-start.2 = (bf16[45,128,128]{2,1,0:T(8,128)(2,1)}, bf16[45,128,128]{2,1,0:T(8,128)(2,1)S(1)}, u32[]{:S(2)}, u32[]{:S(2)}) collective-permute-start(bf16[45,128,128]{2,1,0:T(8,128)(2,1)} %merge.1), channel_id=1, source_target_pairs={{0,8},{8,0},{1,9},{9,1},{2,10},{10,2},{3,11},{11,3},{4,12},{12,4},... | collective-permute-start | bytes 4423688 | tf_op jit(solution)/shard_map/ppermute | solution.py:509
  108.8 0.2 copy.19
  109.0 0.1 copy.20.gain_ref
  109.2 80.5 %collective-permute-done.2.far_ref = bf16[45,128,128]{2,1,0:T(8,128)(2,1)S(1)} collective-permute-done((bf16[45,128,128]{2,1,0:T(8,128)(2,1)}, bf16[45,128,128]{2,1,0:T(8,128)(2,1)S(1)}, u32[]{:S(2)}, u32[]{:S(2)}) %collective-permute-start.2) | collective-permute-done | bytes 1474592 | tf_op jit(solution)/shard_map/ppermute | solution.py:509
  189.7 0.0 all-to-all-done.1.near_ref
  189.7 15.5 %ocean.1 = bf16[200,5760]{1,0:T(8,128)(2,1)} custom-call(bf16[200,5760]{1,0:T(8,128)(2,1)} %fusion.16.mix_ref, bf16[16,1040,128]{2,1,0:T(8,128)(2,1)} %all-to-all-done.1.near_ref, bf16[45,128,128]{2,1,0:T(8,128)(2,1)S(1)} %collective-permute-done.2.far_ref, bf16[200,5760]{1,0:T(8,128)(2,1)} %now_ref.1, s32[1,5760]{1,0:T(1,128)S(1)} %broadcast_in_dim.50.sea_ref, ...), custom_call_target="tpu_custom_call" | custom-call | tf_op jit(solution)/shard_map/ocean/pallas_call | solution.py:402
  (27 shorter events, 0.1 us)
Async XLA Ops:
  2.1 26.4 %collective-permute-start = (bf16[200,1440]{1,0:T(8,128)(2,1)S(1)}, bf16[200,1440]{1,0:T(8,128)(2,1)S(1)}, u32[]{:S(2)}, u32[]{:S(2)}) collective-permute-start(bf16[200,1440]{1,0:T(8,128)(2,1)S(1)} %get-tuple-element.21), channel_id=1, source_target_pairs={{0,1},{1,2},{2,3},{3,4},{4,5},{5,6},{6,7},{7,8},{8,9},{9,10},{10,1... | collective-permute-start | bytes 1728008 | tf_op jit(solution)/shard_map/ppermute | solution.py:438
  5.5 26.1 %collective-permute-start.1 = (bf16[200,1440]{1,0:T(8,128)(2,1)S(1)}, bf16[200,1440]{1,0:T(8,128)(2,1)S(1)}, u32[]{:S(2)}, u32[]{:S(2)}) collective-permute-start(bf16[200,1440]{1,0:T(8,128)(2,1)S(1)} %get-tuple-element.20), channel_id=1, source_target_pairs={{1,0},{2,1},{3,2},{4,3},{5,4},{6,5},{7,6},{8,7},{9,8},{10,9},{11,1... | collective-permute-start | bytes 1728008 | tf_op jit(solution)/shard_map/ppermute | solution.py:439
  28.5 9.9 %copy-start.2 = (s32[128,1]{0,1:T(1,128)S(1)}, s32[128,1]{0,1:T(1,128)}, u32[]{:S(2)}) copy-start(s32[128,1]{0,1:T(1,128)} %param.22) | copy-start | bytes 1540
  28.5 9.9 %copy-start.3 = (s32[128]{0:T(128)S(1)}, s32[128]{0:T(128)}, u32[]{:S(2)}) copy-start(s32[128]{0:T(128)} %source_ref.3) | copy-start | bytes 1540
  28.6 9.9 %copy-start.4 = (s32[128]{0:T(128)S(1)}, s32[128]{0:T(128)}, u32[]{:S(2)}) copy-start(s32[128]{0:T(128)} %block_ref.3) | copy-start | bytes 1540
  31.7 61.7 %all-to-all-start = ((bf16[16,1040,128]{2,1,0:T(8,128)(2,1)}), bf16[16,1040,128]{2,1,0:T(8,128)(2,1)}, u32[]{:S(2)}, u32[]{:S(2)}) async-start(bf16[16,1040,128]{2,1,0:T(8,128)(2,1)} %get-tuple-element.13), calls=%async_computation | async-start | bytes 8519680 | tf_op jit(solution)/shard_map/all_to_all | solution.py:493
  38.4 8.0 %copy-start.8 = (f32[200,9]{0,1:T(8,128)S(1)}, f32[200,9]{0,1:T(8,128)}, u32[]{:S(2)}) copy-start(f32[200,9]{0,1:T(8,128)} %param.27) | copy-start | bytes 21604
  38.4 8.6 %copy-start.5 = (bf16[200,5760]{1,0:T(8,128)(2,1)S(1)}, bf16[200,5760]{1,0:T(8,128)(2,1)}, u32[]{:S(2)}) copy-start(bf16[200,5760]{1,0:T(8,128)(2,1)} %now_ref.1) | copy-start | bytes 6912004
  52.7 2.8 %copy-start.9 = (f32[200,1]{0,1:T(1,128)S(1)}, f32[200,1]{0,1:T(1,128)}, u32[]{:S(2)}) copy-start(f32[200,1]{0,1:T(1,128)} %get-tuple-element.23) | copy-start | bytes 2404
  52.7 2.8 %copy-start.10 = (f32[200,1]{0,1:T(1,128)S(1)}, f32[200,1]{0,1:T(1,128)}, u32[]{:S(2)}) copy-start(f32[200,1]{0,1:T(1,128)} %get-tuple-element.24) | copy-start | bytes 2404
  52.7 2.9 %copy-start.11 = (f32[200,1]{0,1:T(1,128)S(1)}, f32[200,1]{0,1:T(1,128)}, u32[]{:S(2)}) copy-start(f32[200,1]{0,1:T(1,128)} %get-tuple-element.25) | copy-start | bytes 2404
  52.7 2.9 %copy-start.12 = (f32[200,1]{0,1:T(1,128)S(1)}, f32[200,1]{0,1:T(1,128)}, u32[]{:S(2)}) copy-start(f32[200,1]{0,1:T(1,128)} %get-tuple-element.26) | copy-start | bytes 2404
  52.7 2.9 %copy-start.13 = (f32[200,1]{0,1:T(1,128)S(1)}, f32[200,1]{0,1:T(1,128)}, u32[]{:S(2)}) copy-start(f32[200,1]{0,1:T(1,128)} %get-tuple-element.27) | copy-start | bytes 2404
  52.7 2.9 %copy-start.14 = (f32[200,1]{0,1:T(1,128)S(1)}, f32[200,1]{0,1:T(1,128)}, u32[]{:S(2)}) copy-start(f32[200,1]{0,1:T(1,128)} %get-tuple-element.28) | copy-start | bytes 2404
  52.7 2.9 %copy-start.15 = (f32[200,1]{0,1:T(1,128)S(1)}, f32[200,1]{0,1:T(1,128)}, u32[]{:S(2)}) copy-start(f32[200,1]{0,1:T(1,128)} %get-tuple-element.29) | copy-start | bytes 2404
  52.7 2.9 %copy-start.16 = (f32[200,1]{0,1:T(1,128)S(1)}, f32[200,1]{0,1:T(1,128)}, u32[]{:S(2)}) copy-start(f32[200,1]{0,1:T(1,128)} %get-tuple-element.30) | copy-start | bytes 2404
  93.3 96.4 %all-to-all-start.1 = ((bf16[16,1040,128]{2,1,0:T(8,128)(2,1)}), bf16[16,1040,128]{2,1,0:T(8,128)(2,1)}, u32[]{:S(2)}, u32[]{:S(2)}) async-start(bf16[16,1040,128]{2,1,0:T(8,128)(2,1)} %near_remap.1), calls=%async_computation.1 | async-start | bytes 8519680 | tf_op jit(solution)/shard_map/all_to_all | solution.py:493
  100.3 8.5 %copy-start.6 = (bf16[200,800]{1,0:T(8,128)(2,1)S(1)}, bf16[200,800]{1,0:T(8,128)(2,1)}, u32[]{:S(2)}) copy-start(bf16[200,800]{1,0:T(8,128)(2,1)} %param.30) | copy-start | bytes 960004
  100.3 8.7 %copy-start.17 = (f32[200]{0:T(256)S(1)}, f32[200]{0:T(256)}, u32[]{:S(2)}) copy-start(f32[200]{0:T(256)} %param.29) | copy-start | bytes 2404
  100.3 8.8 %copy-start.7 = (s32[5760]{0:T(1024)S(1)}, s32[5760]{0:T(1024)}, u32[]{:S(2)}) copy-start(s32[5760]{0:T(1024)} %param.26) | copy-start | bytes 69124
  100.3 89.4 %copy-start = (bf16[800,200]{0,1:T(8,128)(2,1)S(1)}, bf16[800,200]{0,1:T(8,128)(2,1)}, u32[]{:S(2)}) copy-start(bf16[800,200]{0,1:T(8,128)(2,1)} %param.31) | copy-start | bytes 960004
  100.3 89.4 %copy-start.1 = (bf16[128,200]{0,1:T(8,128)(2,1)S(1)}, bf16[128,200]{0,1:T(8,128)(2,1)}, u32[]{:S(2)}) copy-start(bf16[128,200]{0,1:T(8,128)(2,1)} %param.28) | copy-start | bytes 153604
  105.9 83.8 %collective-permute-start.2 = (bf16[45,128,128]{2,1,0:T(8,128)(2,1)}, bf16[45,128,128]{2,1,0:T(8,128)(2,1)S(1)}, u32[]{:S(2)}, u32[]{:S(2)}) collective-permute-start(bf16[45,128,128]{2,1,0:T(8,128)(2,1)} %merge.1), channel_id=1, source_target_pairs={{0,8},{8,0},{1,9},{9,1},{2,10},{10,2},{3,11},{11,3},{4,12},{12,4},... | collective-permute-start | bytes 4423688 | tf_op jit(solution)/shard_map/ppermute | solution.py:509

commit v6 on v4

--- a/solution.py
+++ b/solution.py
@@ -28,6 +28,10 @@
 
 def in_hbm(value):
     return pltpu.with_memory_space_constraint(value, pltpu.HBM)
+
+
+def in_vmem(value):
+    return pltpu.with_memory_space_constraint(value, pltpu.VMEM)
 
 
 def whole(shape):
@@ -341,14 +345,14 @@
             pltpu.SemaphoreType.DMA((peers,)),
             pltpu.SemaphoreType.DMA,
         ],
-        out_shape=pltpu.HBM((blocks, block, features), BF16),
+        out_shape=jax.ShapeDtypeStruct((blocks, block, features), BF16),
         compiler_params=pltpu.CompilerParams(vmem_limit_bytes=32 << 20),
     )(in_hbm(arrived))
 
 
 def ocean_kernel(mix_ref, near_ref, far_ref, now_ref, sea_ref, force_ref, gain_ref, up_ref, down_ref, out_ref):
     forcing = (near_ref[...].astype(F32) + far_ref[...].astype(F32)).astype(BF16)
-    driven = mix_ref[...] + lax.dot_general(
+    driven = mix_ref[...].astype(F32) + lax.dot_general(
         force_ref[...], forcing, (((1,), (1,)), ((), ())), preferred_element_type=F32
     )
     normed = (normalised(driven, 0) * gain_ref[...]).astype(BF16)
@@ -362,7 +366,7 @@
 def ocean(mixing, near, far, now, sea, w_force, gain, w_up, w_down):
     channels, cells = now.shape
     features = near.shape[1]
-    part = cells // 5
+    part = cells // 3
     if part % 128:
         part = cells
     tall = pl.BlockSpec((channels, part), lambda i: (0, i))
@@ -384,17 +388,17 @@
         ],
         out_specs=tall,
         out_shape=jax.ShapeDtypeStruct((channels, cells), BF16),
-        compiler_params=pltpu.CompilerParams(vmem_limit_bytes=48 << 20),
+        compiler_params=pltpu.CompilerParams(vmem_limit_bytes=32 << 20),
     )(
-        in_hbm(mixing),
-        in_hbm(near),
-        far,
-        in_hbm(now),
-        sea[None, :],
-        w_force,
-        gain[:, None],
-        w_up,
-        w_down,
+        in_vmem(mixing),
+        in_vmem(near),
+        in_vmem(far),
+        in_vmem(now),
+        in_vmem(sea[None, :]),
+        in_vmem(w_force),
+        in_vmem(gain[:, None]),
+        in_vmem(w_up),
+        in_vmem(w_down),
     )
 
 
@@ -469,7 +473,7 @@
     far_arrived = exchange(far_made)
     near_made = near_remap(plan, *entry, surface, remap_weights)
     padded = jnp.concatenate([low, ocean_state, high], axis=1)
-    mixing = flat_mixing(padded, conv_kernel, OX, cell_count)
+    mixing = flat_mixing(padded, conv_kernel, OX, cell_count).astype(BF16)
     far_arrived, near_made, mixing = lax.optimization_barrier((far_arrived, near_made, mixing))
     near_arrived = exchange(near_made)
     far_sum = merged(capacity, far_arrived, ocean_blocks, block_rows)

time: 201 us -> 201 us (level)
    add x1 -> x0, other arithmetic: 13.4 us -> none  [flat_mixing(): summed = summed + kernel[:, 3 * row_step + col_step][:, None] * shifted]
    convert_element_type x0 -> x1, other arithmetic: none -> 13.3 us  [local(): mixing = flat_mixing(padded, conv_kernel, OX, cell_count).astype(BF16)]
where the time goes in v6:
time: 201 us; the launch traced here: 200 us
  waiting for transfers between devices  103 us (51%)
  Pallas kernels  49.8 us (25%)
  starting transfers between devices  22.4 us (11%)
  other arithmetic  16.1 us (8%)
  local copies, waits for them, and re-layouts  8.09 us (4%)
    all_to_all x2, waiting for transfers between devices, exchange(): lax.all_to_all(values, PEERS, split_axis=0, concat_axis=0, tiled=True)  93.3 us
    pallas_call x1, Pallas kernels, atmosphere(): pl.pallas_call(functools.partial(atm_kernel, plan), name='atmosphere', gr...  20.8 us
    all_to_all x2, starting transfers between devices, exchange(): lax.all_to_all(values, PEERS, split_axis=0, concat_axis=0, tiled=True)  13.7 us
    convert_element_type x1, other arithmetic, local(): mixing = flat_mixing(padded, conv_kernel, OX, cell_count).astype(BF16)  13.3 us
    pallas_call x1, Pallas kernels, ocean(): pl.pallas_call(ocean_kernel, name='ocean', grid=(cells // part,), in_spec...  10.3 us
    pallas_call x2, Pallas kernels, merged(): pl.pallas_call(functools.partial(merge_kernel, capacity), name='merge', g...  10.3 us
    pallas_call x1, Pallas kernels, near_remap(): pl.pallas_call(functools.partial(near_kernel, plan), name='near_remap', g...  8.32 us
    ppermute x1, waiting for transfers between devices, local(): far_sum = lax.ppermute(far_sum, 'half', [(0, 1), (1, 0)])  6.67 us
  transfers between devices with their start and end apart: 5, of which 4 were waited for; matrix products, arithmetic and copies ran while one was open for 11% of the time, Pallas kernels for 20%

profile of v6, /device:TPU:14, one launch (start us, length us, event | category | flops | bytes accessed | tf_op | source)
XLA Modules:
  0.0 200.1 jit_solution(11130529552502008693)
XLA Ops:
  0.6 1.5 fusion.22
  2.1 3.4 %collective-permute-start = (bf16[200,1440]{1,0:T(8,128)(2,1)S(1)}, bf16[200,1440]{1,0:T(8,128)(2,1)S(1)}, u32[]{:S(2)}, u32[]{:S(2)}) collective-permute-start(bf16[200,1440]{1,0:T(8,128)(2,1)S(1)} %get-tuple-element.21), channel_id=1, source_target_pairs={{0,1},{1,2},{2,3},{3,4},{4,5},{5,6},{6,7},{7,8},{8,9},{9,10},{10,1... | collective-permute-start | bytes 1728008 | tf_op jit(solution)/shard_map/ppermute | solution.py:409
  5.5 2.4 %collective-permute-start.1 = (bf16[200,1440]{1,0:T(8,128)(2,1)S(1)}, bf16[200,1440]{1,0:T(8,128)(2,1)S(1)}, u32[]{:S(2)}, u32[]{:S(2)}) collective-permute-start(bf16[200,1440]{1,0:T(8,128)(2,1)S(1)} %get-tuple-element.20), channel_id=1, source_target_pairs={{1,0},{2,1},{3,2},{4,3},{5,4},{6,5},{7,6},{8,7},{9,8},{10,9},{11,1... | collective-permute-start | bytes 1728008 | tf_op jit(solution)/shard_map/ppermute | solution.py:410
  8.0 20.8 %atmosphere.1 = (bf16[1024,1024]{1,0:T(8,128)(2,1)}, bf16[1024,128]{1,0:T(8,128)(2,1)}, bf16[16,1040,128]{2,1,0:T(8,128)(2,1)}) custom-call(s32[1]{0:T(128)} %bitcast.half_ref, s32[128]{0:T(128)} %bitcast.22, s32[128]{0:T(128)} %source_ref.3, s32[128]{0:T(128)} %block_ref.3, bf16[1024,1024]{1,0:T(8,128)(2,1)} %x_ref.1, f32[1,1024]{1,0:T(1,128)} %bitcast.24, ...), custom_call_target="tpu_custom_call" | custom-call | tf_op jit(solution)/shard_map/atmosphere/pallas_call | solution.py:203
  28.8 0.0 copy-start.4
  28.9 0.0 copy-start.5
  28.9 0.0 copy-start.6
  28.9 0.0 collective-permute-done
  28.9 2.8 %collective-permute-done.1 = bf16[200,1440]{1,0:T(8,128)(2,1)S(1)} collective-permute-done((bf16[200,1440]{1,0:T(8,128)(2,1)S(1)}, bf16[200,1440]{1,0:T(8,128)(2,1)S(1)}, u32[]{:S(2)}, u32[]{:S(2)}) %collective-permute-start.1) | collective-permute-done | bytes 576032 | tf_op jit(solution)/shard_map/ppermute | solution.py:410
  31.7 6.7 %all-to-all-start = ((bf16[16,1040,128]{2,1,0:T(8,128)(2,1)}), bf16[16,1040,128]{2,1,0:T(8,128)(2,1)}, u32[]{:S(2)}, u32[]{:S(2)}) async-start(bf16[16,1040,128]{2,1,0:T(8,128)(2,1)} %get-tuple-element.13), calls=%async_computation | async-start | bytes 8519680 | tf_op jit(solution)/shard_map/all_to_all | solution.py:464
  38.4 0.0 copy-start
  38.4 0.0 copy-done.4
  38.5 8.3 %near_remap.1 = bf16[16,1040,128]{2,1,0:T(8,128)(2,1)} custom-call(s32[1]{0:T(128)} %bitcast.half_ref, s32[128]{0:T(128)S(1)} %bitcast.23, s32[128]{0:T(128)S(1)} %copy-done.5, s32[128]{0:T(128)S(1)} %copy-done.6, bf16[1024,128]{1,0:T(8,128)(2,1)} %get-tuple-element.14.surface_ref, bf16[128,128,128]{2,1,0:T(8,128)(2,1)} %weight_ref.3), custom_call_target="tpu_custom_call" | custom-call | tf_op jit(solution)/shard_map/near_remap/pallas_call | solution.py:279
  46.8 0.6 fusion.23
  47.4 5.6 %concatenate.3 = bf16[200,8640]{1,0:T(8,128)(2,1)} concatenate(bf16[200,1440]{1,0:T(8,128)(2,1)S(1)} %collective-permute-done, bf16[200,5760]{1,0:T(8,128)(2,1)S(1)} %copy-done, bf16[200,1440]{1,0:T(8,128)(2,1)S(1)} %collective-permute-done.1), dimensions={1} | concatenate | bytes 6912000 | tf_op jit(solution)/shard_map/concatenate | solution.py:475
  53.1 2.8 %convert_element_type.8 = f32[200,8640]{1,0:T(8,128)S(1)} convert(bf16[200,8640]{1,0:T(8,128)(2,1)} %concatenate.3) | non-fusion elementwise | flops 1728000 | bytes 10368000 | tf_op jit(solution)/shard_map/convert_element_type | solution.py:415
  55.9 13.3 %fusion.16.mix_ref = bf16[200,5760]{1,0:T(8,128)(2,1)} fusion(f32[200,8640]{1,0:T(8,128)S(1)} %convert_element_type.8, f32[200]{0:T(256)S(1)} %bitcast.32, f32[200]{0:T(256)S(1)} %bitcast.33, f32[200]{0:T(256)S(1)} %bitcast.26, f32[200]{0:T(256)S(1)} %bitcast.27, f32[200]{0:T(256)S(1)} %bitcast.28, f32[200]{0:T(256)S(1)} %bitcast.29, f32[200]{0:T(256)S(1)} %bitcast.30, ...), kind=kLoop, calls=%fused_computation.23 | loop fusion | flops 27648000 | bytes 41544704 | tf_op jit(solution)/shard_map/convert_element_type | solution.py:476
  69.3 24.0 %all-to-all-done.arrived_ref = bf16[16,1040,128]{2,1,0:T(8,128)(2,1)} async-done(((bf16[16,1040,128]{2,1,0:T(8,128)(2,1)}), bf16[16,1040,128]{2,1,0:T(8,128)(2,1)}, u32[]{:S(2)}, u32[]{:S(2)}) %all-to-all-start) | async-done | bytes 4259872 | tf_op jit(solution)/shard_map/all_to_all | solution.py:464
  93.3 6.9 %all-to-all-start.1 = ((bf16[16,1040,128]{2,1,0:T(8,128)(2,1)}), bf16[16,1040,128]{2,1,0:T(8,128)(2,1)}, u32[]{:S(2)}, u32[]{:S(2)}) async-start(bf16[16,1040,128]{2,1,0:T(8,128)(2,1)} %near_remap.1), calls=%async_computation.1 | async-start | bytes 8519680 | tf_op jit(solution)/shard_map/all_to_all | solution.py:464
  100.3 0.0 copy-start.18
  100.3 0.0 copy-start.8
  100.3 5.5 %merge.3 = bf16[45,128,128]{2,1,0:T(8,128)(2,1)} custom-call(bf16[16,1040,128]{2,1,0:T(8,128)(2,1)} %all-to-all-done.arrived_ref), custom_call_target="tpu_custom_call" | custom-call | tf_op jit(solution)/shard_map/merge/pallas_call | solution.py:333
  105.8 0.0 copy-start.2
  105.8 0.0 copy-start.3
  105.8 2.9 %collective-permute-start.2 = (bf16[45,128,128]{2,1,0:T(8,128)(2,1)}, bf16[45,128,128]{2,1,0:T(8,128)(2,1)}, u32[]{:S(2)}, u32[]{:S(2)}) collective-permute-start(bf16[45,128,128]{2,1,0:T(8,128)(2,1)} %merge.3), channel_id=1, source_target_pairs={{0,8},{8,0},{1,9},{9,1},{2,10},{10,2},{3,11},{11,3},{4,12},{12,4},... | collective-permute-start | bytes 4423688 | tf_op jit(solution)/shard_map/ppermute | solution.py:480
  108.8 0.2 copy.19
  109.0 0.1 copy.20.gain_ref
  109.1 69.2 %all-to-all-done.1.arrived_ref = bf16[16,1040,128]{2,1,0:T(8,128)(2,1)} async-done(((bf16[16,1040,128]{2,1,0:T(8,128)(2,1)}), bf16[16,1040,128]{2,1,0:T(8,128)(2,1)}, u32[]{:S(2)}, u32[]{:S(2)}) %all-to-all-start.1) | async-done | bytes 4259872 | tf_op jit(solution)/shard_map/all_to_all | solution.py:464
  178.4 4.8 %merge.2 = bf16[45,128,128]{2,1,0:T(8,128)(2,1)S(1)} custom-call(bf16[16,1040,128]{2,1,0:T(8,128)(2,1)} %all-to-all-done.1.arrived_ref), custom_call_target="tpu_custom_call" | custom-call | tf_op jit(solution)/shard_map/merge/pallas_call | solution.py:333
  183.1 6.7 %collective-permute-done.2 = bf16[45,128,128]{2,1,0:T(8,128)(2,1)} collective-permute-done((bf16[45,128,128]{2,1,0:T(8,128)(2,1)}, bf16[45,128,128]{2,1,0:T(8,128)(2,1)}, u32[]{:S(2)}, u32[]{:S(2)}) %collective-permute-start.2) | collective-permute-done | bytes 1474592 | tf_op jit(solution)/shard_map/ppermute | solution.py:480
  189.8 0.0 copy-done.1
  189.8 10.3 %ocean.1 = bf16[200,5760]{1,0:T(8,128)(2,1)} custom-call(bf16[200,5760]{1,0:T(8,128)(2,1)S(1)} %copy-done.1, bf16[5760,128]{1,0:T(8,128)(2,1)S(1)} %bitcast.18, bf16[5760,128]{1,0:T(8,128)(2,1)} %bitcast.13.far_ref, bf16[200,5760]{1,0:T(8,128)(2,1)S(1)} %copy-done, s32[1,5760]{1,0:T(1,128)S(1)} %broadcast_in_dim.50.sea_ref, bf16[200,128]{1,0:T(8,128)(2,1)S(1)} %bitcast.21, ...), custom_call_target="tpu_custom_call" | custom-call | tf_op jit(solution)/shard_map/ocean/pallas_call | solution.py:374
  (30 shorter events, 0.1 us)
Async XLA Ops:
  2.1 26.7 %collective-permute-start = (bf16[200,1440]{1,0:T(8,128)(2,1)S(1)}, bf16[200,1440]{1,0:T(8,128)(2,1)S(1)}, u32[]{:S(2)}, u32[]{:S(2)}) collective-permute-start(bf16[200,1440]{1,0:T(8,128)(2,1)S(1)} %get-tuple-element.21), channel_id=1, source_target_pairs={{0,1},{1,2},{2,3},{3,4},{4,5},{5,6},{6,7},{7,8},{8,9},{9,10},{10,1... | collective-permute-start | bytes 1728008 | tf_op jit(solution)/shard_map/ppermute | solution.py:409
  5.5 26.1 %collective-permute-start.1 = (bf16[200,1440]{1,0:T(8,128)(2,1)S(1)}, bf16[200,1440]{1,0:T(8,128)(2,1)S(1)}, u32[]{:S(2)}, u32[]{:S(2)}) collective-permute-start(bf16[200,1440]{1,0:T(8,128)(2,1)S(1)} %get-tuple-element.20), channel_id=1, source_target_pairs={{1,0},{2,1},{3,2},{4,3},{5,4},{6,5},{7,6},{8,7},{9,8},{10,9},{11,1... | collective-permute-start | bytes 1728008 | tf_op jit(solution)/shard_map/ppermute | solution.py:410
  28.8 9.6 %copy-start.4 = (s32[128,1]{0,1:T(1,128)S(1)}, s32[128,1]{0,1:T(1,128)}, u32[]{:S(2)}) copy-start(s32[128,1]{0,1:T(1,128)} %param.22) | copy-start | bytes 1540
  28.9 9.6 %copy-start.5 = (s32[128]{0:T(128)S(1)}, s32[128]{0:T(128)}, u32[]{:S(2)}) copy-start(s32[128]{0:T(128)} %source_ref.3) | copy-start | bytes 1540
  28.9 9.6 %copy-start.6 = (s32[128]{0:T(128)S(1)}, s32[128]{0:T(128)}, u32[]{:S(2)}) copy-start(s32[128]{0:T(128)} %block_ref.3) | copy-start | bytes 1540
  31.7 61.6 %all-to-all-start = ((bf16[16,1040,128]{2,1,0:T(8,128)(2,1)}), bf16[16,1040,128]{2,1,0:T(8,128)(2,1)}, u32[]{:S(2)}, u32[]{:S(2)}) async-start(bf16[16,1040,128]{2,1,0:T(8,128)(2,1)} %get-tuple-element.13), calls=%async_computation | async-start | bytes 8519680 | tf_op jit(solution)/shard_map/all_to_all | solution.py:464
  38.4 8.4 %copy-start.9 = (f32[200,9]{0,1:T(8,128)S(1)}, f32[200,9]{0,1:T(8,128)}, u32[]{:S(2)}) copy-start(f32[200,9]{0,1:T(8,128)} %param.27) | copy-start | bytes 21604
  38.4 9.0 %copy-start = (bf16[200,5760]{1,0:T(8,128)(2,1)S(1)}, bf16[200,5760]{1,0:T(8,128)(2,1)}, u32[]{:S(2)}) copy-start(bf16[200,5760]{1,0:T(8,128)(2,1)} %now_ref.1) | copy-start | bytes 6912004
  53.0 2.8 %copy-start.10 = (f32[200,1]{0,1:T(1,128)S(1)}, f32[200,1]{0,1:T(1,128)}, u32[]{:S(2)}) copy-start(f32[200,1]{0,1:T(1,128)} %get-tuple-element.23) | copy-start | bytes 2404
  53.0 2.8 %copy-start.11 = (f32[200,1]{0,1:T(1,128)S(1)}, f32[200,1]{0,1:T(1,128)}, u32[]{:S(2)}) copy-start(f32[200,1]{0,1:T(1,128)} %get-tuple-element.24) | copy-start | bytes 2404
  53.0 2.9 %copy-start.12 = (f32[200,1]{0,1:T(1,128)S(1)}, f32[200,1]{0,1:T(1,128)}, u32[]{:S(2)}) copy-start(f32[200,1]{0,1:T(1,128)} %get-tuple-element.25) | copy-start | bytes 2404
  53.0 2.9 %copy-start.13 = (f32[200,1]{0,1:T(1,128)S(1)}, f32[200,1]{0,1:T(1,128)}, u32[]{:S(2)}) copy-start(f32[200,1]{0,1:T(1,128)} %get-tuple-element.26) | copy-start | bytes 2404
  53.0 2.9 %copy-start.14 = (f32[200,1]{0,1:T(1,128)S(1)}, f32[200,1]{0,1:T(1,128)}, u32[]{:S(2)}) copy-start(f32[200,1]{0,1:T(1,128)} %get-tuple-element.27) | copy-start | bytes 2404
  53.0 2.9 %copy-start.15 = (f32[200,1]{0,1:T(1,128)S(1)}, f32[200,1]{0,1:T(1,128)}, u32[]{:S(2)}) copy-start(f32[200,1]{0,1:T(1,128)} %get-tuple-element.28) | copy-start | bytes 2404
  53.1 2.9 %copy-start.16 = (f32[200,1]{0,1:T(1,128)S(1)}, f32[200,1]{0,1:T(1,128)}, u32[]{:S(2)}) copy-start(f32[200,1]{0,1:T(1,128)} %get-tuple-element.29) | copy-start | bytes 2404
  53.1 2.9 %copy-start.17 = (f32[200,1]{0,1:T(1,128)S(1)}, f32[200,1]{0,1:T(1,128)}, u32[]{:S(2)}) copy-start(f32[200,1]{0,1:T(1,128)} %get-tuple-element.30) | copy-start | bytes 2404
  93.3 85.0 %all-to-all-start.1 = ((bf16[16,1040,128]{2,1,0:T(8,128)(2,1)}), bf16[16,1040,128]{2,1,0:T(8,128)(2,1)}, u32[]{:S(2)}, u32[]{:S(2)}) async-start(bf16[16,1040,128]{2,1,0:T(8,128)(2,1)} %near_remap.1), calls=%async_computation.1 | async-start | bytes 8519680 | tf_op jit(solution)/shard_map/all_to_all | solution.py:464
  100.3 8.5 %copy-start.7 = (bf16[200,800]{1,0:T(8,128)(2,1)S(1)}, bf16[200,800]{1,0:T(8,128)(2,1)}, u32[]{:S(2)}) copy-start(bf16[200,800]{1,0:T(8,128)(2,1)} %param.30) | copy-start | bytes 960004
  100.3 8.7 %copy-start.18 = (f32[200]{0:T(256)S(1)}, f32[200]{0:T(256)}, u32[]{:S(2)}) copy-start(f32[200]{0:T(256)} %param.29) | copy-start | bytes 2404
  100.3 8.8 %copy-start.8 = (s32[5760]{0:T(1024)S(1)}, s32[5760]{0:T(1024)}, u32[]{:S(2)}) copy-start(s32[5760]{0:T(1024)} %param.26) | copy-start | bytes 69124
  105.8 84.0 %copy-start.2 = (bf16[800,200]{0,1:T(8,128)(2,1)S(1)}, bf16[800,200]{0,1:T(8,128)(2,1)}, u32[]{:S(2)}) copy-start(bf16[800,200]{0,1:T(8,128)(2,1)} %param.31) | copy-start | bytes 960004
  105.8 84.0 %copy-start.3 = (bf16[128,200]{0,1:T(8,128)(2,1)S(1)}, bf16[128,200]{0,1:T(8,128)(2,1)}, u32[]{:S(2)}) copy-start(bf16[128,200]{0,1:T(8,128)(2,1)} %param.28) | copy-start | bytes 153604
  105.8 84.0 %collective-permute-start.2 = (bf16[45,128,128]{2,1,0:T(8,128)(2,1)}, bf16[45,128,128]{2,1,0:T(8,128)(2,1)}, u32[]{:S(2)}, u32[]{:S(2)}) collective-permute-start(bf16[45,128,128]{2,1,0:T(8,128)(2,1)} %merge.3), channel_id=1, source_target_pairs={{0,8},{8,0},{1,9},{9,1},{2,10},{10,2},{3,11},{11,3},{4,12},{12,4},... | collective-permute-start | bytes 4423688 | tf_op jit(solution)/shard_map/ppermute | solution.py:480
  178.4 11.5 %copy-start.1 = (bf16[200,5760]{1,0:T(8,128)(2,1)S(1)}, bf16[200,5760]{1,0:T(8,128)(2,1)}, u32[]{:S(2)}) copy-start(bf16[200,5760]{1,0:T(8,128)(2,1)} %fusion.16.mix_ref) | copy-start | bytes 6912004

commit v7 on v6

--- a/solution.py
+++ b/solution.py
@@ -404,11 +404,16 @@
 
 def edge_rows(block):
     count = math.prod(lax.axis_size(axis) for axis in ALL)
-    forward = [(i, i + 1) for i in range(count - 1)]
-    backward = [(target, source) for source, target in forward]
-    low = lax.ppermute(block[:, -OX:], ALL, forward)
-    high = lax.ppermute(block[:, :OX], ALL, backward)
-    return low, high
+    even = (lax.axis_index(ALL) & 1) == 0
+    first, last = block[:, :OX], block[:, -OX:]
+
+    def exchanged(mine, start):
+        pairs = [(i, i + 1) for i in range(start, count - 1, 2)]
+        return lax.ppermute(mine, ALL, pairs + [(upper, lower) for lower, upper in pairs])
+
+    across = exchanged(jnp.where(even, first, last), 1)
+    beside = exchanged(jnp.where(even, last, first), 0)
+    return even, across, beside
 
 
 def flat_mixing(padded_flat, kernel, row_len, cell_count):
@@ -468,10 +473,11 @@
     atm_next, surface, far_made = atmosphere(
         plan, *entry, atm_state, gain_atm, w_up_atm, w_down_atm, w_flux, remap_weights
     )
-    low, high = edge_rows(ocean_state)
-    far_made, low, high = lax.optimization_barrier((far_made, low, high))
+    even, across, beside = edge_rows(ocean_state)
+    far_made, across, beside = lax.optimization_barrier((far_made, across, beside))
     far_arrived = exchange(far_made)
     near_made = near_remap(plan, *entry, surface, remap_weights)
+    low, high = jnp.where(even, across, beside), jnp.where(even, beside, across)
     padded = jnp.concatenate([low, ocean_state, high], axis=1)
     mixing = flat_mixing(padded, conv_kernel, OX, cell_count).astype(BF16)
     far_arrived, near_made, mixing = lax.optimization_barrier((far_arrived, near_made, mixing))

time: 201 us -> 201 us (level)
  starting transfers between devices: 22.4 us -> 19.4 us
  other arithmetic: 16.1 us -> 19 us
    ppermute x2, waiting for transfers between devices: 2.8 us -> 5.86 us  [exchanged(): lax.ppermute(mine, ALL, pairs + [(upper, lower) for lower, upper in pairs])]
    select_n x0 -> x2, other arithmetic: none -> 2.84 us  [the longest x1 1.5 us: edge_rows(): beside = exchanged(jnp.where(even, last, first), 0)]
  transfers between devices with their start and end apart: 5 -> 5, of which waited for: 4 -> 4; matrix products, arithmetic and copies ran while one was open for 11% -> 12% of each run, Pallas kernels for 20% -> 20%
where the time goes in v7:
time: 201 us; the launch traced here: 200 us
  waiting for transfers between devices  104 us (52%)
  Pallas kernels  49.9 us (25%)
  starting transfers between devices  19.4 us (10%)
  other arithmetic  19 us (9%)
  local copies, waits for them, and re-layouts  6.61 us (3%)
    all_to_all x2, waiting for transfers between devices, exchange(): lax.all_to_all(values, PEERS, split_axis=0, concat_axis=0, tiled=True)  92 us
    pallas_call x1, Pallas kernels, atmosphere(): pl.pallas_call(functools.partial(atm_kernel, plan), name='atmosphere', gr...  20.8 us
    convert_element_type x1, other arithmetic, local(): mixing = flat_mixing(padded, conv_kernel, OX, cell_count).astype(BF16)  13.4 us
    all_to_all x2, starting transfers between devices, exchange(): lax.all_to_all(values, PEERS, split_axis=0, concat_axis=0, tiled=True)  12.6 us
    pallas_call x2, Pallas kernels, merged(): pl.pallas_call(functools.partial(merge_kernel, capacity), name='merge', g...  10.4 us
    pallas_call x1, Pallas kernels, ocean(): pl.pallas_call(ocean_kernel, name='ocean', grid=(cells // part,), in_spec...  10.3 us
    pallas_call x1, Pallas kernels, near_remap(): pl.pallas_call(functools.partial(near_kernel, plan), name='near_remap', g...  8.35 us
    ppermute x1, waiting for transfers between devices, local(): far_sum = lax.ppermute(far_sum, 'half', [(0, 1), (1, 0)])  6.52 us
  transfers between devices with their start and end apart: 5, of which 4 were waited for; matrix products, arithmetic and copies ran while one was open for 12% of the time, Pallas kernels for 20%

profile of v7, /device:TPU:14, one launch (start us, length us, event | category | flops | bytes accessed | tf_op | source)
XLA Modules:
  0.0 200.2 jit_solution(3686952120063256952)
XLA Ops:
  0.6 1.5 broadcast_select_fusion.2
  2.1 3.4 %collective-permute-start = (bf16[200,1440]{1,0:T(8,128)(2,1)S(1)}, bf16[200,1440]{1,0:T(8,128)(2,1)}, u32[]{:S(2)}, u32[]{:S(2)}) collective-permute-start(bf16[200,1440]{1,0:T(8,128)(2,1)S(1)} %get-tuple-element.21), channel_id=1, source_target_pairs={{1,2},{3,4},{5,6},{7,8},{9,10},{11,12},{13,14},{15,16},{17,18},{19... | collective-permute-start | bytes 1728008 | tf_op jit(solution)/shard_map/ppermute | solution.py:412
  5.6 0.5 collective-permute-start.1
  6.1 20.8 %atmosphere.1 = (bf16[1024,1024]{1,0:T(8,128)(2,1)}, bf16[1024,128]{1,0:T(8,128)(2,1)}, bf16[16,1040,128]{2,1,0:T(8,128)(2,1)}) custom-call(s32[1]{0:T(128)} %bitcast.half_ref, s32[128]{0:T(128)} %bitcast.22, s32[128]{0:T(128)} %source_ref.3, s32[128]{0:T(128)} %block_ref.3, bf16[1024,1024]{1,0:T(8,128)(2,1)} %x_ref.1, f32[1,1024]{1,0:T(1,128)} %bitcast.24, ...), custom_call_target="tpu_custom_call" | custom-call | tf_op jit(solution)/shard_map/atmosphere/pallas_call | solution.py:203
  26.9 0.0 copy-start.4
  27.0 0.0 copy-start.5
  27.0 0.0 copy-start.6
  27.0 0.0 collective-permute-done
  27.0 5.9 %collective-permute-done.1 = bf16[200,1440]{1,0:T(8,128)(2,1)} collective-permute-done((bf16[200,1440]{1,0:T(8,128)(2,1)S(1)}, bf16[200,1440]{1,0:T(8,128)(2,1)}, u32[]{:S(2)}, u32[]{:S(2)}) %collective-permute-start.1) | collective-permute-done | bytes 576032 | tf_op jit(solution)/shard_map/ppermute | solution.py:412
  32.8 5.7 %all-to-all-start = ((bf16[16,1040,128]{2,1,0:T(8,128)(2,1)}), bf16[16,1040,128]{2,1,0:T(8,128)(2,1)}, u32[]{:S(2)}, u32[]{:S(2)}) async-start(bf16[16,1040,128]{2,1,0:T(8,128)(2,1)} %get-tuple-element.13), calls=%async_computation | async-start | bytes 8519680 | tf_op jit(solution)/shard_map/all_to_all | solution.py:469
  38.5 0.0 copy-done.4
  38.6 0.0 copy-start
  38.6 8.3 %near_remap.1 = bf16[16,1040,128]{2,1,0:T(8,128)(2,1)} custom-call(s32[1]{0:T(128)} %bitcast.half_ref, s32[128]{0:T(128)S(1)} %bitcast.23, s32[128]{0:T(128)S(1)} %copy-done.5, s32[128]{0:T(128)S(1)} %copy-done.6, bf16[1024,128]{1,0:T(8,128)(2,1)} %get-tuple-element.14.surface_ref, bf16[128,128,128]{2,1,0:T(8,128)(2,1)} %weight_ref.3), custom_call_target="tpu_custom_call" | custom-call | tf_op jit(solution)/shard_map/near_remap/pallas_call | solution.py:279
  47.0 0.6 fusion.22
  47.6 1.3 broadcast_select_fusion
  49.0 5.6 %concatenate.3 = bf16[200,8640]{1,0:T(8,128)(2,1)} concatenate(bf16[200,1440]{1,0:T(8,128)(2,1)S(1)} %get-tuple-element.23, bf16[200,5760]{1,0:T(8,128)(2,1)S(1)} %copy-done, bf16[200,1440]{1,0:T(8,128)(2,1)S(1)} %get-tuple-element.22), dimensions={1} | concatenate | bytes 6912000 | tf_op jit(solution)/shard_map/concatenate | solution.py:481
  54.6 2.8 %convert_element_type.8 = f32[200,8640]{1,0:T(8,128)S(1)} convert(bf16[200,8640]{1,0:T(8,128)(2,1)} %concatenate.3) | non-fusion elementwise | flops 1728000 | bytes 10368000 | tf_op jit(solution)/shard_map/convert_element_type | solution.py:420
  57.4 13.4 %fusion.16.mix_ref = bf16[200,5760]{1,0:T(8,128)(2,1)} fusion(f32[200,8640]{1,0:T(8,128)S(1)} %convert_element_type.8, f32[200]{0:T(256)S(1)} %bitcast.32, f32[200]{0:T(256)S(1)} %bitcast.33, f32[200]{0:T(256)S(1)} %bitcast.26, f32[200]{0:T(256)S(1)} %bitcast.27, f32[200]{0:T(256)S(1)} %bitcast.28, f32[200]{0:T(256)S(1)} %bitcast.29, f32[200]{0:T(256)S(1)} %bitcast.30, ...), kind=kLoop, calls=%fused_computation.23 | loop fusion | flops 27648000 | bytes 41544704 | tf_op jit(solution)/shard_map/convert_element_type | solution.py:482
  70.8 22.6 %all-to-all-done.arrived_ref = bf16[16,1040,128]{2,1,0:T(8,128)(2,1)} async-done(((bf16[16,1040,128]{2,1,0:T(8,128)(2,1)}), bf16[16,1040,128]{2,1,0:T(8,128)(2,1)}, u32[]{:S(2)}, u32[]{:S(2)}) %all-to-all-start) | async-done | bytes 4259872 | tf_op jit(solution)/shard_map/all_to_all | solution.py:469
  93.4 6.9 %all-to-all-start.1 = ((bf16[16,1040,128]{2,1,0:T(8,128)(2,1)}), bf16[16,1040,128]{2,1,0:T(8,128)(2,1)}, u32[]{:S(2)}, u32[]{:S(2)}) async-start(bf16[16,1040,128]{2,1,0:T(8,128)(2,1)} %near_remap.1), calls=%async_computation.1 | async-start | bytes 8519680 | tf_op jit(solution)/shard_map/all_to_all | solution.py:469
  100.4 0.0 copy-start.18
  100.4 0.0 copy-start.8
  100.4 5.6 %merge.3 = bf16[45,128,128]{2,1,0:T(8,128)(2,1)} custom-call(bf16[16,1040,128]{2,1,0:T(8,128)(2,1)} %all-to-all-done.arrived_ref), custom_call_target="tpu_custom_call" | custom-call | tf_op jit(solution)/shard_map/merge/pallas_call | solution.py:333
  106.0 0.0 copy-start.2
  106.0 0.0 copy-start.3
  106.0 2.8 %collective-permute-start.2 = (bf16[45,128,128]{2,1,0:T(8,128)(2,1)}, bf16[45,128,128]{2,1,0:T(8,128)(2,1)}, u32[]{:S(2)}, u32[]{:S(2)}) collective-permute-start(bf16[45,128,128]{2,1,0:T(8,128)(2,1)} %merge.3), channel_id=1, source_target_pairs={{0,8},{8,0},{1,9},{9,1},{2,10},{10,2},{3,11},{11,3},{4,12},{12,4},... | collective-permute-start | bytes 4423688 | tf_op jit(solution)/shard_map/ppermute | solution.py:486
  108.9 0.2 copy.19
  109.1 0.1 copy.20.gain_ref
  109.2 69.3 %all-to-all-done.1.arrived_ref = bf16[16,1040,128]{2,1,0:T(8,128)(2,1)} async-done(((bf16[16,1040,128]{2,1,0:T(8,128)(2,1)}), bf16[16,1040,128]{2,1,0:T(8,128)(2,1)}, u32[]{:S(2)}, u32[]{:S(2)}) %all-to-all-start.1) | async-done | bytes 4259872 | tf_op jit(solution)/shard_map/all_to_all | solution.py:469
  178.6 4.8 %merge.2 = bf16[45,128,128]{2,1,0:T(8,128)(2,1)S(1)} custom-call(bf16[16,1040,128]{2,1,0:T(8,128)(2,1)} %all-to-all-done.1.arrived_ref), custom_call_target="tpu_custom_call" | custom-call | tf_op jit(solution)/shard_map/merge/pallas_call | solution.py:333
  183.4 6.5 %collective-permute-done.2 = bf16[45,128,128]{2,1,0:T(8,128)(2,1)} collective-permute-done((bf16[45,128,128]{2,1,0:T(8,128)(2,1)}, bf16[45,128,128]{2,1,0:T(8,128)(2,1)}, u32[]{:S(2)}, u32[]{:S(2)}) %collective-permute-start.2) | collective-permute-done | bytes 1474592 | tf_op jit(solution)/shard_map/ppermute | solution.py:486
  189.9 10.3 %ocean.1 = bf16[200,5760]{1,0:T(8,128)(2,1)} custom-call(bf16[200,5760]{1,0:T(8,128)(2,1)S(1)} %copy-done.1, bf16[5760,128]{1,0:T(8,128)(2,1)S(1)} %bitcast.18, bf16[5760,128]{1,0:T(8,128)(2,1)} %bitcast.13.far_ref, bf16[200,5760]{1,0:T(8,128)(2,1)S(1)} %copy-done, s32[1,5760]{1,0:T(1,128)S(1)} %broadcast_in_dim.50.sea_ref, bf16[200,128]{1,0:T(8,128)(2,1)S(1)} %bitcast.21, ...), custom_call_target="tpu_custom_call" | custom-call | tf_op jit(solution)/shard_map/ocean/pallas_call | solution.py:374
  (31 shorter events, 0.1 us)
Async XLA Ops:
  2.1 24.8 %collective-permute-start = (bf16[200,1440]{1,0:T(8,128)(2,1)S(1)}, bf16[200,1440]{1,0:T(8,128)(2,1)}, u32[]{:S(2)}, u32[]{:S(2)}) collective-permute-start(bf16[200,1440]{1,0:T(8,128)(2,1)S(1)} %get-tuple-element.21), channel_id=1, source_target_pairs={{1,2},{3,4},{5,6},{7,8},{9,10},{11,12},{13,14},{15,16},{17,18},{19... | collective-permute-start | bytes 1728008 | tf_op jit(solution)/shard_map/ppermute | solution.py:412
  5.6 27.3 %collective-permute-start.1 = (bf16[200,1440]{1,0:T(8,128)(2,1)S(1)}, bf16[200,1440]{1,0:T(8,128)(2,1)}, u32[]{:S(2)}, u32[]{:S(2)}) collective-permute-start(bf16[200,1440]{1,0:T(8,128)(2,1)S(1)} %get-tuple-element.20), channel_id=1, source_target_pairs={{0,1},{2,3},{4,5},{6,7},{8,9},{10,11},{12,13},{14,15},{16,17},{18,... | collective-permute-start | bytes 1728008 | tf_op jit(solution)/shard_map/ppermute | solution.py:412
  26.9 11.6 %copy-start.4 = (s32[128,1]{0,1:T(1,128)S(1)}, s32[128,1]{0,1:T(1,128)}, u32[]{:S(2)}) copy-start(s32[128,1]{0,1:T(1,128)} %param.22) | copy-start | bytes 1540
  27.0 11.6 %copy-start.5 = (s32[128]{0:T(128)S(1)}, s32[128]{0:T(128)}, u32[]{:S(2)}) copy-start(s32[128]{0:T(128)} %source_ref.3) | copy-start | bytes 1540
  27.0 11.6 %copy-start.6 = (s32[128]{0:T(128)S(1)}, s32[128]{0:T(128)}, u32[]{:S(2)}) copy-start(s32[128]{0:T(128)} %block_ref.3) | copy-start | bytes 1540
  32.8 60.6 %all-to-all-start = ((bf16[16,1040,128]{2,1,0:T(8,128)(2,1)}), bf16[16,1040,128]{2,1,0:T(8,128)(2,1)}, u32[]{:S(2)}, u32[]{:S(2)}) async-start(bf16[16,1040,128]{2,1,0:T(8,128)(2,1)} %get-tuple-element.13), calls=%async_computation | async-start | bytes 8519680 | tf_op jit(solution)/shard_map/all_to_all | solution.py:469
  38.5 8.4 %copy-start.9 = (f32[200,9]{0,1:T(8,128)S(1)}, f32[200,9]{0,1:T(8,128)}, u32[]{:S(2)}) copy-start(f32[200,9]{0,1:T(8,128)} %param.27) | copy-start | bytes 21604
  38.6 10.4 %copy-start = (bf16[200,5760]{1,0:T(8,128)(2,1)S(1)}, bf16[200,5760]{1,0:T(8,128)(2,1)}, u32[]{:S(2)}) copy-start(bf16[200,5760]{1,0:T(8,128)(2,1)} %now_ref.1) | copy-start | bytes 6912004
  54.5 2.8 %copy-start.10 = (f32[200,1]{0,1:T(1,128)S(1)}, f32[200,1]{0,1:T(1,128)}, u32[]{:S(2)}) copy-start(f32[200,1]{0,1:T(1,128)} %get-tuple-element.25) | copy-start | bytes 2404
  54.5 2.8 %copy-start.11 = (f32[200,1]{0,1:T(1,128)S(1)}, f32[200,1]{0,1:T(1,128)}, u32[]{:S(2)}) copy-start(f32[200,1]{0,1:T(1,128)} %get-tuple-element.26) | copy-start | bytes 2404
  54.5 2.9 %copy-start.12 = (f32[200,1]{0,1:T(1,128)S(1)}, f32[200,1]{0,1:T(1,128)}, u32[]{:S(2)}) copy-start(f32[200,1]{0,1:T(1,128)} %get-tuple-element.27) | copy-start | bytes 2404
  54.5 2.9 %copy-start.13 = (f32[200,1]{0,1:T(1,128)S(1)}, f32[200,1]{0,1:T(1,128)}, u32[]{:S(2)}) copy-start(f32[200,1]{0,1:T(1,128)} %get-tuple-element.28) | copy-start | bytes 2404
  54.5 2.9 %copy-start.14 = (f32[200,1]{0,1:T(1,128)S(1)}, f32[200,1]{0,1:T(1,128)}, u32[]{:S(2)}) copy-start(f32[200,1]{0,1:T(1,128)} %get-tuple-element.29) | copy-start | bytes 2404
  54.6 2.9 %copy-start.15 = (f32[200,1]{0,1:T(1,128)S(1)}, f32[200,1]{0,1:T(1,128)}, u32[]{:S(2)}) copy-start(f32[200,1]{0,1:T(1,128)} %get-tuple-element.30) | copy-start | bytes 2404
  54.6 2.9 %copy-start.16 = (f32[200,1]{0,1:T(1,128)S(1)}, f32[200,1]{0,1:T(1,128)}, u32[]{:S(2)}) copy-start(f32[200,1]{0,1:T(1,128)} %get-tuple-element.31) | copy-start | bytes 2404
  54.6 2.9 %copy-start.17 = (f32[200,1]{0,1:T(1,128)S(1)}, f32[200,1]{0,1:T(1,128)}, u32[]{:S(2)}) copy-start(f32[200,1]{0,1:T(1,128)} %get-tuple-element.32) | copy-start | bytes 2404
  93.4 85.2 %all-to-all-start.1 = ((bf16[16,1040,128]{2,1,0:T(8,128)(2,1)}), bf16[16,1040,128]{2,1,0:T(8,128)(2,1)}, u32[]{:S(2)}, u32[]{:S(2)}) async-start(bf16[16,1040,128]{2,1,0:T(8,128)(2,1)} %near_remap.1), calls=%async_computation.1 | async-start | bytes 8519680 | tf_op jit(solution)/shard_map/all_to_all | solution.py:469
  100.4 8.5 %copy-start.7 = (bf16[200,800]{1,0:T(8,128)(2,1)S(1)}, bf16[200,800]{1,0:T(8,128)(2,1)}, u32[]{:S(2)}) copy-start(bf16[200,800]{1,0:T(8,128)(2,1)} %param.30) | copy-start | bytes 960004
  100.4 8.7 %copy-start.18 = (f32[200]{0:T(256)S(1)}, f32[200]{0:T(256)}, u32[]{:S(2)}) copy-start(f32[200]{0:T(256)} %param.29) | copy-start | bytes 2404
  100.4 8.8 %copy-start.8 = (s32[5760]{0:T(1024)S(1)}, s32[5760]{0:T(1024)}, u32[]{:S(2)}) copy-start(s32[5760]{0:T(1024)} %param.26) | copy-start | bytes 69124
  106.0 83.9 %copy-start.2 = (bf16[800,200]{0,1:T(8,128)(2,1)S(1)}, bf16[800,200]{0,1:T(8,128)(2,1)}, u32[]{:S(2)}) copy-start(bf16[800,200]{0,1:T(8,128)(2,1)} %param.31) | copy-start | bytes 960004
  106.0 83.9 %copy-start.3 = (bf16[128,200]{0,1:T(8,128)(2,1)S(1)}, bf16[128,200]{0,1:T(8,128)(2,1)}, u32[]{:S(2)}) copy-start(bf16[128,200]{0,1:T(8,128)(2,1)} %param.28) | copy-start | bytes 153604
  106.0 83.9 %collective-permute-start.2 = (bf16[45,128,128]{2,1,0:T(8,128)(2,1)}, bf16[45,128,128]{2,1,0:T(8,128)(2,1)}, u32[]{:S(2)}, u32[]{:S(2)}) collective-permute-start(bf16[45,128,128]{2,1,0:T(8,128)(2,1)} %merge.3), channel_id=1, source_target_pairs={{0,8},{8,0},{1,9},{9,1},{2,10},{10,2},{3,11},{11,3},{4,12},{12,4},... | collective-permute-start | bytes 4423688 | tf_op jit(solution)/shard_map/ppermute | solution.py:486
  178.6 11.3 %copy-start.1 = (bf16[200,5760]{1,0:T(8,128)(2,1)S(1)}, bf16[200,5760]{1,0:T(8,128)(2,1)}, u32[]{:S(2)}) copy-start(bf16[200,5760]{1,0:T(8,128)(2,1)} %fusion.16.mix_ref) | copy-start | bytes 6912004

commit v8 on v6

--- a/solution.py
+++ b/solution.py
@@ -396,19 +396,21 @@
         in_vmem(now),
         in_vmem(sea[None, :]),
         in_vmem(w_force),
-        in_vmem(gain[:, None]),
+        in_vmem(gain),
         in_vmem(w_up),
         in_vmem(w_down),
     )
 
 
-def edge_rows(block):
+def exchanged(row, start):
     count = math.prod(lax.axis_size(axis) for axis in ALL)
-    forward = [(i, i + 1) for i in range(count - 1)]
-    backward = [(target, source) for source, target in forward]
-    low = lax.ppermute(block[:, -OX:], ALL, forward)
-    high = lax.ppermute(block[:, :OX], ALL, backward)
-    return low, high
+    pairs = [(i, i + 1) for i in range(start, count - 1, 2)]
+    return lax.ppermute(row, ALL, pairs + [(upper, lower) for lower, upper in pairs])
+
+
+def row_mixing(row, taps):
+    row = row.astype(F32)
+    return sum(taps[:, step : step + 1] * jnp.roll(row, 1 - step, axis=1) for step in range(3))
 
 
 def flat_mixing(padded_flat, kernel, row_len, cell_count):
@@ -468,16 +470,34 @@
     atm_next, surface, far_made = atmosphere(
         plan, *entry, atm_state, gain_atm, w_up_atm, w_down_atm, w_flux, remap_weights
     )
-    low, high = edge_rows(ocean_state)
-    far_made, low, high = lax.optimization_barrier((far_made, low, high))
+    even = (lax.axis_index(ALL) & 1) == 0
+    first, last = ocean_state[:, :OX], ocean_state[:, -OX:]
+    across = exchanged(jnp.where(even, first, last), 1)
+    far_made, across = lax.optimization_barrier((far_made, across))
     far_arrived = exchange(far_made)
     near_made = near_remap(plan, *entry, surface, remap_weights)
+    none = jnp.zeros_like(across)
+    low, high = jnp.where(even, across, none), jnp.where(even, none, across)
     padded = jnp.concatenate([low, ocean_state, high], axis=1)
-    mixing = flat_mixing(padded, conv_kernel, OX, cell_count).astype(BF16)
-    far_arrived, near_made, mixing = lax.optimization_barrier((far_arrived, near_made, mixing))
+    mixing = flat_mixing(padded, conv_kernel, OX, cell_count)
+    beside = jnp.where(even, last, first)
+    taps = jnp.where(even, conv_kernel[:, 6:9], conv_kernel[:, 0:3])
+    ocean_weights = (w_force.T, gain_ocn[:, None], w_up_ocn.T, w_down_ocn.T)
+    far_arrived, near_made, mixing, beside, taps, ocean_weights = lax.optimization_barrier(
+        (far_arrived, near_made, mixing, beside, taps, ocean_weights)
+    )
     near_arrived = exchange(near_made)
+    beside = exchanged(beside, 0)
     far_sum = merged(capacity, far_arrived, ocean_blocks, block_rows)
     far_sum = lax.ppermute(far_sum, "half", [(0, 1), (1, 0)])
+    added = row_mixing(beside, taps)
+    rest = cell_count - OX
+    mixing = (
+        mixing
+        + jnp.pad(jnp.where(even, 0.0, added), ((0, 0), (0, rest)))
+        + jnp.pad(jnp.where(even, added, 0.0), ((0, 0), (rest, 0)))
+    ).astype(BF16)
+    near_arrived, mixing = lax.optimization_barrier((near_arrived, mixing))
     near_sum = merged(capacity, near_arrived, ocean_blocks, block_rows)
     features = far_sum.shape[2]
     ocean_next = ocean(
@@ -486,10 +506,7 @@
         far_sum.reshape(cell_count, features),
         ocean_state,
         land_sea,
-        w_force.T,
-        gain_ocn,
-        w_up_ocn.T,
-        w_down_ocn.T,
+        *ocean_weights,
     )
     return (atm_next, ocean_next)
 

time: 201 us -> 197 us (0.980)
  waiting for transfers between devices: 103 us -> 92 us
  other arithmetic: 16.1 us -> 23.3 us
  local copies, waits for them, and re-layouts: 8.09 us -> 10.8 us
  starting transfers between devices: 22.4 us -> 19.7 us
    all_to_all x2, waiting for transfers between devices: 93.3 us -> 26.5 us  [exchange(): lax.all_to_all(values, PEERS, split_axis=0, concat_axis=0, tiled=True)]
    ppermute x2, waiting for transfers between devices: 2.8 us -> 59 us  [exchanged(): lax.ppermute(row, ALL, pairs + [(upper, lower) for lower, upper in pairs])]
    add x0 -> x1, other arithmetic: none -> 13.4 us  [flat_mixing(): summed = summed + kernel[:, 3 * row_step + col_step][:, None] * shifted]
    convert_element_type x1, other arithmetic: 13.3 us -> 2 us  [local(): mixing = (mixing + jnp.pad(jnp.where(even, 0.0, added), ((0, 0), (0, rest...]
    select_n x0 -> x5, other arithmetic: none -> 5.13 us  [the longest x1 2.32 us: local(): beside = jnp.where(even, last, first)]
  transfers between devices with their start and end apart: 5 -> 5, of which waited for: 4 -> 4; matrix products, arithmetic and copies ran while one was open for 11% -> 16% of each run, Pallas kernels for 20% -> 20%
where the time goes in v8:
time: 197 us; the launch traced here: 196 us
  waiting for transfers between devices  92 us (47%)
  Pallas kernels  49.3 us (25%)
  other arithmetic  23.3 us (12%)
  starting transfers between devices  19.7 us (10%)
  local copies, waits for them, and re-layouts  10.8 us (5%)
    ppermute x2, waiting for transfers between devices, exchanged(): lax.ppermute(row, ALL, pairs + [(upper, lower) for lower, upper in pairs])  59 us
    all_to_all x2, waiting for transfers between devices, exchange(): lax.all_to_all(values, PEERS, split_axis=0, concat_axis=0, tiled=True)  26.5 us
    pallas_call x1, Pallas kernels, atmosphere(): pl.pallas_call(functools.partial(atm_kernel, plan), name='atmosphere', gr...  20.8 us
    add x1, other arithmetic, flat_mixing(): summed = summed + kernel[:, 3 * row_step + col_step][:, None] * shifted  13.4 us
    all_to_all x2, starting transfers between devices, exchange(): lax.all_to_all(values, PEERS, split_axis=0, concat_axis=0, tiled=True)  13 us
    pallas_call x1, Pallas kernels, ocean(): pl.pallas_call(ocean_kernel, name='ocean', grid=(cells // part,), in_spec...  10.4 us
    pallas_call x2, Pallas kernels, merged(): pl.pallas_call(functools.partial(merge_kernel, capacity), name='merge', g...  10.3 us
    pallas_call x1, Pallas kernels, near_remap(): pl.pallas_call(functools.partial(near_kernel, plan), name='near_remap', g...  7.82 us
  transfers between devices with their start and end apart: 5, of which 4 were waited for; matrix products, arithmetic and copies ran while one was open for 16% of the time, Pallas kernels for 20%

profile of v8, /device:TPU:14, one launch (start us, length us, event | category | flops | bytes accessed | tf_op | source)
XLA Modules:
  0.0 196.0 jit_solution(13275820286010136345)
XLA Ops:
  0.6 2.3 %broadcast_select_fusion.2 = (bf16[200,1440]{1,0:T(8,128)(2,1)}, bf16[200,1440]{1,0:T(8,128)(2,1)S(1)}) fusion(pred[]{:T(512)S(6)} %eq.33, bf16[200,5760]{1,0:T(8,128)(2,1)} %now_ref.1), kind=kLoop, calls=%fused_computation.30 | loop fusion | flops 576000 | bytes 2304001 | tf_op jit(solution)/shard_map/jit(_where)/select_n | solution.py:483
  3.0 3.4 %collective-permute-start = (bf16[200,1440]{1,0:T(8,128)(2,1)S(1)}, bf16[200,1440]{1,0:T(8,128)(2,1)S(1)}, u32[]{:S(2)}, u32[]{:S(2)}) collective-permute-start(bf16[200,1440]{1,0:T(8,128)(2,1)S(1)} %get-tuple-element.37), channel_id=1, source_target_pairs={{1,2},{3,4},{5,6},{7,8},{9,10},{11,12},{13,14},{15,16},{17,18},{19... | collective-permute-start | bytes 1728008 | tf_op jit(solution)/shard_map/ppermute | solution.py:408
  6.4 20.8 %atmosphere.1 = (bf16[1024,1024]{1,0:T(8,128)(2,1)}, bf16[1024,128]{1,0:T(8,128)(2,1)}, bf16[16,1040,128]{2,1,0:T(8,128)(2,1)}) custom-call(s32[1]{0:T(128)} %bitcast.half_ref, s32[128]{0:T(128)} %bitcast.25, s32[128]{0:T(128)} %source_ref.3, s32[128]{0:T(128)} %block_ref.3, bf16[1024,1024]{1,0:T(8,128)(2,1)} %x_ref.1, f32[1,1024]{1,0:T(1,128)} %bitcast.38, ...), custom_call_target="tpu_custom_call" | custom-call | tf_op jit(solution)/shard_map/atmosphere/pallas_call | solution.py:203
  27.2 0.0 copy-start.10
  27.2 0.0 collective-permute-done
  27.2 0.8 copy-done.8
  28.0 6.1 %all-to-all-start = ((bf16[16,1040,128]{2,1,0:T(8,128)(2,1)}), bf16[16,1040,128]{2,1,0:T(8,128)(2,1)}, u32[]{:S(2)}, u32[]{:S(2)}) async-start(bf16[16,1040,128]{2,1,0:T(8,128)(2,1)} %get-tuple-element.20), calls=%async_computation | async-start | bytes 8519680 | tf_op jit(solution)/shard_map/all_to_all | solution.py:466
  34.1 0.0 copy-start.12
  34.2 0.2 copy.19
  34.4 0.0 copy-start
  34.4 7.8 %near_remap.1 = bf16[16,1040,128]{2,1,0:T(8,128)(2,1)} custom-call(s32[1]{0:T(128)} %bitcast.half_ref, s32[128]{0:T(128)S(1)} %bitcast.26, s32[128]{0:T(128)S(1)} %copy-done.5, s32[128]{0:T(128)S(1)} %copy-done.6, bf16[1024,128]{1,0:T(8,128)(2,1)} %get-tuple-element.21.surface_ref, bf16[128,128,128]{2,1,0:T(8,128)(2,1)} %weight_ref.3), custom_call_target="tpu_custom_call" | custom-call | tf_op jit(solution)/shard_map/near_remap/pallas_call | solution.py:279
  42.3 0.9 broadcast_select_fusion.3
  43.2 6.9 %concatenate.11 = bf16[200,8640]{1,0:T(8,128)(2,1)} concatenate(bf16[200,1440]{1,0:T(8,128)(2,1)} %get-tuple-element.43, bf16[200,5760]{1,0:T(8,128)(2,1)S(1)} %copy-done, bf16[200,1440]{1,0:T(8,128)(2,1)S(1)} %get-tuple-element.42), dimensions={1} | concatenate | bytes 6912000 | tf_op jit(solution)/shard_map/concatenate | solution.py:481
  50.1 2.8 %convert_element_type.15 = f32[200,8640]{1,0:T(8,128)S(1)} convert(bf16[200,8640]{1,0:T(8,128)(2,1)} %concatenate.11) | non-fusion elementwise | flops 1728000 | bytes 10368000 | tf_op jit(solution)/shard_map/convert_element_type | solution.py:417
  52.9 13.4 %fusion.9 = f32[200,5760]{1,0:T(8,128)} fusion(f32[200,8640]{1,0:T(8,128)S(1)} %convert_element_type.15, f32[200]{0:T(256)S(1)} %bitcast.37, f32[200]{0:T(256)S(1)} %bitcast.30, f32[200]{0:T(256)S(1)} %bitcast.31, f32[200]{0:T(256)S(1)} %bitcast.32, f32[200]{0:T(256)S(1)} %bitcast.33, f32[200]{0:T(256)S(1)} %bitcast.34, f32[200]{0:T(256)S(1)} %bitcast.35, ...), kind=kLoop, calls=%fused_computation.13 | loop fusion | flops 26496000 | bytes 43848704 | tf_op jit(solution)/shard_map/add | solution.py:435
  66.3 22.7 %all-to-all-done.arrived_ref = bf16[16,1040,128]{2,1,0:T(8,128)(2,1)} async-done(((bf16[16,1040,128]{2,1,0:T(8,128)(2,1)}), bf16[16,1040,128]{2,1,0:T(8,128)(2,1)}, u32[]{:S(2)}, u32[]{:S(2)}) %all-to-all-start) | async-done | bytes 4259872 | tf_op jit(solution)/shard_map/all_to_all | solution.py:466
  89.0 6.9 %all-to-all-start.1 = ((bf16[16,1040,128]{2,1,0:T(8,128)(2,1)}), bf16[16,1040,128]{2,1,0:T(8,128)(2,1)}, u32[]{:S(2)}, u32[]{:S(2)}) async-start(bf16[16,1040,128]{2,1,0:T(8,128)(2,1)} %near_remap.1), calls=%async_computation.1 | async-start | bytes 8519680 | tf_op jit(solution)/shard_map/all_to_all | solution.py:466
  95.9 0.6 collective-permute-start.1
  96.6 0.1 copy.20.gain_ref
  96.7 5.8 %merge.3 = bf16[45,128,128]{2,1,0:T(8,128)(2,1)} custom-call(bf16[16,1040,128]{2,1,0:T(8,128)(2,1)} %all-to-all-done.arrived_ref), custom_call_target="tpu_custom_call" | custom-call | tf_op jit(solution)/shard_map/merge/pallas_call | solution.py:333
  102.5 2.7 %collective-permute-start.2 = (bf16[45,128,128]{2,1,0:T(8,128)(2,1)}, bf16[45,128,128]{2,1,0:T(8,128)(2,1)}, u32[]{:S(2)}, u32[]{:S(2)}) collective-permute-start(bf16[45,128,128]{2,1,0:T(8,128)(2,1)} %merge.3), channel_id=1, source_target_pairs={{0,8},{8,0},{1,9},{9,1},{2,10},{10,2},{3,11},{11,3},{4,12},{12,4},... | collective-permute-start | bytes 4423688 | tf_op jit(solution)/shard_map/ppermute | solution.py:492
  105.2 59.0 %collective-permute-done.1 = bf16[200,1440]{1,0:T(8,128)(2,1)} collective-permute-done((bf16[200,1440]{1,0:T(8,128)(2,1)S(1)}, bf16[200,1440]{1,0:T(8,128)(2,1)}, u32[]{:S(2)}, u32[]{:S(2)}) %collective-permute-start.1) | collective-permute-done | bytes 576032 | tf_op jit(solution)/shard_map/ppermute | solution.py:408
  164.1 0.9 fusion.24
  165.0 0.0 slice-start
  165.1 1.7 fusion.25
  166.8 1.8 broadcast_select_fusion.1
  168.6 0.1 broadcast_select_fusion
  168.8 2.0 %add_convert_fusion.mix_ref = bf16[200,5760]{1,0:T(8,128)(2,1)} fusion(f32[200,1440]{1,0:T(8,128)S(1)} %broadcast_select_fusion, f32[200,5760]{1,0:T(8,128)S(1)} %bitcast.28, f32[200,1440]{1,0:T(8,128)S(1)} %get-tuple-element.34), kind=kLoop, calls=%fused_computation.23 | loop fusion | flops 3456000 | bytes 9216000 | tf_op jit(solution)/shard_map/convert_element_type | solution.py:499
  170.8 3.8 %all-to-all-done.1.arrived_ref = bf16[16,1040,128]{2,1,0:T(8,128)(2,1)} async-done(((bf16[16,1040,128]{2,1,0:T(8,128)(2,1)}), bf16[16,1040,128]{2,1,0:T(8,128)(2,1)}, u32[]{:S(2)}, u32[]{:S(2)}) %all-to-all-start.1) | async-done | bytes 4259872 | tf_op jit(solution)/shard_map/all_to_all | solution.py:466
  174.5 4.5 %merge.2 = bf16[45,128,128]{2,1,0:T(8,128)(2,1)S(1)} custom-call(bf16[16,1040,128]{2,1,0:T(8,128)(2,1)} %all-to-all-done.1.arrived_ref), custom_call_target="tpu_custom_call" | custom-call | tf_op jit(solution)/shard_map/merge/pallas_call | solution.py:333
  179.1 6.6 %collective-permute-done.2 = bf16[45,128,128]{2,1,0:T(8,128)(2,1)} collective-permute-done((bf16[45,128,128]{2,1,0:T(8,128)(2,1)}, bf16[45,128,128]{2,1,0:T(8,128)(2,1)}, u32[]{:S(2)}, u32[]{:S(2)}) %collective-permute-start.2) | collective-permute-done | bytes 1474592 | tf_op jit(solution)/shard_map/ppermute | solution.py:492
  185.7 10.4 %ocean.1 = bf16[200,5760]{1,0:T(8,128)(2,1)} custom-call(bf16[200,5760]{1,0:T(8,128)(2,1)S(1)} %copy-done.1, bf16[5760,128]{1,0:T(8,128)(2,1)S(1)} %bitcast.21, bf16[5760,128]{1,0:T(8,128)(2,1)} %bitcast.20.far_ref, bf16[200,5760]{1,0:T(8,128)(2,1)S(1)} %copy-done, s32[1,5760]{1,0:T(1,128)S(1)} %broadcast_in_dim.62.sea_ref, bf16[200,128]{1,0:T(8,128)(2,1)S(1)} %bitcast.24, ...), custom_call_target="tpu_custom_call" | custom-call | tf_op jit(solution)/shard_map/ocean/pallas_call | solution.py:374
  (33 shorter events, 0.1 us)
Async XLA Ops:
  3.0 24.2 %collective-permute-start = (bf16[200,1440]{1,0:T(8,128)(2,1)S(1)}, bf16[200,1440]{1,0:T(8,128)(2,1)S(1)}, u32[]{:S(2)}, u32[]{:S(2)}) collective-permute-start(bf16[200,1440]{1,0:T(8,128)(2,1)S(1)} %get-tuple-element.37), channel_id=1, source_target_pairs={{1,2},{3,4},{5,6},{7,8},{9,10},{11,12},{13,14},{15,16},{17,18},{19... | collective-permute-start | bytes 1728008 | tf_op jit(solution)/shard_map/ppermute | solution.py:408
  27.2 7.0 %copy-start.10 = (bf16[200,800]{1,0:T(8,128)(2,1)S(1)}, bf16[200,800]{1,0:T(8,128)(2,1)}, u32[]{:S(2)}) copy-start(bf16[200,800]{1,0:T(8,128)(2,1)} %param.30) | copy-start | bytes 960004
  27.2 0.8 copy-start.8
  28.0 6.4 %copy-start.4 = (s32[128,1]{0,1:T(1,128)S(1)}, s32[128,1]{0,1:T(1,128)}, u32[]{:S(2)}) copy-start(s32[128,1]{0,1:T(1,128)} %param.22) | copy-start | bytes 1540
  28.0 6.4 %copy-start.5 = (s32[128]{0:T(128)S(1)}, s32[128]{0:T(128)}, u32[]{:S(2)}) copy-start(s32[128]{0:T(128)} %source_ref.3) | copy-start | bytes 1540
  28.0 6.4 %copy-start.6 = (s32[128]{0:T(128)S(1)}, s32[128]{0:T(128)}, u32[]{:S(2)}) copy-start(s32[128]{0:T(128)} %block_ref.3) | copy-start | bytes 1540
  28.0 61.0 %all-to-all-start = ((bf16[16,1040,128]{2,1,0:T(8,128)(2,1)}), bf16[16,1040,128]{2,1,0:T(8,128)(2,1)}, u32[]{:S(2)}, u32[]{:S(2)}) async-start(bf16[16,1040,128]{2,1,0:T(8,128)(2,1)} %get-tuple-element.20), calls=%async_computation | async-start | bytes 8519680 | tf_op jit(solution)/shard_map/all_to_all | solution.py:466
  34.1 8.1 %copy-start.12 = (f32[200,9]{0,1:T(8,128)S(1)}, f32[200,9]{0,1:T(8,128)}, u32[]{:S(2)}) copy-start(f32[200,9]{0,1:T(8,128)} %param.27) | copy-start | bytes 21604
  34.4 8.0 %copy-start.9 = (bf16[200,1440]{1,0:T(8,128)(2,1)S(1)}, bf16[200,1440]{1,0:T(8,128)(2,1)}, u32[]{:S(2)}) copy-start(bf16[200,1440]{1,0:T(8,128)(2,1)} %copy-done.8) | copy-start | bytes 1728004
  34.4 8.8 %copy-start = (bf16[200,5760]{1,0:T(8,128)(2,1)S(1)}, bf16[200,5760]{1,0:T(8,128)(2,1)}, u32[]{:S(2)}) copy-start(bf16[200,5760]{1,0:T(8,128)(2,1)} %now_ref.1) | copy-start | bytes 6912004
  66.3 29.6 %copy-start.7 = (bf16[200,1440]{1,0:T(8,128)(2,1)S(1)}, bf16[200,1440]{1,0:T(8,128)(2,1)}, u32[]{:S(2)}) copy-start(bf16[200,1440]{1,0:T(8,128)(2,1)} %get-tuple-element.26) | copy-start | bytes 1728004
  66.3 30.2 %copy-start.11 = (s32[5760]{0:T(1024)S(1)}, s32[5760]{0:T(1024)}, u32[]{:S(2)}) copy-start(s32[5760]{0:T(1024)} %param.26) | copy-start | bytes 69124
  66.3 30.2 %copy-start.13 = (f32[200]{0:T(256)S(1)}, f32[200]{0:T(256)}, u32[]{:S(2)}) copy-start(f32[200]{0:T(256)} %param.29) | copy-start | bytes 2404
  89.0 85.5 %all-to-all-start.1 = ((bf16[16,1040,128]{2,1,0:T(8,128)(2,1)}), bf16[16,1040,128]{2,1,0:T(8,128)(2,1)}, u32[]{:S(2)}, u32[]{:S(2)}) async-start(bf16[16,1040,128]{2,1,0:T(8,128)(2,1)} %near_remap.1), calls=%async_computation.1 | async-start | bytes 8519680 | tf_op jit(solution)/shard_map/all_to_all | solution.py:466
  95.9 68.2 %collective-permute-start.1 = (bf16[200,1440]{1,0:T(8,128)(2,1)S(1)}, bf16[200,1440]{1,0:T(8,128)(2,1)}, u32[]{:S(2)}, u32[]{:S(2)}) collective-permute-start(bf16[200,1440]{1,0:T(8,128)(2,1)S(1)} %copy-done.7), channel_id=1, source_target_pairs={{0,1},{2,3},{4,5},{6,7},{8,9},{10,11},{12,13},{14,15},{16,17},{18,... | collective-permute-start | bytes 1728008 | tf_op jit(solution)/shard_map/ppermute | solution.py:408
  102.5 83.2 %collective-permute-start.2 = (bf16[45,128,128]{2,1,0:T(8,128)(2,1)}, bf16[45,128,128]{2,1,0:T(8,128)(2,1)}, u32[]{:S(2)}, u32[]{:S(2)}) collective-permute-start(bf16[45,128,128]{2,1,0:T(8,128)(2,1)} %merge.3), channel_id=1, source_target_pairs={{0,8},{8,0},{1,9},{9,1},{2,10},{10,2},{3,11},{11,3},{4,12},{12,4},... | collective-permute-start | bytes 4423688 | tf_op jit(solution)/shard_map/ppermute | solution.py:492
  165.0 3.7 %slice-start = ((s8[4608000]{0:T(1024)(128)(4,1)}), s8[4194304]{0:T(1024)(128)(4,1)S(1)}, s32[]{:S(2)}) async-start(s8[4608000]{0:T(1024)(128)(4,1)} %bitcast.27), calls=%async_computation.2 | async-start | bytes 8388608
  166.8 1.9 slice-start.1
  170.7 14.9 %copy-start.2 = (bf16[800,200]{0,1:T(8,128)(2,1)S(1)}, bf16[800,200]{0,1:T(8,128)(2,1)}, u32[]{:S(2)}) copy-start(bf16[800,200]{0,1:T(8,128)(2,1)} %param.31) | copy-start | bytes 960004
  170.8 14.9 %copy-start.3 = (bf16[128,200]{0,1:T(8,128)(2,1)S(1)}, bf16[128,200]{0,1:T(8,128)(2,1)}, u32[]{:S(2)}) copy-start(bf16[128,200]{0,1:T(8,128)(2,1)} %param.28) | copy-start | bytes 153604
  174.5 11.1 %copy-start.1 = (bf16[200,5760]{1,0:T(8,128)(2,1)S(1)}, bf16[200,5760]{1,0:T(8,128)(2,1)}, u32[]{:S(2)}) copy-start(bf16[200,5760]{1,0:T(8,128)(2,1)} %add_convert_fusion.mix_ref) | copy-start | bytes 6912004

commit v9 on v8

--- a/solution.py
+++ b/solution.py
@@ -473,14 +473,14 @@
     even = (lax.axis_index(ALL) & 1) == 0
     first, last = ocean_state[:, :OX], ocean_state[:, -OX:]
     across = exchanged(jnp.where(even, first, last), 1)
-    far_made, across = lax.optimization_barrier((far_made, across))
+    far_made, across, later_state = lax.optimization_barrier((far_made, across, ocean_state))
     far_arrived = exchange(far_made)
     near_made = near_remap(plan, *entry, surface, remap_weights)
     none = jnp.zeros_like(across)
     low, high = jnp.where(even, across, none), jnp.where(even, none, across)
     padded = jnp.concatenate([low, ocean_state, high], axis=1)
     mixing = flat_mixing(padded, conv_kernel, OX, cell_count)
-    beside = jnp.where(even, last, first)
+    beside = jnp.where(even, later_state[:, -OX:], later_state[:, :OX])
     taps = jnp.where(even, conv_kernel[:, 6:9], conv_kernel[:, 0:3])
     ocean_weights = (w_force.T, gain_ocn[:, None], w_up_ocn.T, w_down_ocn.T)
     far_arrived, near_made, mixing, beside, taps, ocean_weights = lax.optimization_barrier(

time: 197 us -> 196 us (level)
  no operation moved by 1% of the time
where the time goes in v9:
time: 196 us; the launch traced here: 195 us
  waiting for transfers between devices  91.3 us (47%)
  Pallas kernels  49.8 us (25%)
  other arithmetic  22.9 us (12%)
  starting transfers between devices  19.1 us (10%)
  local copies, waits for them, and re-layouts  10.8 us (6%)
    ppermute x2, waiting for transfers between devices, exchanged(): lax.ppermute(row, ALL, pairs + [(upper, lower) for lower, upper in pairs])  59.5 us
    all_to_all x2, waiting for transfers between devices, exchange(): lax.all_to_all(values, PEERS, split_axis=0, concat_axis=0, tiled=True)  25.9 us
    pallas_call x1, Pallas kernels, atmosphere(): pl.pallas_call(functools.partial(atm_kernel, plan), name='atmosphere', gr...  21.3 us
    add x1, other arithmetic, flat_mixing(): summed = summed + kernel[:, 3 * row_step + col_step][:, None] * shifted  13.4 us
    all_to_all x2, starting transfers between devices, exchange(): lax.all_to_all(values, PEERS, split_axis=0, concat_axis=0, tiled=True)  12.8 us
    pallas_call x1, Pallas kernels, ocean(): pl.pallas_call(ocean_kernel, name='ocean', grid=(cells // part,), in_spec...  10.4 us
    pallas_call x2, Pallas kernels, merged(): pl.pallas_call(functools.partial(merge_kernel, capacity), name='merge', g...  10.3 us
    pallas_call x1, Pallas kernels, near_remap(): pl.pallas_call(functools.partial(near_kernel, plan), name='near_remap', g...  7.82 us
  transfers between devices with their start and end apart: 5, of which 4 were waited for; matrix products, arithmetic and copies ran while one was open for 16% of the time, Pallas kernels for 20%

profile of v9, /device:TPU:14, one launch (start us, length us, event | category | flops | bytes accessed | tf_op | source)
XLA Modules:
  0.0 194.9 jit_solution(5110743684116599054)
XLA Ops:
  0.6 1.5 slice_select_fusion.1
  2.1 3.4 %collective-permute-start = (bf16[200,1440]{1,0:T(8,128)(2,1)S(1)}, bf16[200,1440]{1,0:T(8,128)(2,1)S(1)}, u32[]{:S(2)}, u32[]{:S(2)}) collective-permute-start(bf16[200,1440]{1,0:T(8,128)(2,1)S(1)} %slice_select_fusion.1), channel_id=1, source_target_pairs={{1,2},{3,4},{5,6},{7,8},{9,10},{11,12},{13,14},{15,16},{17,18},{19... | collective-permute-start | bytes 1728008 | tf_op jit(solution)/shard_map/ppermute | solution.py:408
  5.5 21.3 %atmosphere.1 = (bf16[1024,1024]{1,0:T(8,128)(2,1)}, bf16[1024,128]{1,0:T(8,128)(2,1)}, bf16[16,1040,128]{2,1,0:T(8,128)(2,1)}) custom-call(s32[1]{0:T(128)} %bitcast.half_ref, s32[128]{0:T(128)} %bitcast.25, s32[128]{0:T(128)} %source_ref.3, s32[128]{0:T(128)} %block_ref.3, bf16[1024,1024]{1,0:T(8,128)(2,1)} %x_ref.1, f32[1,1024]{1,0:T(1,128)} %bitcast.38, ...), custom_call_target="tpu_custom_call" | custom-call | tf_op jit(solution)/shard_map/atmosphere/pallas_call | solution.py:203
  26.9 0.0 copy-start.10
  26.9 0.0 copy-start.8
  26.9 0.8 copy-done.8
  27.7 5.9 %all-to-all-start = ((bf16[16,1040,128]{2,1,0:T(8,128)(2,1)}), bf16[16,1040,128]{2,1,0:T(8,128)(2,1)}, u32[]{:S(2)}, u32[]{:S(2)}) async-start(bf16[16,1040,128]{2,1,0:T(8,128)(2,1)} %get-tuple-element.21), calls=%async_computation | async-start | bytes 8519680 | tf_op jit(solution)/shard_map/all_to_all | solution.py:466
  33.6 0.0 copy-start.12
  33.6 0.0 copy-start
  33.7 0.2 copy.19
  33.9 0.0 copy-start.9
  33.9 7.8 %near_remap.1 = bf16[16,1040,128]{2,1,0:T(8,128)(2,1)} custom-call(s32[1]{0:T(128)} %bitcast.half_ref, s32[128]{0:T(128)S(1)} %bitcast.26, s32[128]{0:T(128)S(1)} %copy-done.5, s32[128]{0:T(128)S(1)} %copy-done.6, bf16[1024,128]{1,0:T(8,128)(2,1)} %get-tuple-element.22.surface_ref, bf16[128,128,128]{2,1,0:T(8,128)(2,1)} %weight_ref.3), custom_call_target="tpu_custom_call" | custom-call | tf_op jit(solution)/shard_map/near_remap/pallas_call | solution.py:279
  41.8 1.3 broadcast_select_fusion.2
  43.1 6.9 %concatenate.11 = bf16[200,8640]{1,0:T(8,128)(2,1)} concatenate(bf16[200,1440]{1,0:T(8,128)(2,1)} %get-tuple-element.43, bf16[200,5760]{1,0:T(8,128)(2,1)S(1)} %copy-done, bf16[200,1440]{1,0:T(8,128)(2,1)S(1)} %get-tuple-element.42), dimensions={1} | concatenate | bytes 6912000 | tf_op jit(solution)/shard_map/concatenate | solution.py:481
  50.0 2.8 %convert_element_type.15 = f32[200,8640]{1,0:T(8,128)S(1)} convert(bf16[200,8640]{1,0:T(8,128)(2,1)} %concatenate.11) | non-fusion elementwise | flops 1728000 | bytes 10368000 | tf_op jit(solution)/shard_map/convert_element_type | solution.py:417
  52.8 13.4 %fusion.9 = f32[200,5760]{1,0:T(8,128)} fusion(f32[200,8640]{1,0:T(8,128)S(1)} %convert_element_type.15, f32[200]{0:T(256)S(1)} %bitcast.37, f32[200]{0:T(256)S(1)} %bitcast.30, f32[200]{0:T(256)S(1)} %bitcast.31, f32[200]{0:T(256)S(1)} %bitcast.32, f32[200]{0:T(256)S(1)} %bitcast.33, f32[200]{0:T(256)S(1)} %bitcast.34, f32[200]{0:T(256)S(1)} %bitcast.35, ...), kind=kLoop, calls=%fused_computation.13 | loop fusion | flops 26496000 | bytes 43848704 | tf_op jit(solution)/shard_map/add | solution.py:435
  66.2 22.3 %all-to-all-done.arrived_ref = bf16[16,1040,128]{2,1,0:T(8,128)(2,1)} async-done(((bf16[16,1040,128]{2,1,0:T(8,128)(2,1)}), bf16[16,1040,128]{2,1,0:T(8,128)(2,1)}, u32[]{:S(2)}, u32[]{:S(2)}) %all-to-all-start) | async-done | bytes 4259872 | tf_op jit(solution)/shard_map/all_to_all | solution.py:466
  88.5 6.9 %all-to-all-start.1 = ((bf16[16,1040,128]{2,1,0:T(8,128)(2,1)}), bf16[16,1040,128]{2,1,0:T(8,128)(2,1)}, u32[]{:S(2)}, u32[]{:S(2)}) async-start(bf16[16,1040,128]{2,1,0:T(8,128)(2,1)} %near_remap.1), calls=%async_computation.1 | async-start | bytes 8519680 | tf_op jit(solution)/shard_map/all_to_all | solution.py:466
  95.4 0.6 collective-permute-start.1
  96.0 0.1 copy.20.gain_ref
  96.2 5.6 %merge.3 = bf16[45,128,128]{2,1,0:T(8,128)(2,1)} custom-call(bf16[16,1040,128]{2,1,0:T(8,128)(2,1)} %all-to-all-done.arrived_ref), custom_call_target="tpu_custom_call" | custom-call | tf_op jit(solution)/shard_map/merge/pallas_call | solution.py:333
  101.8 2.3 %collective-permute-start.2 = (bf16[45,128,128]{2,1,0:T(8,128)(2,1)}, bf16[45,128,128]{2,1,0:T(8,128)(2,1)}, u32[]{:S(2)}, u32[]{:S(2)}) collective-permute-start(bf16[45,128,128]{2,1,0:T(8,128)(2,1)} %merge.3), channel_id=1, source_target_pairs={{0,8},{8,0},{1,9},{9,1},{2,10},{10,2},{3,11},{11,3},{4,12},{12,4},... | collective-permute-start | bytes 4423688 | tf_op jit(solution)/shard_map/ppermute | solution.py:492
  104.1 59.5 %collective-permute-done.1 = bf16[200,1440]{1,0:T(8,128)(2,1)} collective-permute-done((bf16[200,1440]{1,0:T(8,128)(2,1)S(1)}, bf16[200,1440]{1,0:T(8,128)(2,1)}, u32[]{:S(2)}, u32[]{:S(2)}) %collective-permute-start.1) | collective-permute-done | bytes 576032 | tf_op jit(solution)/shard_map/ppermute | solution.py:408
  163.6 0.9 fusion.24
  164.5 1.7 fusion.25
  166.3 1.8 broadcast_select_fusion.1
  168.1 0.1 broadcast_select_fusion
  168.2 2.0 %add_convert_fusion.mix_ref = bf16[200,5760]{1,0:T(8,128)(2,1)} fusion(f32[200,1440]{1,0:T(8,128)S(1)} %broadcast_select_fusion, f32[200,5760]{1,0:T(8,128)S(1)} %bitcast.28, f32[200,1440]{1,0:T(8,128)S(1)} %get-tuple-element.36), kind=kLoop, calls=%fused_computation.23 | loop fusion | flops 3456000 | bytes 9216000 | tf_op jit(solution)/shard_map/convert_element_type | solution.py:499
  170.2 3.5 %all-to-all-done.1.arrived_ref = bf16[16,1040,128]{2,1,0:T(8,128)(2,1)} async-done(((bf16[16,1040,128]{2,1,0:T(8,128)(2,1)}), bf16[16,1040,128]{2,1,0:T(8,128)(2,1)}, u32[]{:S(2)}, u32[]{:S(2)}) %all-to-all-start.1) | async-done | bytes 4259872 | tf_op jit(solution)/shard_map/all_to_all | solution.py:466
  173.8 4.7 %merge.2 = bf16[45,128,128]{2,1,0:T(8,128)(2,1)S(1)} custom-call(bf16[16,1040,128]{2,1,0:T(8,128)(2,1)} %all-to-all-done.1.arrived_ref), custom_call_target="tpu_custom_call" | custom-call | tf_op jit(solution)/shard_map/merge/pallas_call | solution.py:333
  178.5 5.9 %collective-permute-done.2 = bf16[45,128,128]{2,1,0:T(8,128)(2,1)} collective-permute-done((bf16[45,128,128]{2,1,0:T(8,128)(2,1)}, bf16[45,128,128]{2,1,0:T(8,128)(2,1)}, u32[]{:S(2)}, u32[]{:S(2)}) %collective-permute-start.2) | collective-permute-done | bytes 1474592 | tf_op jit(solution)/shard_map/ppermute | solution.py:492
  184.4 10.4 %ocean.1 = bf16[200,5760]{1,0:T(8,128)(2,1)} custom-call(bf16[200,5760]{1,0:T(8,128)(2,1)S(1)} %copy-done.1, bf16[5760,128]{1,0:T(8,128)(2,1)S(1)} %bitcast.21, bf16[5760,128]{1,0:T(8,128)(2,1)} %bitcast.20.far_ref, bf16[200,5760]{1,0:T(8,128)(2,1)S(1)} %copy-done, s32[1,5760]{1,0:T(1,128)S(1)} %broadcast_in_dim.62.sea_ref, bf16[200,128]{1,0:T(8,128)(2,1)S(1)} %bitcast.24, ...), custom_call_target="tpu_custom_call" | custom-call | tf_op jit(solution)/shard_map/ocean/pallas_call | solution.py:374
  (33 shorter events, 0.1 us)
Async XLA Ops:
  2.1 24.7 %collective-permute-start = (bf16[200,1440]{1,0:T(8,128)(2,1)S(1)}, bf16[200,1440]{1,0:T(8,128)(2,1)S(1)}, u32[]{:S(2)}, u32[]{:S(2)}) collective-permute-start(bf16[200,1440]{1,0:T(8,128)(2,1)S(1)} %slice_select_fusion.1), channel_id=1, source_target_pairs={{1,2},{3,4},{5,6},{7,8},{9,10},{11,12},{13,14},{15,16},{17,18},{19... | collective-permute-start | bytes 1728008 | tf_op jit(solution)/shard_map/ppermute | solution.py:408
  26.9 6.8 %copy-start.10 = (bf16[200,800]{1,0:T(8,128)(2,1)S(1)}, bf16[200,800]{1,0:T(8,128)(2,1)}, u32[]{:S(2)}) copy-start(bf16[200,800]{1,0:T(8,128)(2,1)} %param.30) | copy-start | bytes 960004
  26.9 0.8 copy-start.8
  27.7 6.2 %copy-start.4 = (s32[128,1]{0,1:T(1,128)S(1)}, s32[128,1]{0,1:T(1,128)}, u32[]{:S(2)}) copy-start(s32[128,1]{0,1:T(1,128)} %param.22) | copy-start | bytes 1540
  27.7 6.2 %copy-start.5 = (s32[128]{0:T(128)S(1)}, s32[128]{0:T(128)}, u32[]{:S(2)}) copy-start(s32[128]{0:T(128)} %source_ref.3) | copy-start | bytes 1540
  27.7 6.2 %copy-start.6 = (s32[128]{0:T(128)S(1)}, s32[128]{0:T(128)}, u32[]{:S(2)}) copy-start(s32[128]{0:T(128)} %block_ref.3) | copy-start | bytes 1540
  27.7 60.8 %all-to-all-start = ((bf16[16,1040,128]{2,1,0:T(8,128)(2,1)}), bf16[16,1040,128]{2,1,0:T(8,128)(2,1)}, u32[]{:S(2)}, u32[]{:S(2)}) async-start(bf16[16,1040,128]{2,1,0:T(8,128)(2,1)} %get-tuple-element.21), calls=%async_computation | async-start | bytes 8519680 | tf_op jit(solution)/shard_map/all_to_all | solution.py:466
  33.6 8.1 %copy-start.12 = (f32[200,9]{0,1:T(8,128)S(1)}, f32[200,9]{0,1:T(8,128)}, u32[]{:S(2)}) copy-start(f32[200,9]{0,1:T(8,128)} %param.27) | copy-start | bytes 21604
  33.6 8.1 %copy-start = (bf16[200,5760]{1,0:T(8,128)(2,1)S(1)}, bf16[200,5760]{1,0:T(8,128)(2,1)}, u32[]{:S(2)}) copy-start(bf16[200,5760]{1,0:T(8,128)(2,1)} %now_ref.1) | copy-start | bytes 6912004
  33.9 8.0 %copy-start.9 = (bf16[200,1440]{1,0:T(8,128)(2,1)S(1)}, bf16[200,1440]{1,0:T(8,128)(2,1)}, u32[]{:S(2)}) copy-start(bf16[200,1440]{1,0:T(8,128)(2,1)} %copy-done.8) | copy-start | bytes 1728004
  66.2 29.2 %copy-start.7 = (bf16[200,1440]{1,0:T(8,128)(2,1)S(1)}, bf16[200,1440]{1,0:T(8,128)(2,1)}, u32[]{:S(2)}) copy-start(bf16[200,1440]{1,0:T(8,128)(2,1)} %get-tuple-element.28) | copy-start | bytes 1728004
  66.2 29.8 %copy-start.11 = (s32[5760]{0:T(1024)S(1)}, s32[5760]{0:T(1024)}, u32[]{:S(2)}) copy-start(s32[5760]{0:T(1024)} %param.26) | copy-start | bytes 69124
  66.2 29.8 %copy-start.13 = (f32[200]{0:T(256)S(1)}, f32[200]{0:T(256)}, u32[]{:S(2)}) copy-start(f32[200]{0:T(256)} %param.29) | copy-start | bytes 2404
  88.5 85.2 %all-to-all-start.1 = ((bf16[16,1040,128]{2,1,0:T(8,128)(2,1)}), bf16[16,1040,128]{2,1,0:T(8,128)(2,1)}, u32[]{:S(2)}, u32[]{:S(2)}) async-start(bf16[16,1040,128]{2,1,0:T(8,128)(2,1)} %near_remap.1), calls=%async_computation.1 | async-start | bytes 8519680 | tf_op jit(solution)/shard_map/all_to_all | solution.py:466
  95.4 68.2 %collective-permute-start.1 = (bf16[200,1440]{1,0:T(8,128)(2,1)S(1)}, bf16[200,1440]{1,0:T(8,128)(2,1)}, u32[]{:S(2)}, u32[]{:S(2)}) collective-permute-start(bf16[200,1440]{1,0:T(8,128)(2,1)S(1)} %copy-done.7), channel_id=1, source_target_pairs={{0,1},{2,3},{4,5},{6,7},{8,9},{10,11},{12,13},{14,15},{16,17},{18,... | collective-permute-start | bytes 1728008 | tf_op jit(solution)/shard_map/ppermute | solution.py:408
  101.8 82.7 %collective-permute-start.2 = (bf16[45,128,128]{2,1,0:T(8,128)(2,1)}, bf16[45,128,128]{2,1,0:T(8,128)(2,1)}, u32[]{:S(2)}, u32[]{:S(2)}) collective-permute-start(bf16[45,128,128]{2,1,0:T(8,128)(2,1)} %merge.3), channel_id=1, source_target_pairs={{0,8},{8,0},{1,9},{9,1},{2,10},{10,2},{3,11},{11,3},{4,12},{12,4},... | collective-permute-start | bytes 4423688 | tf_op jit(solution)/shard_map/ppermute | solution.py:492
  164.5 3.7 %slice-start = ((s8[4608000]{0:T(1024)(128)(4,1)}), s8[4194304]{0:T(1024)(128)(4,1)S(1)}, s32[]{:S(2)}) async-start(s8[4608000]{0:T(1024)(128)(4,1)} %bitcast.27), calls=%async_computation.2 | async-start | bytes 8388608
  166.3 1.9 slice-start.1
  170.2 14.2 %copy-start.2 = (bf16[800,200]{0,1:T(8,128)(2,1)S(1)}, bf16[800,200]{0,1:T(8,128)(2,1)}, u32[]{:S(2)}) copy-start(bf16[800,200]{0,1:T(8,128)(2,1)} %param.31) | copy-start | bytes 960004
  170.2 14.2 %copy-start.3 = (bf16[128,200]{0,1:T(8,128)(2,1)S(1)}, bf16[128,200]{0,1:T(8,128)(2,1)}, u32[]{:S(2)}) copy-start(bf16[128,200]{0,1:T(8,128)(2,1)} %param.28) | copy-start | bytes 153604
  173.8 10.7 %copy-start.1 = (bf16[200,5760]{1,0:T(8,128)(2,1)S(1)}, bf16[200,5760]{1,0:T(8,128)(2,1)}, u32[]{:S(2)}) copy-start(bf16[200,5760]{1,0:T(8,128)(2,1)} %add_convert_fusion.mix_ref) | copy-start | bytes 6912004

commit v10 on v9

--- a/solution.py
+++ b/solution.py
@@ -102,8 +102,13 @@
         copy(i).wait()
         return carry
 
+    def sixteen(i, carry):
+        group(16, i * 16)
+        return carry
+
     full = count >> 3
-    lax.fori_loop(0, full, eight, 0)
+    lax.fori_loop(0, full >> 1, sixteen, 0)
+    lax.fori_loop(full >> 1 << 1, full, eight, 0)
     lax.fori_loop(full * 8, count, one, 0)
     tile[...] = jnp.broadcast_to(labels[...].astype(F32)[:, None, :], tile.shape).astype(BF16)
     told = pltpu.make_async_copy(

time: 196 us -> 195 us (level)
  no operation moved by 1% of the time
where the time goes in v10:
time: 195 us; the launch traced here: 194 us
  waiting for transfers between devices  91.8 us (47%)
  Pallas kernels  48.7 us (25%)
  other arithmetic  22.9 us (12%)
  starting transfers between devices  19.3 us (10%)
  local copies, waits for them, and re-layouts  10.8 us (6%)
    ppermute x2, waiting for transfers between devices, exchanged(): lax.ppermute(row, ALL, pairs + [(upper, lower) for lower, upper in pairs])  59.5 us
    all_to_all x2, waiting for transfers between devices, exchange(): lax.all_to_all(values, PEERS, split_axis=0, concat_axis=0, tiled=True)  26.5 us
    pallas_call x1, Pallas kernels, atmosphere(): pl.pallas_call(functools.partial(atm_kernel, plan), name='atmosphere', gr...  20.7 us
    add x1, other arithmetic, flat_mixing(): summed = summed + kernel[:, 3 * row_step + col_step][:, None] * shifted  13.4 us
    all_to_all x2, starting transfers between devices, exchange(): lax.all_to_all(values, PEERS, split_axis=0, concat_axis=0, tiled=True)  12.9 us
    pallas_call x1, Pallas kernels, ocean(): pl.pallas_call(ocean_kernel, name='ocean', grid=(cells // part,), in_spec...  10.4 us
    pallas_call x2, Pallas kernels, merged(): pl.pallas_call(functools.partial(merge_kernel, capacity), name='merge', g...  10.3 us
    pallas_call x1, Pallas kernels, near_remap(): pl.pallas_call(functools.partial(near_kernel, plan), name='near_remap', g...  7.31 us
  transfers between devices with their start and end apart: 5, of which 4 were waited for; matrix products, arithmetic and copies ran while one was open for 16% of the time, Pallas kernels for 20%

profile of v10, /device:TPU:14, one launch (start us, length us, event | category | flops | bytes accessed | tf_op | source)
XLA Modules:
  0.0 194.4 jit_solution(13140565179086102575)
XLA Ops:
  0.6 1.5 slice_select_fusion.1
  2.1 3.4 %collective-permute-start = (bf16[200,1440]{1,0:T(8,128)(2,1)S(1)}, bf16[200,1440]{1,0:T(8,128)(2,1)S(1)}, u32[]{:S(2)}, u32[]{:S(2)}) collective-permute-start(bf16[200,1440]{1,0:T(8,128)(2,1)S(1)} %slice_select_fusion.1), channel_id=1, source_target_pairs={{1,2},{3,4},{5,6},{7,8},{9,10},{11,12},{13,14},{15,16},{17,18},{19... | collective-permute-start | bytes 1728008 | tf_op jit(solution)/shard_map/ppermute | solution.py:413
  5.5 20.7 %atmosphere.1 = (bf16[1024,1024]{1,0:T(8,128)(2,1)}, bf16[1024,128]{1,0:T(8,128)(2,1)}, bf16[16,1040,128]{2,1,0:T(8,128)(2,1)}) custom-call(s32[1]{0:T(128)} %bitcast.half_ref, s32[128]{0:T(128)} %bitcast.25, s32[128]{0:T(128)} %source_ref.3, s32[128]{0:T(128)} %block_ref.3, bf16[1024,1024]{1,0:T(8,128)(2,1)} %x_ref.1, f32[1,1024]{1,0:T(1,128)} %bitcast.38, ...), custom_call_target="tpu_custom_call" | custom-call | tf_op jit(solution)/shard_map/atmosphere/pallas_call | solution.py:208
  26.3 0.0 copy-start.10
  26.3 0.0 copy-start.8
  26.3 0.8 copy-done.8
  27.1 6.0 %all-to-all-start = ((bf16[16,1040,128]{2,1,0:T(8,128)(2,1)}), bf16[16,1040,128]{2,1,0:T(8,128)(2,1)}, u32[]{:S(2)}, u32[]{:S(2)}) async-start(bf16[16,1040,128]{2,1,0:T(8,128)(2,1)} %get-tuple-element.21), calls=%async_computation | async-start | bytes 8519680 | tf_op jit(solution)/shard_map/all_to_all | solution.py:471
  33.2 0.0 copy-start.12
  33.2 0.0 copy-start
  33.2 0.2 copy.19
  33.4 0.0 copy-start.9
  33.4 7.3 %near_remap.1 = bf16[16,1040,128]{2,1,0:T(8,128)(2,1)} custom-call(s32[1]{0:T(128)} %bitcast.half_ref, s32[128]{0:T(128)S(1)} %bitcast.26, s32[128]{0:T(128)S(1)} %copy-done.5, s32[128]{0:T(128)S(1)} %copy-done.6, bf16[1024,128]{1,0:T(8,128)(2,1)} %get-tuple-element.22.surface_ref, bf16[128,128,128]{2,1,0:T(8,128)(2,1)} %weight_ref.3), custom_call_target="tpu_custom_call" | custom-call | tf_op jit(solution)/shard_map/near_remap/pallas_call | solution.py:284
  40.8 1.3 broadcast_select_fusion.2
  42.1 6.9 %concatenate.11 = bf16[200,8640]{1,0:T(8,128)(2,1)} concatenate(bf16[200,1440]{1,0:T(8,128)(2,1)} %get-tuple-element.43, bf16[200,5760]{1,0:T(8,128)(2,1)S(1)} %copy-done, bf16[200,1440]{1,0:T(8,128)(2,1)S(1)} %get-tuple-element.42), dimensions={1} | concatenate | bytes 6912000 | tf_op jit(solution)/shard_map/concatenate | solution.py:486
  49.0 2.8 %convert_element_type.15 = f32[200,8640]{1,0:T(8,128)S(1)} convert(bf16[200,8640]{1,0:T(8,128)(2,1)} %concatenate.11) | non-fusion elementwise | flops 1728000 | bytes 10368000 | tf_op jit(solution)/shard_map/convert_element_type | solution.py:422
  51.8 13.4 %fusion.9 = f32[200,5760]{1,0:T(8,128)} fusion(f32[200,8640]{1,0:T(8,128)S(1)} %convert_element_type.15, f32[200]{0:T(256)S(1)} %bitcast.37, f32[200]{0:T(256)S(1)} %bitcast.30, f32[200]{0:T(256)S(1)} %bitcast.31, f32[200]{0:T(256)S(1)} %bitcast.32, f32[200]{0:T(256)S(1)} %bitcast.33, f32[200]{0:T(256)S(1)} %bitcast.34, f32[200]{0:T(256)S(1)} %bitcast.35, ...), kind=kLoop, calls=%fused_computation.13 | loop fusion | flops 26496000 | bytes 43848704 | tf_op jit(solution)/shard_map/add | solution.py:440
  65.2 22.8 %all-to-all-done.arrived_ref = bf16[16,1040,128]{2,1,0:T(8,128)(2,1)} async-done(((bf16[16,1040,128]{2,1,0:T(8,128)(2,1)}), bf16[16,1040,128]{2,1,0:T(8,128)(2,1)}, u32[]{:S(2)}, u32[]{:S(2)}) %all-to-all-start) | async-done | bytes 4259872 | tf_op jit(solution)/shard_map/all_to_all | solution.py:471
  88.0 6.9 %all-to-all-start.1 = ((bf16[16,1040,128]{2,1,0:T(8,128)(2,1)}), bf16[16,1040,128]{2,1,0:T(8,128)(2,1)}, u32[]{:S(2)}, u32[]{:S(2)}) async-start(bf16[16,1040,128]{2,1,0:T(8,128)(2,1)} %near_remap.1), calls=%async_computation.1 | async-start | bytes 8519680 | tf_op jit(solution)/shard_map/all_to_all | solution.py:471
  94.9 0.6 collective-permute-start.1
  95.6 0.1 copy.20.gain_ref
  95.7 5.6 %merge.3 = bf16[45,128,128]{2,1,0:T(8,128)(2,1)} custom-call(bf16[16,1040,128]{2,1,0:T(8,128)(2,1)} %all-to-all-done.arrived_ref), custom_call_target="tpu_custom_call" | custom-call | tf_op jit(solution)/shard_map/merge/pallas_call | solution.py:338
  101.3 2.4 %collective-permute-start.2 = (bf16[45,128,128]{2,1,0:T(8,128)(2,1)}, bf16[45,128,128]{2,1,0:T(8,128)(2,1)}, u32[]{:S(2)}, u32[]{:S(2)}) collective-permute-start(bf16[45,128,128]{2,1,0:T(8,128)(2,1)} %merge.3), channel_id=1, source_target_pairs={{0,8},{8,0},{1,9},{9,1},{2,10},{10,2},{3,11},{11,3},{4,12},{12,4},... | collective-permute-start | bytes 4423688 | tf_op jit(solution)/shard_map/ppermute | solution.py:497
  103.6 59.5 %collective-permute-done.1 = bf16[200,1440]{1,0:T(8,128)(2,1)} collective-permute-done((bf16[200,1440]{1,0:T(8,128)(2,1)S(1)}, bf16[200,1440]{1,0:T(8,128)(2,1)}, u32[]{:S(2)}, u32[]{:S(2)}) %collective-permute-start.1) | collective-permute-done | bytes 576032 | tf_op jit(solution)/shard_map/ppermute | solution.py:413
  163.1 0.9 fusion.24
  164.1 1.7 fusion.25
  165.8 1.8 broadcast_select_fusion.1
  167.6 0.1 broadcast_select_fusion
  167.8 2.0 %add_convert_fusion.mix_ref = bf16[200,5760]{1,0:T(8,128)(2,1)} fusion(f32[200,1440]{1,0:T(8,128)S(1)} %broadcast_select_fusion, f32[200,5760]{1,0:T(8,128)S(1)} %bitcast.28, f32[200,1440]{1,0:T(8,128)S(1)} %get-tuple-element.36), kind=kLoop, calls=%fused_computation.23 | loop fusion | flops 3456000 | bytes 9216000 | tf_op jit(solution)/shard_map/convert_element_type | solution.py:504
  169.8 3.7 %all-to-all-done.1.arrived_ref = bf16[16,1040,128]{2,1,0:T(8,128)(2,1)} async-done(((bf16[16,1040,128]{2,1,0:T(8,128)(2,1)}), bf16[16,1040,128]{2,1,0:T(8,128)(2,1)}, u32[]{:S(2)}, u32[]{:S(2)}) %all-to-all-start.1) | async-done | bytes 4259872 | tf_op jit(solution)/shard_map/all_to_all | solution.py:471
  173.5 4.7 %merge.2 = bf16[45,128,128]{2,1,0:T(8,128)(2,1)S(1)} custom-call(bf16[16,1040,128]{2,1,0:T(8,128)(2,1)} %all-to-all-done.1.arrived_ref), custom_call_target="tpu_custom_call" | custom-call | tf_op jit(solution)/shard_map/merge/pallas_call | solution.py:338
  178.2 5.8 %collective-permute-done.2 = bf16[45,128,128]{2,1,0:T(8,128)(2,1)} collective-permute-done((bf16[45,128,128]{2,1,0:T(8,128)(2,1)}, bf16[45,128,128]{2,1,0:T(8,128)(2,1)}, u32[]{:S(2)}, u32[]{:S(2)}) %collective-permute-start.2) | collective-permute-done | bytes 1474592 | tf_op jit(solution)/shard_map/ppermute | solution.py:497
  184.0 10.4 %ocean.1 = bf16[200,5760]{1,0:T(8,128)(2,1)} custom-call(bf16[200,5760]{1,0:T(8,128)(2,1)S(1)} %copy-done.1, bf16[5760,128]{1,0:T(8,128)(2,1)S(1)} %bitcast.21, bf16[5760,128]{1,0:T(8,128)(2,1)} %bitcast.20.far_ref, bf16[200,5760]{1,0:T(8,128)(2,1)S(1)} %copy-done, s32[1,5760]{1,0:T(1,128)S(1)} %broadcast_in_dim.62.sea_ref, bf16[200,128]{1,0:T(8,128)(2,1)S(1)} %bitcast.24, ...), custom_call_target="tpu_custom_call" | custom-call | tf_op jit(solution)/shard_map/ocean/pallas_call | solution.py:379
  (33 shorter events, 0.1 us)
Async XLA Ops:
  2.1 24.1 %collective-permute-start = (bf16[200,1440]{1,0:T(8,128)(2,1)S(1)}, bf16[200,1440]{1,0:T(8,128)(2,1)S(1)}, u32[]{:S(2)}, u32[]{:S(2)}) collective-permute-start(bf16[200,1440]{1,0:T(8,128)(2,1)S(1)} %slice_select_fusion.1), channel_id=1, source_target_pairs={{1,2},{3,4},{5,6},{7,8},{9,10},{11,12},{13,14},{15,16},{17,18},{19... | collective-permute-start | bytes 1728008 | tf_op jit(solution)/shard_map/ppermute | solution.py:413
  26.3 6.9 %copy-start.10 = (bf16[200,800]{1,0:T(8,128)(2,1)S(1)}, bf16[200,800]{1,0:T(8,128)(2,1)}, u32[]{:S(2)}) copy-start(bf16[200,800]{1,0:T(8,128)(2,1)} %param.30) | copy-start | bytes 960004
  26.3 0.8 copy-start.8
  27.1 6.3 %copy-start.4 = (s32[128,1]{0,1:T(1,128)S(1)}, s32[128,1]{0,1:T(1,128)}, u32[]{:S(2)}) copy-start(s32[128,1]{0,1:T(1,128)} %param.22) | copy-start | bytes 1540
  27.1 6.3 %copy-start.5 = (s32[128]{0:T(128)S(1)}, s32[128]{0:T(128)}, u32[]{:S(2)}) copy-start(s32[128]{0:T(128)} %source_ref.3) | copy-start | bytes 1540
  27.1 6.3 %copy-start.6 = (s32[128]{0:T(128)S(1)}, s32[128]{0:T(128)}, u32[]{:S(2)}) copy-start(s32[128]{0:T(128)} %block_ref.3) | copy-start | bytes 1540
  27.1 60.9 %all-to-all-start = ((bf16[16,1040,128]{2,1,0:T(8,128)(2,1)}), bf16[16,1040,128]{2,1,0:T(8,128)(2,1)}, u32[]{:S(2)}, u32[]{:S(2)}) async-start(bf16[16,1040,128]{2,1,0:T(8,128)(2,1)} %get-tuple-element.21), calls=%async_computation | async-start | bytes 8519680 | tf_op jit(solution)/shard_map/all_to_all | solution.py:471
  33.2 7.6 %copy-start.12 = (f32[200,9]{0,1:T(8,128)S(1)}, f32[200,9]{0,1:T(8,128)}, u32[]{:S(2)}) copy-start(f32[200,9]{0,1:T(8,128)} %param.27) | copy-start | bytes 21604
  33.2 7.6 %copy-start = (bf16[200,5760]{1,0:T(8,128)(2,1)S(1)}, bf16[200,5760]{1,0:T(8,128)(2,1)}, u32[]{:S(2)}) copy-start(bf16[200,5760]{1,0:T(8,128)(2,1)} %now_ref.1) | copy-start | bytes 6912004
  33.4 7.4 %copy-start.9 = (bf16[200,1440]{1,0:T(8,128)(2,1)S(1)}, bf16[200,1440]{1,0:T(8,128)(2,1)}, u32[]{:S(2)}) copy-start(bf16[200,1440]{1,0:T(8,128)(2,1)} %copy-done.8) | copy-start | bytes 1728004
  65.2 29.7 %copy-start.7 = (bf16[200,1440]{1,0:T(8,128)(2,1)S(1)}, bf16[200,1440]{1,0:T(8,128)(2,1)}, u32[]{:S(2)}) copy-start(bf16[200,1440]{1,0:T(8,128)(2,1)} %get-tuple-element.28) | copy-start | bytes 1728004
  65.2 30.3 %copy-start.11 = (s32[5760]{0:T(1024)S(1)}, s32[5760]{0:T(1024)}, u32[]{:S(2)}) copy-start(s32[5760]{0:T(1024)} %param.26) | copy-start | bytes 69124
  65.2 30.3 %copy-start.13 = (f32[200]{0:T(256)S(1)}, f32[200]{0:T(256)}, u32[]{:S(2)}) copy-start(f32[200]{0:T(256)} %param.29) | copy-start | bytes 2404
  88.0 85.4 %all-to-all-start.1 = ((bf16[16,1040,128]{2,1,0:T(8,128)(2,1)}), bf16[16,1040,128]{2,1,0:T(8,128)(2,1)}, u32[]{:S(2)}, u32[]{:S(2)}) async-start(bf16[16,1040,128]{2,1,0:T(8,128)(2,1)} %near_remap.1), calls=%async_computation.1 | async-start | bytes 8519680 | tf_op jit(solution)/shard_map/all_to_all | solution.py:471
  94.9 68.2 %collective-permute-start.1 = (bf16[200,1440]{1,0:T(8,128)(2,1)S(1)}, bf16[200,1440]{1,0:T(8,128)(2,1)}, u32[]{:S(2)}, u32[]{:S(2)}) collective-permute-start(bf16[200,1440]{1,0:T(8,128)(2,1)S(1)} %copy-done.7), channel_id=1, source_target_pairs={{0,1},{2,3},{4,5},{6,7},{8,9},{10,11},{12,13},{14,15},{16,17},{18,... | collective-permute-start | bytes 1728008 | tf_op jit(solution)/shard_map/ppermute | solution.py:413
  101.3 82.7 %collective-permute-start.2 = (bf16[45,128,128]{2,1,0:T(8,128)(2,1)}, bf16[45,128,128]{2,1,0:T(8,128)(2,1)}, u32[]{:S(2)}, u32[]{:S(2)}) collective-permute-start(bf16[45,128,128]{2,1,0:T(8,128)(2,1)} %merge.3), channel_id=1, source_target_pairs={{0,8},{8,0},{1,9},{9,1},{2,10},{10,2},{3,11},{11,3},{4,12},{12,4},... | collective-permute-start | bytes 4423688 | tf_op jit(solution)/shard_map/ppermute | solution.py:497
  164.1 3.7 %slice-start = ((s8[4608000]{0:T(1024)(128)(4,1)}), s8[4194304]{0:T(1024)(128)(4,1)S(1)}, s32[]{:S(2)}) async-start(s8[4608000]{0:T(1024)(128)(4,1)} %bitcast.27), calls=%async_computation.2 | async-start | bytes 8388608
  165.8 1.9 slice-start.1
  169.8 14.2 %copy-start.2 = (bf16[800,200]{0,1:T(8,128)(2,1)S(1)}, bf16[800,200]{0,1:T(8,128)(2,1)}, u32[]{:S(2)}) copy-start(bf16[800,200]{0,1:T(8,128)(2,1)} %param.31) | copy-start | bytes 960004
  169.8 14.2 %copy-start.3 = (bf16[128,200]{0,1:T(8,128)(2,1)S(1)}, bf16[128,200]{0,1:T(8,128)(2,1)}, u32[]{:S(2)}) copy-start(bf16[128,200]{0,1:T(8,128)(2,1)} %param.28) | copy-start | bytes 153604
  173.5 10.5 %copy-start.1 = (bf16[200,5760]{1,0:T(8,128)(2,1)S(1)}, bf16[200,5760]{1,0:T(8,128)(2,1)}, u32[]{:S(2)}) copy-start(bf16[200,5760]{1,0:T(8,128)(2,1)} %add_convert_fusion.mix_ref) | copy-start | bytes 6912004
